TPU v7x, 32 devices: a whole 2x2x4 slice. The times are simulated.
32 devices in a mesh: gx: 4 (over y, x), gy: 4 (over z), gz: 2 (over core).
Axes of the slice: x: 2, y: 2, z: 4, core: 2. Of those that a mesh axis runs over, the one named last changes fastest.
Arguments:
- offsets: float32 [3, 4, 4, 6, 128], P(None, 'gx', 'gy', 'gz'), may hold values from 0 to 1
- velocity: float32 [3, 4, 4, 6, 128], P(None, 'gx', 'gy', 'gz'), may hold values from -6 to 6
- counts: int32 [4, 4, 6], P('gx', 'gy', 'gz'), may hold values from 0 to 128, as said below
- neighbours: int32 [4, 4, 6, 27], P('gx', 'gy', 'gz'), may hold values from 0 to 27, as said below
Outputs:
- velocity_star: float32 [3, 4, 4, 6, 128], P(None, 'gx', 'gy', 'gz')
- pressure: float32 [4, 4, 6, 128], P('gx', 'gy', 'gz')
Inputs may be any that keep to these rules, and one draw needn't show every extreme that they name: `counts`: each column along the entry direction is filled up to a surface height of at least its lowest block; blocks above it are empty, blocks below hold 42 or more particles, and some hold 128. `neighbours`: for each block, the codes 9 (dx + 1) + 3 (dy + 1) + (dz + 1) of the adjacent blocks, itself included, that lie in the grid and hold particles, in increasing order, then the code 27 to fill 27 entries.
All inputs are finite; a program needn't handle non-finite values.
Results may differ from a plain program's by a relative error of at most 0.0003.
Values sent between devices are 32-bit elements; how exact they have to be, the bound alone decides.
No kernel may reach another device: no remote copies, remote signals or barrier semaphores. Data moves between devices by JAX's collectives and lax.ppermute only.
A program may use at most 64 MiB of HBM per device.

v0:
```python
import jax
import jax.numpy as jnp
from jax import lax
from jax.sharding import PartitionSpec as P

ITERS_V = 3
ITERS_P = 2


VISCOUS = 4.0
STIFFNESS = 0.25
GRAVITY_STEP = 0.5
HIGHEST = lax.Precision.HIGHEST


def with_halo(block, sides, width):
    for axis, dim in sides:
        count = lax.axis_size(axis)
        forward = [(i, i + 1) for i in range(count - 1)]
        backward = [(target, source) for source, target in forward]
        low = lax.ppermute(
            lax.slice_in_dim(block, block.shape[dim] - width, None, axis=dim), axis, forward
        )
        high = lax.ppermute(lax.slice_in_dim(block, 0, width, axis=dim), axis, backward)
        block = jnp.concatenate([low, block, high], axis=dim)
    return block


def code_shift(codes):
    live = codes < 27
    shift_x = jnp.where(live, codes // 9 - 1, 0)
    shift_y = jnp.where(live, codes // 3 % 3 - 1, 0)
    shift_z = jnp.where(live, codes % 3 - 1, 0)
    return (live, shift_x, shift_y, shift_z)


def block_tile(own_block, near_block, live_block, shift_block):
    width = own_block.shape[-1]
    squared = jnp.zeros((near_block.shape[1], width, width), jnp.float32)
    for axis in range(3):
        apart = (
            shift_block[axis][:, None, None]
            + near_block[axis][:, None, :]
            - own_block[axis][None, :, None]
        )
        squared = squared + apart * apart
    bump = jnp.maximum(1.0 - squared, 0.0)
    weight = bump * bump * bump * (2.0 / width)
    return (
        weight * live_block[:, None, None] * own_block[3][None, :, None] * near_block[3][:, None, :]
    )


def totals_norm(residual):
    return lax.psum(jnp.sum(residual * residual, axis=(1, 2)), ("gx", "gy", "gz"))


def totals_curve(direction, image):
    return lax.psum(jnp.sum(direction * image, axis=(1, 2)), ("gx", "gy", "gz"))


def widen_three(scalars):
    return scalars[:, None, None]


def conjugate(right, operate, iterations):
    solution = jnp.zeros_like(right)
    solution_rim = None
    residual = right
    direction = right
    current = totals_norm(residual)
    for step in range(iterations):
        image, direction_rim = operate(direction)
        alpha = current / totals_curve(direction, image)
        solution = solution + widen_three(alpha) * direction
        residual = residual - widen_three(alpha) * image
        if step + 1 < iterations:
            following = totals_norm(residual)
            direction = residual + widen_three(following / current) * direction
            current = following
    return (solution, solution_rim)


def local(offsets, velocity, counts, neighbours):
    blocks_x, blocks_y, blocks_z = counts.shape
    width = offsets.shape[-1]
    nblocks = blocks_x * blocks_y * blocks_z
    slots = jnp.arange(width, dtype=jnp.int32)
    valid = (slots < counts[..., None]).astype(jnp.float32)
    geometry = jnp.concatenate([offsets, valid[None]], 0)
    geometry_pad = with_halo(geometry, (("gx", 1), ("gy", 2), ("gz", 3)), 1)
    geometry_flat = geometry_pad.reshape(4, -1, width)
    own_geometry = geometry.reshape(4, nblocks, width)
    codes = neighbours.reshape(nblocks, 27)
    live, shift_x, shift_y, shift_z = code_shift(codes)
    pad_y = blocks_y + 2
    pad_z = blocks_z + 2
    index_x = jnp.arange(blocks_x, dtype=jnp.int32)[:, None, None]
    index_y = jnp.arange(blocks_y, dtype=jnp.int32)[None, :, None]
    index_z = jnp.arange(blocks_z, dtype=jnp.int32)[None, None, :]
    anchor = (((index_x + 1) * pad_y + index_y + 1) * pad_z + index_z + 1).reshape(nblocks)
    index = anchor[:, None] + (shift_x * pad_y + shift_y) * pad_z + shift_z
    shifts = jnp.stack([shift_x, shift_y, shift_z]).astype(jnp.float32)
    live_weight = live.astype(jnp.float32)
    near_geometry = geometry_flat[:, index]

    def tile_of(block):
        return block_tile(
            own_geometry[:, block], near_geometry[:, block], live_weight[block], shifts[:, block]
        )

    tiles = lax.map(tile_of, jnp.arange(nblocks, dtype=jnp.int32))
    row_parts = jnp.sum(tiles, axis=3)
    row_total = jnp.sum(row_parts, axis=1)

    def field_rim(vector):
        grid = vector.reshape((vector.shape[0], blocks_x, blocks_y, blocks_z, width))
        return with_halo(grid, (("gx", 1), ("gy", 2), ("gz", 3)), 1)

    def pairs(vector, padded):
        flat = padded.reshape(padded.shape[0], -1, width)
        beside_all = flat[:, index]
        mixed = jnp.einsum("bkij,cbkj->cbi", tiles, beside_all, precision=HIGHEST)
        return row_total * vector - mixed

    def viscous(vector):
        padded = field_rim(vector)
        return (vector + VISCOUS * pairs(vector, padded), padded)

    def poisson(vector):
        padded = field_rim(vector)
        return (STIFFNESS * vector + pairs(vector, padded), padded)

    gravity = jnp.array([GRAVITY_STEP, 0.0, 0.0], jnp.float32)[:, None, None]
    right = own_geometry[3][None] * (velocity.reshape(3, nblocks, width) + gravity)
    star, unused = conjugate(right, viscous, ITERS_V)
    star_pad = with_halo(
        star.reshape((3, blocks_x, blocks_y, blocks_z, width)), (("gx", 1), ("gy", 2), ("gz", 3)), 1
    )
    star_flat = star_pad.reshape(3, -1, width)
    beside_all = star_flat[:, index]
    near_offsets = near_geometry[0:3]
    stacked = jnp.concatenate([beside_all, beside_all * near_offsets, near_offsets], 0)
    mixed = jnp.einsum("bkij,ybkj->ybki", tiles, stacked, precision=HIGHEST)
    w_velocity = mixed[0:3]
    w_product = mixed[3:6]
    w_offset = mixed[6:9]
    centre_velocity = star[:, :, None, :]
    centre_offset = own_geometry[0:3][:, :, None, :]
    reach = row_parts[None]
    terms = (
        shifts[..., None] * (w_velocity - centre_velocity * reach)
        + w_product
        - centre_offset * w_velocity
        - centre_velocity * w_offset
        + centre_velocity * centre_offset * reach
    )
    divergence = jnp.sum(terms, axis=(0, 2))
    source = -divergence
    pressure, ignored = conjugate(source[None], poisson, ITERS_P)
    return (
        star.reshape((3, blocks_x, blocks_y, blocks_z, width)),
        pressure.reshape((blocks_x, blocks_y, blocks_z, width)),
    )


def solution(mesh):
    in_specs = (
        P(None, "gx", "gy", "gz", None),
        P(None, "gx", "gy", "gz", None),
        P("gx", "gy", "gz"),
        P("gx", "gy", "gz", None),
    )
    out_specs = (P(None, "gx", "gy", "gz", None), P("gx", "gy", "gz", None))
    return jax.shard_map(local, mesh=mesh, in_specs=in_specs, out_specs=out_specs, check_vma=False)
```

profile of v0, /device:TPU:0, one launch (start us, length us, event | category | flops | bytes accessed | tf_op | source)
XLA Modules:
  0.0 553.3 jit_solution(15201475393399325699)
XLA Ops:
  2.1 4.8 collective-permute-start
  9.7 4.5 collective-permute-start.6
  25.0 4.5 collective-permute-start.2
  40.4 21.1 %while.10 = (s32[]{:T(128)}, f32[3,27,128,128]{3,2,1,0:T(8,128)}, s32[3]{0:T(128)S(1)}, f32[3,3,27]{2,1,0:T(4,128)S(1)}, f32[4,3,27,128]{3,0,2,1:T(4,128)S(1)}, ...) while((s32[]{:T(128)}, f32[3,27,128,128]{3,2,1,0:T(8,128)}, ...), condition=%wide.region_3.4_spmd, body=%wide.region_2.3_spmd.sunk | while | flops 6645923 | bytes 2054159 | solution.py:112
  43.3 4.2 fusion.93
  50.3 4.2 fusion.93
  57.3 4.2 fusion.93
  61.5 4.2 fusion.68
  65.8 4.7 multiply_reduce_fusion.3
  70.5 41.7 %all-reduce.1 = (f32[3]{0:T(128)S(1)}, f32[3]{0:T(128)S(1)}) all-reduce(f32[3]{0:T(128)S(1)} %get-tuple-element.61, f32[3]{0:T(128)S(1)} %get-tuple-element.60), channel_id=1, replica_groups=mesh['gx'=4,'gy'=4,'gz'=2] {'gx','gy','gz'}, use_global_device_ids=true, to_apply=%region_1.2 | all-reduce | flops 6 | bytes 48 | tf_op jit(solution)/shard_map/psum | solution.py:55
  112.3 41.4 %psum.72 = f32[3]{0:T(128)S(1)} all-reduce(f32[3]{0:T(128)S(1)} %get-tuple-element.84), channel_id=1, replica_groups=mesh['gx'=4,'gy'=4,'gz'=2] {'gx','gy','gz'}, use_global_device_ids=true, to_apply=%region_8.9 | all-reduce | flops 3 | bytes 24 | tf_op jit(solution)/shard_map/psum | solution.py:55
  159.3 4.2 collective-permute-done.13
  167.4 4.2 collective-permute-done.15
  176.7 6.6 %multiply_reduce_fusion.1 = (f32[3]{0:T(128)S(1)}, f32[3,3,128]{2,0,1:T(4,128)S(1)}) fusion(f32[3,3,128]{2,0,1:T(4,128)S(1)} %multiply_add_fusion.2, f32[3,3,27,128]{3,0,2,1:T(4,128)S(1)} %bitcast.230, f32[3,27,128,128]{3,2,1,0:T(8,128)} %get-tuple-element.39, f32[3,128]{1,0:T(4,128)S(1)} %get-tuple-element.59), kind=kOutput, calls=%fused_computation.115 | convolution fusion | flops 47782652 | bytes 5443596 | tf_op jit(solution)/shard_map/bkij,cbkj->cbi/dot_general | solution.py:123
  183.3 39.8 %psum.73 = f32[3]{0:T(128)S(1)} all-reduce(f32[3]{0:T(128)S(1)} %get-tuple-element.131), channel_id=1, replica_groups=mesh['gx'=4,'gy'=4,'gz'=2] {'gx','gy','gz'}, use_global_device_ids=true, to_apply=%region_10.11 | all-reduce | flops 3 | bytes 24 | tf_op jit(solution)/shard_map/psum | solution.py:59
  223.3 40.4 %psum.74 = f32[3]{0:T(128)S(1)} all-reduce(f32[3]{0:T(128)S(1)} %multiply_reduce_fusion), channel_id=1, replica_groups=mesh['gx'=4,'gy'=4,'gz'=2] {'gx','gy','gz'}, use_global_device_ids=true, to_apply=%region_12.13 | all-reduce | flops 3 | bytes 24 | tf_op jit(solution)/shard_map/psum | solution.py:55
  269.2 4.2 collective-permute-done.19
  278.2 4.2 collective-permute-done.21
  287.5 6.6 %fusion.26 = f32[3]{0:T(128)S(1)} fusion(f32[3,3,128]{2,0,1:T(4,128)S(1)} %multiply_add_fusion.1, f32[3,3,27,128]{3,0,2,1:T(4,128)S(1)} %bitcast.231, f32[3,27,128,128]{3,2,1,0:T(8,128)} %get-tuple-element.39, f32[3,128]{1,0:T(4,128)S(1)} %get-tuple-element.59), kind=kOutput, calls=%fused_computation.54 | convolution fusion | flops 47782652 | bytes 5438988 | tf_op jit(solution)/shard_map/bkij,cbkj->cbi/dot_general | solution.py:123
  294.1 39.7 %psum.75 = f32[3]{0:T(128)S(1)} all-reduce(f32[3]{0:T(128)S(1)} %fusion.26), channel_id=1, replica_groups=mesh['gx'=4,'gy'=4,'gz'=2] {'gx','gy','gz'}, use_global_device_ids=true, to_apply=%region_14.15 | all-reduce | flops 3 | bytes 24 | tf_op jit(solution)/shard_map/psum | solution.py:59
  339.4 4.2 collective-permute-done.25
  347.5 4.2 collective-permute-done.27
  356.9 10.8 %convolution_bitcast_fusion = f32[9,3,27,128]{3,0,2,1:T(8,128)S(1)} fusion(f32[3,27,128,128]{3,2,1,0:T(8,128)} %get-tuple-element.39, f32[3,3,27,128]{3,0,2,1:T(4,128)S(1)} %get-tuple-element.103, f32[3,3,27,128]{3,0,2,1:T(4,128)S(1)} %get-tuple-element.102, f32[3,3,27,128]{3,0,2,1:T(4,128)S(1)} %bitcast.223), kind=kOutput, calls=%fused_computation.40 | convolution fusion | flops 143513856 | bytes 6054912 | tf_op jit(solution)/shard_map/bkij,ybkj->ybki/dot_general | solution.py:144
  368.0 4.3 collective-permute-start.30
  381.7 4.2 collective-permute-done.33
  390.9 6.4 %fusion.69 = f32[3,1,128,1]{2,1,3,0:T(1,128)S(1)} fusion(f32[3,27,128,1]{2,3,1,0:T(1,128)S(1)} %reshape.807, f32[3,27,128,128]{3,2,1,0:T(8,128)} %get-tuple-element.39), kind=kOutput, calls=%fused_computation.203 | convolution fusion | flops 15925248 | bytes 5351424 | tf_op jit(solution)/shard_map/bkij,cbkj->cbi/dot_general | solution.py:123
  398.0 39.4 %all-reduce = (f32[1]{0:T(128)}, f32[1]{0:T(128)}) all-reduce(f32[1]{0:T(128)} %bitcast.53, f32[1]{0:T(128)} %bitcast.56), channel_id=1, replica_groups=mesh['gx'=4,'gy'=4,'gz'=2] {'gx','gy','gz'}, use_global_device_ids=true, to_apply=%region_18.19 | all-reduce | flops 2 | bytes 16 | tf_op jit(solution)/shard_map/psum | solution.py:55
  439.4 40.7 %psum.78 = f32[1]{0:T(128)} all-reduce(f32[1]{0:T(128)} %bitcast.58), channel_id=1, replica_groups=mesh['gx'=4,'gy'=4,'gz'=2] {'gx','gy','gz'}, use_global_device_ids=true, to_apply=%region_22.23 | all-reduce | flops 1 | bytes 8 | tf_op jit(solution)/shard_map/psum | solution.py:55
  481.4 4.2 collective-permute-start.36
  495.8 4.2 collective-permute-done.39
  505.0 6.4 %fusion.70 = f32[3,1,128,1]{2,1,3,0:T(1,128)S(1)} fusion(f32[3,27,128,1]{2,3,1,0:T(1,128)S(1)} %reshape.809, f32[3,27,128,128]{3,2,1,0:T(8,128)} %get-tuple-element.39), kind=kOutput, calls=%fused_computation.204 | convolution fusion | flops 15925248 | bytes 5351424 | tf_op jit(solution)/shard_map/bkij,cbkj->cbi/dot_general | solution.py:123
  512.1 39.3 %psum.79 = f32[1]{0:T(128)} all-reduce(f32[1]{0:T(128)} %bitcast.62), channel_id=1, replica_groups=mesh['gx'=4,'gy'=4,'gz'=2] {'gx','gy','gz'}, use_global_device_ids=true, to_apply=%region_24.25 | all-reduce | flops 1 | bytes 8 | tf_op jit(solution)/shard_map/psum | solution.py:59
  (176 shorter events, 105.3 us)
Async XLA Ops:
  2.1 22.9 %collective-permute-start = (f32[4,1,1,3,128]{4,3,0,2,1:T(4,128)S(1)}, f32[4,1,1,3,128]{4,3,0,2,1:T(4,128)S(1)}, u32[]{:S(2)}, u32[]{:S(2)}) collective-permute-start(f32[4,1,1,3,128]{4,3,0,2,1:T(4,128)S(1)} %get-tuple-element.119), channel_id=1, source_target_pairs={{0,8},{8,16},{16,24},{1,9},{9,17},{17,25},{2,10},{10,18},{18,26},{... | collective-permute-start | bytes 18440 | tf_op jit(solution)/shard_map/ppermute | solution.py:21
  6.9 18.0 %collective-permute-start.1 = (f32[4,1,1,3,128]{4,3,0,2,1:T(4,128)S(1)}, f32[4,1,1,3,128]{4,3,0,2,1:T(4,128)S(1)}, u32[]{:S(2)}, u32[]{:S(2)}) collective-permute-start(f32[4,1,1,3,128]{4,3,0,2,1:T(4,128)S(1)} %get-tuple-element.119), channel_id=1, source_target_pairs={{8,0},{16,8},{24,16},{9,1},{17,9},{25,17},{10,2},{18,10},{26,18},{... | collective-permute-start | bytes 18440 | tf_op jit(solution)/shard_map/ppermute | solution.py:24
  9.7 7.5 %collective-permute-start.6 = (f32[3,1,1,3,128]{4,2,3,1,0:T(1,128)S(1)}, f32[3,1,1,3,128]{4,2,3,1,0:T(1,128)S(1)}, u32[]{:S(2)}, u32[]{:S(2)}) collective-permute-start(f32[3,1,1,3,128]{4,2,3,1,0:T(1,128)S(1)} %add_multiply_fusion), channel_id=1, source_target_pairs={{0,8},{8,16},{16,24},{1,9},{9,17},{17,25},{2,10},{10,18},{18,26},{... | collective-permute-start | bytes 13832 | tf_op jit(solution)/shard_map/ppermute | solution.py:21
  14.2 5.9 %collective-permute-start.7 = (f32[3,1,1,3,128]{4,2,3,1,0:T(1,128)S(1)}, f32[3,1,1,3,128]{4,2,3,1,0:T(1,128)S(1)}, u32[]{:S(2)}, u32[]{:S(2)}) collective-permute-start(f32[3,1,1,3,128]{4,2,3,1,0:T(1,128)S(1)} %add_multiply_fusion), channel_id=1, source_target_pairs={{8,0},{16,8},{24,16},{9,1},{17,9},{25,17},{10,2},{18,10},{26,18},{... | collective-permute-start | bytes 13832 | tf_op jit(solution)/shard_map/ppermute | solution.py:24
  20.1 10.7 %collective-permute-start.8 = (f32[3,3,1,3,128]{4,2,3,1,0:T(1,128)S(1)}, f32[3,3,1,3,128]{4,2,3,1,0:T(1,128)S(1)}, u32[]{:S(2)}, u32[]{:S(2)}) collective-permute-start(f32[3,3,1,3,128]{4,2,3,1,0:T(1,128)S(1)} %pad_maximum_fusion.37), channel_id=1, source_target_pairs={{0,2},{2,4},{4,6},{1,3},{3,5},{5,7},{8,10},{10,12},{12,14},{9,11},... | collective-permute-start | bytes 41480 | tf_op jit(solution)/shard_map/ppermute | solution.py:21
  23.6 7.2 %collective-permute-start.9 = (f32[3,3,1,3,128]{4,2,3,1,0:T(1,128)S(1)}, f32[3,3,1,3,128]{4,2,3,1,0:T(1,128)S(1)}, u32[]{:S(2)}, u32[]{:S(2)}) collective-permute-start(f32[3,3,1,3,128]{4,2,3,1,0:T(1,128)S(1)} %pad_maximum_fusion.37), channel_id=1, source_target_pairs={{2,0},{4,2},{6,4},{3,1},{5,3},{7,5},{10,8},{12,10},{14,12},{11,9},... | collective-permute-start | bytes 41480 | tf_op jit(solution)/shard_map/ppermute | solution.py:24
  25.0 8.5 %collective-permute-start.2 = (f32[4,3,1,3,128]{4,3,0,2,1:T(4,128)S(1)}, f32[4,3,1,3,128]{4,3,0,2,1:T(4,128)S(1)}, u32[]{:S(2)}, u32[]{:S(2)}) collective-permute-start(f32[4,3,1,3,128]{4,3,0,2,1:T(4,128)S(1)} %pad_maximum_fusion.7), channel_id=1, source_target_pairs={{0,2},{2,4},{4,6},{1,3},{3,5},{5,7},{8,10},{10,12},{12,14},{9,11},... | collective-permute-start | bytes 55304 | tf_op jit(solution)/shard_map/ppermute | solution.py:21
  29.5 5.7 %collective-permute-start.3 = (f32[4,3,1,3,128]{4,3,0,2,1:T(4,128)S(1)}, f32[4,3,1,3,128]{4,3,0,2,1:T(4,128)S(1)}, u32[]{:S(2)}, u32[]{:S(2)}) collective-permute-start(f32[4,3,1,3,128]{4,3,0,2,1:T(4,128)S(1)} %pad_maximum_fusion.7), channel_id=1, source_target_pairs={{2,0},{4,2},{6,4},{3,1},{5,3},{7,5},{10,8},{12,10},{14,12},{11,9},... | collective-permute-start | bytes 55304 | tf_op jit(solution)/shard_map/ppermute | solution.py:24
  30.9 7.0 %collective-permute-start.10 = (f32[3,3,3,1,128]{4,2,3,1,0:T(4,128)S(1)}, f32[3,3,3,1,128]{4,2,3,1,0:T(4,128)S(1)}, u32[]{:S(2)}, u32[]{:S(2)}) collective-permute-start(f32[3,3,3,1,128]{4,2,3,1,0:T(4,128)S(1)} %get-tuple-element.112), channel_id=1, source_target_pairs={{0,1},{2,3},{4,5},{6,7},{8,9},{10,11},{12,13},{14,15},{16,17},{18,... | collective-permute-start | bytes 41480 | tf_op jit(solution)/shard_map/ppermute | solution.py:21
  32.2 5.7 %collective-permute-start.11 = (f32[3,3,3,1,128]{4,2,3,1,0:T(4,128)S(1)}, f32[3,3,3,1,128]{4,2,3,1,0:T(4,128)S(1)}, u32[]{:S(2)}, u32[]{:S(2)}) collective-permute-start(f32[3,3,3,1,128]{4,2,3,1,0:T(4,128)S(1)} %get-tuple-element.113), channel_id=1, source_target_pairs={{1,0},{3,2},{5,4},{7,6},{9,8},{11,10},{13,12},{15,14},{17,16},{19,... | collective-permute-start | bytes 41480 | tf_op jit(solution)/shard_map/ppermute | solution.py:24
  35.3 3.4 collective-permute-start.4
  153.8 5.5 collective-permute-start.12
  158.0 5.5 collective-permute-start.13
  163.5 3.9 collective-permute-start.14
  166.0 5.7 %collective-permute-start.15 = (f32[3,3,1,3,128]{4,0,3,2,1:T(4,128)S(1)}, f32[3,3,1,3,128]{4,0,3,2,1:T(4,128)S(1)}, u32[]{:S(2)}, u32[]{:S(2)}) collective-permute-start(f32[3,3,1,3,128]{4,0,3,2,1:T(4,128)S(1)} %pad_maximum_fusion.34), channel_id=1, source_target_pairs={{2,0},{4,2},{6,4},{3,1},{5,3},{7,5},{10,8},{12,10},{14,12},{11,9},... | collective-permute-start | bytes 41480 | tf_op jit(solution)/shard_map/ppermute | solution.py:24
  263.7 5.5 collective-permute-start.18
  267.9 5.5 collective-permute-start.19
  273.4 4.8 collective-permute-start.20
  276.8 5.7 %collective-permute-start.21 = (f32[3,3,1,3,128]{4,0,3,2,1:T(4,128)S(1)}, f32[3,3,1,3,128]{4,0,3,2,1:T(4,128)S(1)}, u32[]{:S(2)}, u32[]{:S(2)}) collective-permute-start(f32[3,3,1,3,128]{4,0,3,2,1:T(4,128)S(1)} %pad_maximum_fusion.35), channel_id=1, source_target_pairs={{2,0},{4,2},{6,4},{3,1},{5,3},{7,5},{10,8},{12,10},{14,12},{11,9},... | collective-permute-start | bytes 41480 | tf_op jit(solution)/shard_map/ppermute | solution.py:24
  333.9 5.5 collective-permute-start.24
  338.1 5.5 collective-permute-start.25
  343.6 3.9 collective-permute-start.26
  346.1 5.7 %collective-permute-start.27 = (f32[3,3,1,3,128]{4,0,3,2,1:T(4,128)S(1)}, f32[3,3,1,3,128]{4,0,3,2,1:T(4,128)S(1)}, u32[]{:S(2)}, u32[]{:S(2)}) collective-permute-start(f32[3,3,1,3,128]{4,0,3,2,1:T(4,128)S(1)} %pad_maximum_fusion.36), channel_id=1, source_target_pairs={{2,0},{4,2},{6,4},{3,1},{5,3},{7,5},{10,8},{12,10},{14,12},{11,9},... | collective-permute-start | bytes 41480 | tf_op jit(solution)/shard_map/ppermute | solution.py:24
  368.0 5.6 %collective-permute-start.30 = (f32[1,1,1,3,128]{4,3,2,1,0:T(4,128)S(1)}, f32[1,1,1,3,128]{4,3,2,1,0:T(4,128)S(1)}, u32[]{:S(2)}, u32[]{:S(2)}) collective-permute-start(f32[1,1,1,3,128]{4,3,2,1,0:T(4,128)S(1)} %negate_bitcast_fusion), channel_id=1, source_target_pairs={{0,8},{8,16},{16,24},{1,9},{9,17},{17,25},{2,10},{10,18},{18,26},{... | collective-permute-start | bytes 4616 | tf_op jit(solution)/shard_map/ppermute | solution.py:21
  372.3 5.5 collective-permute-start.31
  377.8 3.9 collective-permute-start.32
  380.3 5.5 collective-permute-start.33
  481.4 5.5 collective-permute-start.36
  485.6 5.5 collective-permute-start.37
  491.1 4.6 collective-permute-start.38
  494.4 5.5 collective-permute-start.39
  500.0 3.5 collective-permute-start.40
  (14 other events, 199.1 us)
where the time goes:
time: 556 us; the launch traced here: 553 us
  blocking collectives  322 us (58%)
  starting transfers between devices  89.3 us (16%)
  waiting for transfers between devices  55.6 us (10%)
  matrix products  41.5 us (7%)
  other arithmetic  24.3 us (4%)
  local copies, waits for them, and re-layouts  8.86 us (2%)
  loops' own time  5.94 us (1%)
    psum x5, blocking collectives, totals_norm(): lax.psum(jnp.sum(residual * residual, axis=(1, 2)), ('gx', 'gy', 'gz'))  204 us
    psum x3, blocking collectives, totals_curve(): return lax.psum(jnp.sum(direction * image, axis=(1, 2)), ('gx', 'gy', 'gz'))  119 us
    ppermute x21, starting transfers between devices, with_halo(): lax.ppermute(lax.slice_in_dim(block, block.shape[dim] - width, None, axis...  61.5 us
    ppermute x21, waiting for transfers between devices, with_halo(): lax.ppermute(lax.slice_in_dim(block, 0, width, axis=dim), axis, backward)  55 us
    dot_general x5, matrix products, pairs(): mixed = jnp.einsum('bkij,cbkj->cbi', tiles, beside_all, precision=HIGHEST)  30.7 us
    ppermute x21, starting transfers between devices, with_halo(): lax.ppermute(lax.slice_in_dim(block, 0, width, axis=dim), axis, backward)  27.8 us
    dynamic_update_slice x3, other arithmetic, local(): tiles = lax.map(tile_of, jnp.arange(nblocks, dtype=jnp.int32))  12.7 us
  transfers between devices with their start and end apart: 42, of which 21 were waited for; matrix products, arithmetic and copies ran while one was open for 1% of the time, Pallas kernels for 0%

commit v1 on v0

v1 whole, which is shorter than its diff:
```python
import functools

import jax
import jax.numpy as jnp
from jax import lax
from jax.experimental import pallas as pl
from jax.experimental.pallas import tpu as pltpu
from jax.sharding import PartitionSpec as P

VISCOUS = 4.0
STIFFNESS = 0.25
GRAVITY_STEP = 0.5
AXES = ("gx", "gy", "gz")
FAR = 1.0e4
LANES = 128


def exchange(send):
    return lax.all_to_all(send, AXES, 0, 0, tiled=True)


class Plan:
    def __init__(self, mesh, blocks, width):
        self.count = [mesh.shape[axis] for axis in AXES]
        self.devices = self.count[0] * self.count[1] * self.count[2]
        self.blocks = blocks
        self.width = width
        self.deep = blocks + 2
        self.ring = 9 * self.deep
        self.pad = -(-self.ring // 8) * 8
        self.cube = (2.0 / width) ** (1.0 / 3.0)
        self.unit = self.cube ** 0.5

    def own(self, block):
        return 4 * self.deep + block + 1

    def beside(self, block, code):
        return (code // 3) * self.deep + block + code % 3


def rows_of(plan, field):
    return slice(field * plan.pad, field * plan.pad + plan.ring)


def slots(plan):
    place = [lax.axis_index(axis) for axis in AXES]
    found = {}
    for code in range(27):
        at = [place[0] + code // 9 - 1, place[1] + code // 3 % 3 - 1, place[2] + code % 3 - 1]
        present = None
        slot = 0
        for value, count in zip(at, plan.count):
            inside = jnp.logical_and(value >= 0, value < count)
            present = inside if present is None else jnp.logical_and(present, inside)
            slot = slot * count + jnp.clip(value, 0, count - 1)
        found[code] = (slot, present)
    return found


def gather_ring(plan, found, recv, fields, store):
    for column in range(9):
        for level in range(plan.deep):
            if level == 0:
                code, block = column * 3, plan.blocks - 1
            elif level == plan.deep - 1:
                code, block = column * 3 + 2, 0
            else:
                code, block = column * 3 + 1, level - 1
            slot, present = found[code]
            for field in range(fields):
                row = recv[slot, field * plan.blocks + block]
                store(field, column * plan.deep + level, column, level, row, present)


def ring_into(plan, found, recv, fields, ref):
    def store(field, at, column, level, row, present):
        ref[pl.ds(field * plan.pad + at, 1), :] = row

    gather_ring(plan, found, recv, fields, store)


def lane_ids():
    return lax.broadcasted_iota(jnp.int32, (1, LANES), 1)


def totals(recv, row, number):
    summed = jnp.sum(recv[:, row], axis=0)
    lane = lane_ids()
    return [
        jnp.sum(jnp.where(lane == m, summed, 0.0), axis=1, keepdims=True) for m in range(number)
    ]


def pack(partials):
    lane = lane_ids()
    row = jnp.zeros((1, LANES), jnp.float32)
    for m, partial in enumerate(partials):
        row = jnp.where(lane == m, jnp.sum(partial, axis=1, keepdims=True), row)
    return row


def dot(first, second):
    total = first[0] * second[0]
    for a, b in zip(first[1:], second[1:]):
        total = total + a * b
    return total


def spread(plan, send, rows):
    def body(slot, carry):
        for r, row in enumerate(rows):
            send[slot, r] = row
        return carry

    lax.fori_loop(0, plan.devices, body, 0)


def columns_to_rows(plan, cols, rows, number):
    for block in range(plan.blocks):
        flipped = jnp.transpose(cols[block])
        rows[block] = flipped[0:8]


def apply_tiles(plan, tiles, fields, cols, chunk):
    lane = lax.broadcasted_iota(jnp.int32, (chunk, LANES), 1)

    def body(step, carry):
        start = pl.multiple_of(step * chunk, chunk)
        for block in range(plan.blocks):
            sums = [None] * len(fields)
            for code in range(27):
                at = plan.beside(block, code)
                tile = tiles[block * 27 + code, pl.ds(start, chunk), :]
                for f, (ref, base) in enumerate(fields):
                    term = tile * ref[pl.ds(base + at, 1), :]
                    sums[f] = term if sums[f] is None else sums[f] + term
            merged = jnp.zeros((chunk, LANES), jnp.float32)
            for f, total in enumerate(sums):
                merged = jnp.where(lane == f, jnp.sum(total, axis=1, keepdims=True), merged)
            cols[block, pl.ds(start, chunk), :] = merged
        return carry

    lax.fori_loop(0, plan.width // chunk, body, 0)


def pack_kernel(plan, counts, offsets, velocity, send):
    lane = lane_ids()
    rows = []
    for axis in range(3):
        for block in range(plan.blocks):
            valid = lane < counts[0, 0, block]
            row = offsets[axis, 0, 0, pl.ds(block, 1), :]
            rows.append(jnp.where(valid, row, FAR) if axis == 0 else row)
    for axis in range(3):
        for block in range(plan.blocks):
            valid = lane < counts[0, 0, block]
            row = velocity[axis, 0, 0, pl.ds(block, 1), :]
            if axis == 0:
                row = row + GRAVITY_STEP
            rows.append(jnp.where(valid, row, 0.0))
    spread(plan, send, rows)


def build_kernel(plan, recv, send, tiles, where, right, state, cols, rows):
    found = slots(plan)

    def store(field, at, column, level, row, present):
        if field < 3:
            shift = (column // 3 - 1, column % 3 - 1, level - 1)[field]
            row = plan.unit * (row + shift)
            if field == 0:
                row = jnp.where(present, row, FAR)
            where[pl.ds(field * plan.pad + at, 1), :] = row
        else:
            row = jnp.where(present, row, 0.0)
            right[pl.ds((field - 3) * plan.pad + at, 1), :] = row

    gather_ring(plan, found, recv, 6, store)
    chunk = 32
    lane = lax.broadcasted_iota(jnp.int32, (chunk, LANES), 1)
    sub = lax.broadcasted_iota(jnp.int32, (chunk, LANES), 0)

    def body(step, carry):
        start = pl.multiple_of(step * chunk, chunk)
        eye = lane == sub + start
        for block in range(plan.blocks):
            centre = []
            for axis in range(3):
                row = where[pl.ds(axis * plan.pad + plan.own(block), 1), :]
                if axis == 0:
                    row = jnp.where(row > 0.25 * FAR, -FAR, row)
                column = jnp.sum(jnp.where(eye, row, 0.0), axis=1, keepdims=True)
                centre.append(jnp.broadcast_to(column, (chunk, LANES)))
            sums = [None] * 7
            for code in range(27):
                at = plan.beside(block, code)
                near = [where[pl.ds(axis * plan.pad + at, 1), :] for axis in range(3)]
                rest = plan.cube
                for axis in range(3):
                    apart = near[axis] - centre[axis]
                    rest = rest - apart * apart
                bump = jnp.maximum(rest, 0.0)
                tile = bump * bump * bump
                tiles[block * 27 + code, pl.ds(start, chunk), :] = tile
                terms = [tile]
                for axis in range(3):
                    terms.append(tile * right[pl.ds(axis * plan.pad + at, 1), :])
                for axis in range(3):
                    terms.append(tile * near[axis])
                sums = [t if s is None else s + t for s, t in zip(sums, terms)]
            merged = jnp.zeros((chunk, LANES), jnp.float32)
            for f, total in enumerate(sums):
                merged = jnp.where(lane == f, jnp.sum(total, axis=1, keepdims=True), merged)
            cols[block, pl.ds(start, chunk), :] = merged
        return carry

    lax.fori_loop(0, plan.width // chunk, body, 0)
    columns_to_rows(plan, cols, rows, 7)
    image = [[None] * plan.blocks for _ in range(3)]
    whole = [[None] * plan.blocks for _ in range(3)]
    start = [[None] * plan.blocks for _ in range(3)]
    for block in range(plan.blocks):
        reach = rows[block, pl.ds(0, 1), :]
        state[pl.ds(block, 1), :] = reach
        for axis in range(3):
            field = right[pl.ds(axis * plan.pad + plan.own(block), 1), :]
            start[axis][block] = field
            image[axis][block] = reach * field - rows[block, pl.ds(1 + axis, 1), :]
            whole[axis][block] = field + VISCOUS * image[axis][block]
            spot = where[pl.ds(axis * plan.pad + plan.own(block), 1), :]
            state[pl.ds((1 + axis) * plan.blocks + block, 1), :] = (
                reach * spot - rows[block, pl.ds(4 + axis, 1), :]
            )
    partials = []
    for axis in range(3):
        partials.append(dot(start[axis], start[axis]))
        partials.append(dot(start[axis], whole[axis]))
        partials.append(dot(whole[axis], whole[axis]))
    spread(plan, send, sum(image, []) + [pack(partials)])


def second_kernel(plan, recv, tiles, right, state, send, residual, direction, scalars, image, cols, rows):
    found = slots(plan)
    ring_into(plan, found, recv, 3, image)
    sums = totals(recv, 3 * plan.blocks, 9)
    for axis in range(3):
        current, curve, square = sums[3 * axis : 3 * axis + 3]
        alpha = current / curve
        following = jnp.maximum(alpha * alpha * square - current, 0.0)
        beta = following / current
        span = rows_of(plan, axis)
        field = right[span, :]
        left = field - alpha * (field + VISCOUS * image[span, :])
        residual[span, :] = left
        direction[span, :] = left + beta * field
        scalars[pl.ds(axis, 1), :] = jnp.broadcast_to(alpha, (1, LANES))
        for block in range(plan.blocks):
            at = 3 + axis * plan.blocks + block
            scalars[pl.ds(at, 1), :] = image[pl.ds(axis * plan.pad + plan.own(block), 1), :]
    apply_tiles(plan, tiles, [(direction, axis * plan.pad) for axis in range(3)], cols, 64)
    columns_to_rows(plan, cols, rows, 3)
    out = []
    partials = []
    for axis in range(3):
        left, ahead, shot, whole = [], [], [], []
        for block in range(plan.blocks):
            at = axis * plan.pad + plan.own(block)
            left.append(residual[pl.ds(at, 1), :])
            ahead.append(direction[pl.ds(at, 1), :])
            shot.append(state[pl.ds(block, 1), :] * ahead[block] - rows[block, pl.ds(axis, 1), :])
            whole.append(ahead[block] + VISCOUS * shot[block])
        out.extend(shot)
        partials.append(dot(left, left))
        partials.append(dot(ahead, whole))
        partials.append(dot(left, whole))
        partials.append(dot(whole, whole))
    spread(plan, send, out + [pack(partials)])


def third_kernel(
    plan, recv, tiles, where, right, residual, direction, state, scalars,
    send, ends, image, sofar, ahead, product, moved, cols, rows,
):
    found = slots(plan)
    ring_into(plan, found, recv, 3, image)
    sums = totals(recv, 3 * plan.blocks, 12)
    alphas = []
    left = []
    for axis in range(3):
        current, curve, cross, square = sums[4 * axis : 4 * axis + 4]
        alpha = current / curve
        following = jnp.maximum(current - 2.0 * alpha * cross + alpha * alpha * square, 0.0)
        beta = following / current
        alphas.append(alpha)
        span = rows_of(plan, axis)
        field = direction[span, :]
        rest = residual[span, :] - alpha * (field + VISCOUS * image[span, :])
        image[span, :] = rest
        fresh = rest + beta * field
        ahead[span, :] = fresh
        spot = where[span, :]
        product[span, :] = fresh * spot
        first = scalars[pl.ds(axis, 1), :]
        made = first * right[span, :] + alpha * field
        sofar[span, :] = made
        if axis == 0:
            carried = made * spot
        else:
            carried = carried + made * spot
    moved[rows_of(plan, 0), :] = carried
    fields = [(ahead, axis * plan.pad) for axis in range(3)]
    fields += [(product, axis * plan.pad) for axis in range(3)]
    fields += [(moved, 0)]
    apply_tiles(plan, tiles, fields, cols, 32)
    columns_to_rows(plan, cols, rows, 7)
    scale = 1.0 / plan.unit
    base = []
    each = [[None] * plan.blocks for _ in range(3)]
    rests = [[None] * plan.blocks for _ in range(3)]
    heads = [[None] * plan.blocks for _ in range(3)]
    wholes = [[None] * plan.blocks for _ in range(3)]
    for block in range(plan.blocks):
        reach = state[pl.ds(block, 1), :]
        own = plan.own(block)
        total = rows[block, pl.ds(6, 1), :] - reach * moved[pl.ds(own, 1), :]
        for axis in range(3):
            at = axis * plan.pad + own
            head = ahead[pl.ds(at, 1), :]
            spot = where[pl.ds(at, 1), :]
            lean = state[pl.ds((1 + axis) * plan.blocks + block, 1), :]
            shot = reach * head - rows[block, pl.ds(axis, 1), :]
            twice = reach * product[pl.ds(at, 1), :] - rows[block, pl.ds(3 + axis, 1), :]
            each[axis][block] = scale * (spot * shot + head * lean - twice)
            made = sofar[pl.ds(at, 1), :]
            first = scalars[pl.ds(axis, 1), :]
            before = scalars[pl.ds(3 + axis * plan.blocks + block, 1), :]
            latest = recv_own(plan, recv, found, axis, block)
            total = total + spot * (first * before + alphas[axis] * latest) + made * lean
            rests[axis][block] = image[pl.ds(at, 1), :]
            heads[axis][block] = head
            wholes[axis][block] = head + VISCOUS * shot
            ends[pl.ds(axis * plan.blocks + block, 1), :] = made
            ends[pl.ds((3 + axis) * plan.blocks + block, 1), :] = head
        base.append(scale * total)
    partials = []
    for axis in range(3):
        partials.append(dot(rests[axis], rests[axis]))
        partials.append(dot(heads[axis], wholes[axis]))
    spread(plan, send, base + sum(each, []) + [pack(partials)])


def recv_own(plan, recv, found, axis, block):
    return recv[found[13][0], axis * plan.blocks + block]


def fourth_kernel(plan, recv, tiles, ends, state, send, star, source, parts, cols, rows):
    found = slots(plan)
    ring_into(plan, found, recv, 4, parts)
    sums = totals(recv, 4 * plan.blocks, 6)
    gathered = parts[rows_of(plan, 0), :]
    for axis in range(3):
        alpha = sums[2 * axis] / sums[2 * axis + 1]
        gathered = gathered + alpha * parts[rows_of(plan, 1 + axis), :]
        for block in range(plan.blocks):
            star[axis, 0, 0, pl.ds(block, 1), :] = (
                ends[pl.ds(axis * plan.blocks + block, 1), :]
                + alpha * ends[pl.ds((3 + axis) * plan.blocks + block, 1), :]
            )
    source[rows_of(plan, 0), :] = -gathered
    apply_tiles(plan, tiles, [(source, 0)], cols, plan.width)
    columns_to_rows(plan, cols, rows, 1)
    field, shot, whole = [], [], []
    for block in range(plan.blocks):
        field.append(source[pl.ds(plan.own(block), 1), :])
        shot.append(state[pl.ds(block, 1), :] * field[block] - rows[block, pl.ds(0, 1), :])
        whole.append(STIFFNESS * field[block] + shot[block])
    spread(plan, send, shot + [pack([dot(field, field), dot(field, whole), dot(whole, whole)])])


def fifth_kernel(plan, recv, tiles, source, state, send, ends, image, ahead, cols, rows):
    found = slots(plan)
    ring_into(plan, found, recv, 1, image)
    current, curve, square = totals(recv, plan.blocks, 3)
    alpha = current / curve
    beta = jnp.maximum(alpha * alpha * square - current, 0.0) / current
    span = rows_of(plan, 0)
    field = source[span, :]
    left = field - alpha * (STIFFNESS * field + image[span, :])
    image[span, :] = left
    ahead[span, :] = left + beta * field
    apply_tiles(plan, tiles, [(ahead, 0)], cols, plan.width)
    columns_to_rows(plan, cols, rows, 1)
    rests, heads, wholes = [], [], []
    for block in range(plan.blocks):
        own = plan.own(block)
        rests.append(image[pl.ds(own, 1), :])
        heads.append(ahead[pl.ds(own, 1), :])
        shot = state[pl.ds(block, 1), :] * heads[block] - rows[block, pl.ds(0, 1), :]
        wholes.append(STIFFNESS * heads[block] + shot)
        ends[pl.ds(block, 1), :] = alpha * source[pl.ds(own, 1), :]
        ends[pl.ds(plan.blocks + block, 1), :] = heads[block]
    spread(plan, send, [pack([dot(rests, rests), dot(heads, wholes)])])


def last_kernel(plan, recv, ends, pressure):
    current, curve = totals(recv, 0, 2)
    alpha = current / curve
    for block in range(plan.blocks):
        pressure[0, 0, pl.ds(block, 1), :] = (
            ends[pl.ds(block, 1), :] + alpha * ends[pl.ds(plan.blocks + block, 1), :]
        )


def call(plan, kernel, operands, outs, scratch=(), smem=0):
    in_specs = [
        pl.BlockSpec(memory_space=pltpu.SMEM if i < smem else pltpu.VMEM)
        for i in range(len(operands))
    ]
    return pl.pallas_call(
        functools.partial(kernel, plan),
        out_shape=[jax.ShapeDtypeStruct(shape, jnp.float32) for shape in outs],
        in_specs=in_specs,
        out_specs=[pl.BlockSpec(memory_space=pltpu.VMEM) for _ in outs],
        scratch_shapes=[pltpu.VMEM(shape, jnp.float32) for shape in scratch],
        compiler_params=pltpu.CompilerParams(vmem_limit_bytes=48 * 1024 * 1024),
        name=kernel.__name__,
    )(*operands)


def local(mesh, offsets, velocity, counts, neighbours):
    blocks = counts.shape[2]
    width = offsets.shape[-1]
    plan = Plan(mesh, blocks, width)
    slot = lambda rows: (plan.devices, rows, 1, width)
    ring = lambda fields: (fields * plan.pad, width)
    cols = (blocks, width, LANES)
    rows = (blocks, 8, LANES)
    (send,) = call(plan, pack_kernel, [counts, offsets, velocity], [slot(6 * blocks)], smem=1)
    recv = exchange(send)
    send, tiles, where, right, state = call(
        plan, build_kernel, [recv],
        [slot(3 * blocks + 1), (27 * blocks, width, width), ring(3), ring(3), (4 * blocks, width)],
        [cols, rows],
    )
    recv = exchange(send)
    send, residual, direction, scalars = call(
        plan, second_kernel, [recv, tiles, right, state],
        [slot(3 * blocks + 1), ring(3), ring(3), (3 + 3 * blocks, width)],
        [ring(3), cols, rows],
    )
    recv = exchange(send)
    send, ends = call(
        plan, third_kernel, [recv, tiles, where, right, residual, direction, state, scalars],
        [slot(4 * blocks + 1), (6 * blocks, width)],
        [ring(3), ring(3), ring(3), ring(3), ring(1), cols, rows],
    )
    recv = exchange(send)
    send, star, source = call(
        plan, fourth_kernel, [recv, tiles, ends, state],
        [slot(blocks + 1), (3, 1, 1, blocks, width), ring(1)],
        [ring(4), cols, rows],
    )
    recv = exchange(send)
    send, ends = call(
        plan, fifth_kernel, [recv, tiles, source, state],
        [slot(1), (2 * blocks, width)],
        [ring(1), ring(1), cols, rows],
    )
    recv = exchange(send)
    (pressure,) = call(plan, last_kernel, [recv, ends], [(1, 1, blocks, width)])
    return star, pressure


def solution(mesh):
    in_specs = (
        P(None, "gx", "gy", "gz", None),
        P(None, "gx", "gy", "gz", None),
        P("gx", "gy", "gz"),
        P("gx", "gy", "gz", None),
    )
    out_specs = (P(None, "gx", "gy", "gz", None), P("gx", "gy", "gz", None))
    return jax.shard_map(
        functools.partial(local, mesh),
        mesh=mesh, in_specs=in_specs, out_specs=out_specs, check_vma=False,
    )
```

time: 556 us -> 90.8 us (0.16)
  blocking collectives: 322 us -> 60.7 us
  starting transfers between devices: 89.3 us -> 2.48 us
  waiting for transfers between devices: 55.6 us -> 6.55 us
  matrix products: 41.5 us -> 0 us
  other arithmetic: 24.3 us -> 0 us
  Pallas kernels: 0 us -> 16.9 us
  loops' own time: 5.94 us -> 0 us
  local copies, waits for them, and re-layouts: 8.86 us -> 3.21 us
    psum x8 -> x0, blocking collectives: 322 us -> none  [the longest x5 204 us: totals_norm(): lax.psum(jnp.sum(residual * residual, axis=(1, 2)), ('gx', 'gy', 'gz'))]
    ppermute x42 -> x0, starting transfers between devices: 89.3 us -> none  [the longest x21 61.5 us: with_halo(): lax.ppermute(lax.slice_in_dim(block, block.shape[dim] - width, None, axis...]
    all_to_all x0 -> x5, blocking collectives: none -> 60.7 us  [exchange(): return lax.all_to_all(send, AXES, 0, 0, tiled=True)]
    ppermute x42 -> x0, waiting for transfers between devices: 55.6 us -> none  [the longest x21 55 us: with_halo(): lax.ppermute(lax.slice_in_dim(block, 0, width, axis=dim), axis, backward)]
    dot_general x6 -> x0, matrix products: 41.5 us -> none  [the longest x5 30.7 us: pairs(): mixed = jnp.einsum('bkij,cbkj->cbi', tiles, beside_all, precision=HIGHEST)]
    pallas_call x0 -> x7, Pallas kernels: none -> 16.9 us  [call(): pl.pallas_call(functools.partial(kernel, plan), out_shape=[jax.ShapeDtype...]
    dynamic_update_slice x3 -> x0, other arithmetic: 12.7 us -> none  [local(): tiles = lax.map(tile_of, jnp.arange(nblocks, dtype=jnp.int32))]
    reduce_sum x7 -> x0, other arithmetic: 6.76 us -> none  [the longest x1 4.18 us: local(): row_parts = jnp.sum(tiles, axis=3)]
  transfers between devices with their start and end apart: 42 -> 1, of which waited for: 21 -> 1; matrix products, arithmetic and copies ran while one was open for 1% -> 1% of each run, Pallas kernels for 0% -> 0%
where the time goes in v1:
time: 90.8 us; the launch traced here: 90.5 us
  blocking collectives  60.7 us (67%)
  Pallas kernels  16.9 us (19%)
  waiting for transfers between devices  6.55 us (7%)
  local copies, waits for them, and re-layouts  3.21 us (4%)
  starting transfers between devices  2.48 us (3%)
    all_to_all x5, blocking collectives, exchange(): return lax.all_to_all(send, AXES, 0, 0, tiled=True)  60.7 us
    pallas_call x7, Pallas kernels, call(): pl.pallas_call(functools.partial(kernel, plan), out_shape=[jax.ShapeDtype...  16.9 us
    all_to_all x1, waiting for transfers between devices, exchange(): return lax.all_to_all(send, AXES, 0, 0, tiled=True)  6.55 us
    unnamed x6, local copies, waits for them, and re-layouts  3.21 us
    all_to_all x1, starting transfers between devices, exchange(): return lax.all_to_all(send, AXES, 0, 0, tiled=True)  2.48 us
  transfers between devices with their start and end apart: 1, of which 1 were waited for; matrix products, arithmetic and copies ran while one was open for 1% of the time, Pallas kernels for 0%

profile of v1, /device:TPU:0, one launch (start us, length us, event | category | flops | bytes accessed | tf_op | source)
XLA Modules:
  0.0 90.5 jit_solution(8142292874191320845)
XLA Ops:
  0.6 0.7 copy.5.offsets
  1.3 0.7 copy.6.velocity
  2.0 0.0 copy-start
  2.0 0.7 copy-done
  2.7 0.7 pack_kernel.1
  3.4 18.5 %all_to_all.30.recv = f32[32,18,1,128]{3,2,1,0:T(1,128)S(1)} all-to-all(f32[32,18,1,128]{3,2,1,0:T(1,128)S(1)} %pack_kernel.1), channel_id=1, replica_groups=mesh['gx'=4,'gy'=4,'gz'=2] {'gx','gy','gz'}, dimensions={0} | all-to-all | bytes 589824 | tf_op jit(solution)/shard_map/all_to_all | solution.py:19
  22.0 6.5 %build_kernel.1 = (f32[32,10,1,128]{3,2,1,0:T(1,128)S(1)}, f32[81,128,128]{2,1,0:T(8,128)S(1)}, f32[144,128]{1,0:T(8,128)S(1)}, f32[144,128]{1,0:T(8,128)S(1)}, f32[12,128]{1,0:T(8,128)S(1)}) custom-call(f32[32,18,1,128]{3,2,1,0:T(1,128)S(1)} %all_to_all.30.recv), custom_call_target="tpu_custom_call" | custom-call | tf_op jit(solution)/shard_map/build_kernel/pallas_call | solution.py:419
  28.4 10.4 %all_to_all.31.recv = f32[32,10,1,128]{3,2,1,0:T(1,128)S(1)} all-to-all(f32[32,10,1,128]{3,2,1,0:T(1,128)S(1)} %get-tuple-element.18), channel_id=1, replica_groups=mesh['gx'=4,'gy'=4,'gz'=2] {'gx','gy','gz'}, dimensions={0} | all-to-all | bytes 327680 | tf_op jit(solution)/shard_map/all_to_all | solution.py:19
  38.9 2.1 %second_kernel.1 = (f32[32,10,1,128]{3,2,1,0:T(1,128)S(1)}, f32[144,128]{1,0:T(8,128)S(1)}, f32[144,128]{1,0:T(8,128)S(1)}, f32[12,128]{1,0:T(8,128)S(1)}) custom-call(f32[32,10,1,128]{3,2,1,0:T(1,128)S(1)} %all_to_all.31.recv, f32[81,128,128]{2,1,0:T(8,128)S(1)} %get-tuple-element.19.tiles, f32[144,128]{1,0:T(8,128)S(1)} %get-tuple-element.20.right, ...), custom_call_target="tpu_custom_call" | custom-call | tf_op jit(solution)/shard_map/second_kernel/pallas_call | solution.py:419
  41.0 10.6 %all_to_all.32.recv = f32[32,10,1,128]{3,2,1,0:T(1,128)S(1)} all-to-all(f32[32,10,1,128]{3,2,1,0:T(1,128)S(1)} %get-tuple-element.22), channel_id=1, replica_groups=mesh['gx'=4,'gy'=4,'gz'=2] {'gx','gy','gz'}, dimensions={0} | all-to-all | bytes 327680 | tf_op jit(solution)/shard_map/all_to_all | solution.py:19
  51.5 5.1 %third_kernel.1 = (f32[32,13,1,128]{3,2,1,0:T(1,128)S(1)}, f32[18,128]{1,0:T(8,128)S(1)}) custom-call(f32[32,10,1,128]{3,2,1,0:T(1,128)S(1)} %all_to_all.32.recv, f32[81,128,128]{2,1,0:T(8,128)S(1)} %get-tuple-element.19.tiles, f32[144,128]{1,0:T(8,128)S(1)} %get-tuple-element.23.where, f32[144,128]{1,0:T(8,128)S(1)} %get-tuple-element.20.right, ...), custom_call_target="tpu_custom_call" | custom-call | tf_op jit(solution)/shard_map/third_kernel/pallas_call | solution.py:419
  56.7 11.1 %all_to_all.33.recv = f32[32,13,1,128]{3,2,1,0:T(1,128)S(1)} all-to-all(f32[32,13,1,128]{3,2,1,0:T(1,128)S(1)} %get-tuple-element.27), channel_id=1, replica_groups=mesh['gx'=4,'gy'=4,'gz'=2] {'gx','gy','gz'}, dimensions={0} | all-to-all | bytes 425984 | tf_op jit(solution)/shard_map/all_to_all | solution.py:19
  67.8 0.9 fourth_kernel.1
  68.6 10.1 %all_to_all.34.recv = f32[32,4,1,128]{3,2,1,0:T(1,128)S(1)} all-to-all(f32[32,4,1,128]{3,2,1,0:T(1,128)S(1)} %get-tuple-element.30), channel_id=1, replica_groups=mesh['gx'=4,'gy'=4,'gz'=2] {'gx','gy','gz'}, dimensions={0} | all-to-all | bytes 131072 | tf_op jit(solution)/shard_map/all_to_all | solution.py:19
  78.7 1.5 %fifth_kernel.1 = (f32[32,1,1,128]{3,2,1,0:T(1,128)}, f32[6,128]{1,0:T(8,128)S(1)}) custom-call(f32[32,4,1,128]{3,2,1,0:T(1,128)S(1)} %all_to_all.34.recv, f32[81,128,128]{2,1,0:T(8,128)S(1)} %get-tuple-element.19.tiles, f32[48,128]{1,0:T(8,128)S(1)} %get-tuple-element.31.source, f32[12,128]{1,0:T(8,128)S(1)} %get-tuple-element.21.state), custom_call_target="tpu_custom_call" | custom-call | tf_op jit(solution)/shard_map/fifth_kernel/pallas_call | solution.py:419
  80.2 2.5 %all-to-all-start.5 = ((f32[32,1,1,128]{3,2,1,0:T(1,128)}), f32[32,1,1,128]{3,2,1,0:T(1,128)S(1)}, u32[]{:S(2)}, u32[]{:S(2)}) async-start(f32[32,1,1,128]{3,2,1,0:T(1,128)} %get-tuple-element.32), calls=%async_computation.5 | async-start | bytes 32768 | tf_op jit(solution)/shard_map/all_to_all | solution.py:19
  82.7 0.6 copy.7
  83.3 6.5 %all-to-all-done.5.recv = f32[32,1,1,128]{3,2,1,0:T(1,128)S(1)} async-done(((f32[32,1,1,128]{3,2,1,0:T(1,128)}), f32[32,1,1,128]{3,2,1,0:T(1,128)S(1)}, u32[]{:S(2)}, u32[]{:S(2)}) %all-to-all-start.5) | async-done | bytes 16416 | tf_op jit(solution)/shard_map/all_to_all | solution.py:19
  89.8 0.1 last_kernel.1
  89.9 0.6 copy.8
Async XLA Ops:
  2.0 0.7 copy-start
  80.2 9.6 %all-to-all-start.5 = ((f32[32,1,1,128]{3,2,1,0:T(1,128)}), f32[32,1,1,128]{3,2,1,0:T(1,128)S(1)}, u32[]{:S(2)}, u32[]{:S(2)}) async-start(f32[32,1,1,128]{3,2,1,0:T(1,128)} %get-tuple-element.32), calls=%async_computation.5 | async-start | bytes 32768 | tf_op jit(solution)/shard_map/all_to_all | solution.py:19

commit v2 on v1

v2 whole, which is shorter than its diff:
```python
import functools

import jax
import jax.numpy as jnp
from jax import lax
from jax.experimental import pallas as pl
from jax.experimental.pallas import tpu as pltpu
from jax.sharding import PartitionSpec as P

VISCOUS = 4.0
STIFFNESS = 0.25
GRAVITY_STEP = 0.5
AXES = ("gx", "gy", "gz")
FAR = 1.0e3
LANES = 128


def exchange(send):
    return lax.all_to_all(send, AXES, 0, 0, tiled=True)


class Plan:
    def __init__(self, mesh, blocks, width):
        self.count = [mesh.shape[axis] for axis in AXES]
        self.devices = self.count[0] * self.count[1] * self.count[2]
        self.blocks = blocks
        self.width = width
        self.deep = blocks + 2
        self.ring = 9 * self.deep
        self.cube = (2.0 / width) ** (1.0 / 3.0)
        self.unit = self.cube ** 0.5

    def own(self, block):
        return 4 * self.deep + block + 1


def slots(plan):
    place = [lax.axis_index(axis) for axis in AXES]
    found = {}
    for code in range(27):
        at = [place[0] + code // 9 - 1, place[1] + code // 3 % 3 - 1, place[2] + code % 3 - 1]
        present = None
        slot = 0
        for value, count in zip(at, plan.count):
            inside = jnp.logical_and(value >= 0, value < count)
            present = inside if present is None else jnp.logical_and(present, inside)
            slot = slot * count + jnp.clip(value, 0, count - 1)
        found[code] = (slot, present)
    return found


def gather_ring(plan, found, recv, fields, store):
    for column in range(9):
        for level in range(plan.deep):
            if level == 0:
                code, block = column * 3, plan.blocks - 1
            elif level == plan.deep - 1:
                code, block = column * 3 + 2, 0
            else:
                code, block = column * 3 + 1, level - 1
            slot, present = found[code]
            rows = [recv[slot, field * plan.blocks + block] for field in range(fields)]
            store(column * plan.deep + level, column, level, rows, present)


def ring_into(plan, found, recv, fields, ref):
    def store(at, column, level, rows, present):
        for field, row in enumerate(rows):
            ref[at, pl.ds(field, 1), :] = row

    gather_ring(plan, found, recv, fields, store)


def lane_ids(sublanes=1):
    return lax.broadcasted_iota(jnp.int32, (sublanes, LANES), 1)


def sublane_ids():
    return lax.broadcasted_iota(jnp.int32, (8, LANES), 0)


def totals(recv, row, number):
    summed = jnp.broadcast_to(jnp.sum(recv[:, row], axis=0), (8, LANES))
    place = lane_ids(8) - sublane_ids()
    return [
        jnp.broadcast_to(
            jnp.sum(jnp.where(place == 8 * m, summed, 0.0), axis=1, keepdims=True), (8, LANES)
        )
        for m in range(number)
    ]


def pack(groups):
    lane = lane_ids()
    row = jnp.zeros((1, LANES), jnp.float32)
    for m, group in enumerate(groups):
        for c, partial in enumerate(group):
            row = jnp.where(lane == 8 * m + c, jnp.sum(partial, axis=1, keepdims=True), row)
    return row


def dot(first, second):
    total = first[0] * second[0]
    for a, b in zip(first[1:], second[1:]):
        total = total + a * b
    return total


def spread(plan, send, rows):
    def body(slot, carry):
        for r, row in enumerate(rows):
            send[slot, r] = row
        return carry

    lax.fori_loop(0, plan.devices, body, 0)


def coarse(value):
    return value.astype(jnp.bfloat16).astype(jnp.float32)


def split(value):
    first = coarse(value)
    rest = value - first
    second = coarse(rest)
    return first, second, rest - second


def split_ring(plan, ref, packed):
    for at in range(plan.ring):
        first, second, third = split(ref[at])
        stacked = jnp.concatenate([first, second, third, jnp.zeros_like(third)], axis=0)
        packed[:, pl.ds(at * LANES, LANES)] = stacked.astype(jnp.bfloat16)


def tile_sum(plan, tiles, packed, block, column):
    ahead = packed[:, pl.ds((column * plan.deep + block) * LANES, 3 * LANES)]
    return jnp.dot(
        jnp.concatenate([ahead, ahead], axis=1),
        tiles[block * 9 + column],
        preferred_element_type=jnp.float32,
    )


def fold(total):
    return total[0:8] + total[8:16] + total[16:24]


def apply_tiles(plan, tiles, ring, packed, rows):
    split_ring(plan, ring, packed)
    for block in range(plan.blocks):
        total = tile_sum(plan, tiles, packed, block, 0)
        for column in range(1, 9):
            total = total + tile_sum(plan, tiles, packed, block, column)
        rows[block] = fold(total)


def pack_kernel(plan, counts, offsets, velocity, send):
    lane = lane_ids()
    rows = []
    for axis in range(3):
        for block in range(plan.blocks):
            valid = lane < counts[0, 0, block]
            row = offsets[axis * plan.blocks + block]
            rows.append(jnp.where(valid, row, FAR) if axis == 0 else row)
    for axis in range(3):
        for block in range(plan.blocks):
            valid = lane < counts[0, 0, block]
            row = velocity[axis * plan.blocks + block]
            if axis == 0:
                row = row + GRAVITY_STEP
            rows.append(jnp.where(valid, row, 0.0))
    spread(plan, send, rows)


def build_kernel(plan, recv, send, tiles, where, right, state, points, flipped, mixed, packed, rows):
    found = slots(plan)

    def store(at, column, level, got, present):
        shift = (column // 3 - 1, column % 3 - 1, level - (plan.deep - 1) // 2)
        spots = [plan.unit * (got[axis] + shift[axis]) for axis in range(3)]
        spots[0] = jnp.where(present, spots[0], FAR)
        points[at, pl.ds(3, 1), :] = spots[0] * spots[0] + spots[1] * spots[1] + spots[2] * spots[2]
        points[at, pl.ds(4, 1), :] = jnp.ones((1, LANES), jnp.float32)
        points[at, pl.ds(5, 3), :] = jnp.zeros((3, LANES), jnp.float32)
        mixed[at, pl.ds(3, 1), :] = jnp.ones((1, LANES), jnp.float32)
        mixed[at, pl.ds(7, 1), :] = jnp.zeros((1, LANES), jnp.float32)
        for axis in range(3):
            points[at, pl.ds(axis, 1), :] = spots[axis]
            where[at, pl.ds(axis, 1), :] = spots[axis]
            mixed[at, pl.ds(4 + axis, 1), :] = spots[axis]
            field = jnp.where(present, got[3 + axis], 0.0)
            right[at, pl.ds(axis, 1), :] = field
            mixed[at, pl.ds(axis, 1), :] = field

    gather_ring(plan, found, recv, 6, store)
    for at in range(plan.ring):
        first, second, third = split(points[at])
        stacked = jnp.concatenate([first, second, third, first, second, first], axis=0)
        padded = jnp.concatenate([stacked, jnp.zeros((LANES - 48, LANES), jnp.float32)], axis=0)
        flipped[pl.ds(at * plan.width, plan.width), :] = jnp.transpose(padded).astype(jnp.bfloat16)
    split_ring(plan, mixed, packed)
    sub = sublane_ids()
    for block in range(plan.blocks):
        own = points[plan.own(block)]
        own = jnp.where(jnp.logical_and(sub == 0, own > 0.25 * FAR), -FAR, own)
        square = jnp.broadcast_to(own[3:4], (8, LANES))
        own = jnp.where(sub < 3, 2.0 * own, 0.0)
        own = jnp.where(sub == 3, -1.0, own)
        own = jnp.where(sub == 4, plan.cube - square, own)
        first, second, third = split(own)
        stacked = jnp.concatenate([first, first, first, second, second, third], axis=0)
        padded = jnp.concatenate([stacked, jnp.zeros((LANES - 48, LANES), jnp.float32)], axis=0)
        centre = padded.astype(jnp.bfloat16)
        total = None
        for column in range(9):
            at = (column * plan.deep + block) * plan.width
            rest = jnp.dot(
                flipped[pl.ds(at, 3 * plan.width), :], centre, preferred_element_type=jnp.float32
            )
            bump = jnp.maximum(rest, 0.0)
            weight = bump * bump * bump
            high = weight.astype(jnp.bfloat16)
            tiles[block * 9 + column, pl.ds(0, 3 * plan.width), :] = high
            tiles[block * 9 + column, pl.ds(3 * plan.width, 3 * plan.width), :] = (
                weight - high.astype(jnp.float32)
            ).astype(jnp.bfloat16)
            part = tile_sum(plan, tiles, packed, block, column)
            total = part if total is None else total + part
        rows[block] = fold(total)
    image = [[None] * plan.blocks for _ in range(3)]
    whole = [[None] * plan.blocks for _ in range(3)]
    start = [[None] * plan.blocks for _ in range(3)]
    for block in range(plan.blocks):
        own = plan.own(block)
        reach = rows[block, pl.ds(3, 1), :]
        state[pl.ds(block, 1), :] = reach
        for axis in range(3):
            field = right[own, pl.ds(axis, 1), :]
            start[axis][block] = field
            image[axis][block] = reach * field - rows[block, pl.ds(axis, 1), :]
            whole[axis][block] = field + VISCOUS * image[axis][block]
            spot = where[own, pl.ds(axis, 1), :]
            state[pl.ds((1 + axis) * plan.blocks + block, 1), :] = (
                reach * spot - rows[block, pl.ds(4 + axis, 1), :]
            )
    groups = [
        [dot(start[axis], start[axis]) for axis in range(3)],
        [dot(start[axis], whole[axis]) for axis in range(3)],
        [dot(whole[axis], whole[axis]) for axis in range(3)],
    ]
    spread(plan, send, sum(image, []) + [pack(groups)])


def second_kernel(plan, recv, tiles, right, state, send, residual, direction, scalars, image, packed, rows):
    found = slots(plan)
    ring_into(plan, found, recv, 3, image)
    current, curve, square = totals(recv, 3 * plan.blocks, 3)
    alpha = current / curve
    following = jnp.maximum(alpha * alpha * square - current, 0.0)
    beta = following / current
    for at in range(plan.ring):
        field = right[at]
        left = field - alpha * (field + VISCOUS * image[at])
        residual[at] = left
        direction[at] = left + beta * field
    scalars[plan.blocks] = alpha
    for block in range(plan.blocks):
        scalars[block] = image[plan.own(block)]
    apply_tiles(plan, tiles, direction, packed, rows)
    out = []
    groups = [[], [], [], []]
    for axis in range(3):
        left, ahead, shot, whole = [], [], [], []
        for block in range(plan.blocks):
            own = plan.own(block)
            left.append(residual[own, pl.ds(axis, 1), :])
            ahead.append(direction[own, pl.ds(axis, 1), :])
            shot.append(state[pl.ds(block, 1), :] * ahead[block] - rows[block, pl.ds(axis, 1), :])
            whole.append(ahead[block] + VISCOUS * shot[block])
        out.extend(shot)
        groups[0].append(dot(left, left))
        groups[1].append(dot(ahead, whole))
        groups[2].append(dot(left, whole))
        groups[3].append(dot(whole, whole))
    spread(plan, send, out + [pack(groups)])


def third_kernel(
    plan, recv, tiles, where, right, residual, direction, state, scalars,
    send, ends, image, sofar, ahead, steps, packed, rows,
):
    found = slots(plan)
    ring_into(plan, found, recv, 3, image)
    current, curve, cross, square = totals(recv, 3 * plan.blocks, 4)
    alpha = current / curve
    following = jnp.maximum(current - 2.0 * alpha * cross + alpha * alpha * square, 0.0)
    beta = following / current
    first = scalars[plan.blocks]
    steps[...] = alpha
    sub = sublane_ids()
    for block in range(plan.blocks):
        own = plan.own(block)
        rows[block] = first * scalars[block] + alpha * image[own]
    latest = [
        [rows[block, pl.ds(axis, 1), :] for axis in range(3)] for block in range(plan.blocks)
    ]
    for at in range(plan.ring):
        field = direction[at]
        rest = residual[at] - alpha * (field + VISCOUS * image[at])
        fresh = rest + beta * field
        spot = where[at]
        made = first * right[at] + alpha * field
        moved = made * spot
        moved = pltpu.roll(moved, 6, 0) + pltpu.roll(moved, 5, 0) + pltpu.roll(moved, 4, 0)
        joined = jnp.where(sub < 3, fresh, pltpu.roll(fresh * spot, 3, 0))
        ahead[at] = jnp.where(sub < 6, joined, moved)
        if at - plan.own(0) in range(plan.blocks):
            image[at] = rest
            sofar[at - plan.own(0)] = made
    apply_tiles(plan, tiles, ahead, packed, rows)
    scale = 1.0 / plan.unit
    base = []
    each = [[None] * plan.blocks for _ in range(3)]
    rests = [[None] * plan.blocks for _ in range(3)]
    heads = [[None] * plan.blocks for _ in range(3)]
    wholes = [[None] * plan.blocks for _ in range(3)]
    for block in range(plan.blocks):
        reach = state[pl.ds(block, 1), :]
        own = plan.own(block)
        total = rows[block, pl.ds(6, 1), :] - reach * ahead[own, pl.ds(6, 1), :]
        for axis in range(3):
            head = ahead[own, pl.ds(axis, 1), :]
            spot = where[own, pl.ds(axis, 1), :]
            lean = state[pl.ds((1 + axis) * plan.blocks + block, 1), :]
            shot = reach * head - rows[block, pl.ds(axis, 1), :]
            twice = reach * ahead[own, pl.ds(3 + axis, 1), :] - rows[block, pl.ds(3 + axis, 1), :]
            each[axis][block] = scale * (spot * shot + head * lean - twice)
            made = sofar[block, pl.ds(axis, 1), :]
            total = total + spot * latest[block][axis] + made * lean
            rests[axis][block] = image[own, pl.ds(axis, 1), :]
            heads[axis][block] = head
            wholes[axis][block] = head + VISCOUS * shot
            ends[pl.ds(axis * plan.blocks + block, 1), :] = made
            ends[pl.ds((3 + axis) * plan.blocks + block, 1), :] = head
        base.append(scale * total)
    groups = [
        [dot(rests[axis], rests[axis]) for axis in range(3)],
        [dot(heads[axis], wholes[axis]) for axis in range(3)],
    ]
    spread(plan, send, base + sum(each, []) + [pack(groups)])


def fourth_kernel(plan, recv, tiles, ends, state, send, star, source, parts, steps, packed, rows):
    found = slots(plan)
    ring_into(plan, found, recv, 4, parts)
    current, curve = totals(recv, 4 * plan.blocks, 2)
    sub = sublane_ids()
    steps[...] = current / curve
    factor = jnp.where(sub == 0, 1.0, pltpu.roll(steps[...], 1, 0))
    for at in range(plan.ring):
        gathered = jnp.where(sub < 4, parts[at] * factor, 0.0)
        source[at] = jnp.broadcast_to(-jnp.sum(gathered, axis=0, keepdims=True), (8, LANES))
    for axis in range(3):
        alpha = steps[pl.ds(axis, 1), :]
        for block in range(plan.blocks):
            star[axis * plan.blocks + block] = (
                ends[pl.ds(axis * plan.blocks + block, 1), :]
                + alpha * ends[pl.ds((3 + axis) * plan.blocks + block, 1), :]
            )
    apply_tiles(plan, tiles, source, packed, rows)
    field, shot, whole = [], [], []
    for block in range(plan.blocks):
        field.append(source[plan.own(block), pl.ds(0, 1), :])
        shot.append(state[pl.ds(block, 1), :] * field[block] - rows[block, pl.ds(0, 1), :])
        whole.append(STIFFNESS * field[block] + shot[block])
    groups = [[dot(field, field)], [dot(field, whole)], [dot(whole, whole)]]
    spread(plan, send, shot + [pack(groups)])


def fifth_kernel(plan, recv, tiles, source, state, send, ends, image, ahead, steps, packed, rows):
    found = slots(plan)
    ring_into(plan, found, recv, 1, image)
    current, curve, square = totals(recv, plan.blocks, 3)
    steps[...] = current / curve
    alpha = steps[pl.ds(0, 1), :]
    steps[...] = jnp.maximum(alpha * alpha * square - current, 0.0) / current
    beta = steps[pl.ds(0, 1), :]
    for at in range(plan.ring):
        field = source[at]
        left = field - alpha * (STIFFNESS * field + image[at])
        image[at] = left
        ahead[at] = left + beta * field
    apply_tiles(plan, tiles, ahead, packed, rows)
    rests, heads, wholes = [], [], []
    for block in range(plan.blocks):
        own = plan.own(block)
        rests.append(image[own, pl.ds(0, 1), :])
        heads.append(ahead[own, pl.ds(0, 1), :])
        shot = state[pl.ds(block, 1), :] * heads[block] - rows[block, pl.ds(0, 1), :]
        wholes.append(STIFFNESS * heads[block] + shot)
        ends[pl.ds(block, 1), :] = alpha * source[own, pl.ds(0, 1), :]
        ends[pl.ds(plan.blocks + block, 1), :] = heads[block]
    spread(plan, send, [pack([[dot(rests, rests)], [dot(heads, wholes)]])])


def last_kernel(plan, recv, ends, pressure, steps):
    current, curve = totals(recv, 0, 2)
    steps[...] = current / curve
    alpha = steps[pl.ds(0, 1), :]
    for block in range(plan.blocks):
        pressure[block] = (
            ends[pl.ds(block, 1), :] + alpha * ends[pl.ds(plan.blocks + block, 1), :]
        )


def call(plan, kernel, operands, outs, scratch=(), smem=0):
    in_specs = [
        pl.BlockSpec(memory_space=pltpu.SMEM if i < smem else pltpu.VMEM)
        for i in range(len(operands))
    ]
    typed = lambda shape: (shape, jnp.float32) if isinstance(shape[0], int) else shape
    return pl.pallas_call(
        functools.partial(kernel, plan),
        out_shape=[jax.ShapeDtypeStruct(*typed(shape)) for shape in outs],
        in_specs=in_specs,
        out_specs=[pl.BlockSpec(memory_space=pltpu.VMEM) for _ in outs],
        scratch_shapes=[pltpu.VMEM(*typed(shape)) for shape in scratch],
        compiler_params=pltpu.CompilerParams(vmem_limit_bytes=24 * 1024 * 1024),
        name=kernel.__name__,
    )(*operands)


def local(mesh, offsets, velocity, counts, neighbours):
    blocks = counts.shape[2]
    width = offsets.shape[-1]
    plan = Plan(mesh, blocks, width)
    lined = lambda field: field.transpose(0, 1, 3, 2, 4).reshape(3 * blocks, 1, width)
    slot = lambda rows: (plan.devices, rows, 1, width)
    ring = (plan.ring, 8, width)
    tile = (8, width)
    rows = (blocks, 8, width)
    packed = ((32, plan.ring * width), jnp.bfloat16)
    (send,) = call(
        plan, pack_kernel, [counts, lined(offsets), lined(velocity)], [slot(6 * blocks)], smem=1
    )
    recv = exchange(send)
    send, tiles, where, right, state = call(
        plan, build_kernel, [recv],
        [
            slot(3 * blocks + 1), ((9 * blocks, 6 * width, width), jnp.bfloat16),
            ring, ring, (4 * blocks, width),
        ],
        [ring, ((plan.ring * width, LANES), jnp.bfloat16), ring, packed, rows],
    )
    recv = exchange(send)
    send, residual, direction, scalars = call(
        plan, second_kernel, [recv, tiles, right, state],
        [slot(3 * blocks + 1), ring, ring, (blocks + 1, 8, width)],
        [ring, packed, rows],
    )
    recv = exchange(send)
    send, ends = call(
        plan, third_kernel, [recv, tiles, where, right, residual, direction, state, scalars],
        [slot(4 * blocks + 1), (6 * blocks, width)],
        [ring, rows, ring, tile, packed, rows],
    )
    recv = exchange(send)
    send, star, source = call(
        plan, fourth_kernel, [recv, tiles, ends, state],
        [slot(blocks + 1), (3 * blocks, 1, width), ring],
        [ring, tile, packed, rows],
    )
    recv = exchange(send)
    send, ends = call(
        plan, fifth_kernel, [recv, tiles, source, state],
        [slot(1), (2 * blocks, width)],
        [ring, ring, tile, packed, rows],
    )
    recv = exchange(send)
    (pressure,) = call(plan, last_kernel, [recv, ends], [(blocks, 1, width)], [tile])
    star = star.reshape(3, 1, blocks, 1, width).transpose(0, 1, 3, 2, 4)
    pressure = pressure.reshape(1, blocks, 1, width).transpose(0, 2, 1, 3)
    return star, pressure


def solution(mesh):
    in_specs = (
        P(None, "gx", "gy", "gz", None),
        P(None, "gx", "gy", "gz", None),
        P("gx", "gy", "gz"),
        P("gx", "gy", "gz", None),
    )
    out_specs = (P(None, "gx", "gy", "gz", None), P("gx", "gy", "gz", None))
    return jax.shard_map(
        functools.partial(local, mesh),
        mesh=mesh, in_specs=in_specs, out_specs=out_specs, check_vma=False,
    )
```

time: 90.8 us -> 83.2 us (0.916)
  blocking collectives: 60.7 us -> 69.6 us
  waiting for transfers between devices: 6.55 us -> 0 us
  Pallas kernels: 16.9 us -> 10.6 us
  starting transfers between devices: 2.48 us -> 0 us
  local copies, waits for them, and re-layouts: 3.21 us -> 2.02 us
    all_to_all x5 -> x6, blocking collectives: 60.7 us -> 69.6 us  [exchange(): return lax.all_to_all(send, AXES, 0, 0, tiled=True)]
    all_to_all x1 -> x0, waiting for transfers between devices: 6.55 us -> none  [exchange(): return lax.all_to_all(send, AXES, 0, 0, tiled=True)]
    pallas_call x7, Pallas kernels: 16.9 us -> 10.6 us  [call(): pl.pallas_call(functools.partial(kernel, plan), out_shape=[jax.ShapeDtype...]
    all_to_all x1 -> x0, starting transfers between devices: 2.48 us -> none  [exchange(): return lax.all_to_all(send, AXES, 0, 0, tiled=True)]
    unnamed x6, local copies, waits for them, and re-layouts: 3.21 us -> 2.02 us
  transfers between devices with their start and end apart: 1 -> 0, of which waited for: 1 -> 0; matrix products, arithmetic and copies ran while one was open for 1% -> 0% of each run, Pallas kernels for 0% -> 0%
where the time goes in v2:
time: 83.2 us; the launch traced here: 82.9 us
  blocking collectives  69.6 us (84%)
  Pallas kernels  10.6 us (13%)
  local copies, waits for them, and re-layouts  2.02 us (2%)
    all_to_all x6, blocking collectives, exchange(): return lax.all_to_all(send, AXES, 0, 0, tiled=True)  69.6 us
    pallas_call x7, Pallas kernels, call(): pl.pallas_call(functools.partial(kernel, plan), out_shape=[jax.ShapeDtype...  10.6 us
    unnamed x6, local copies, waits for them, and re-layouts  2.02 us

profile of v2, /device:TPU:0, one launch (start us, length us, event | category | flops | bytes accessed | tf_op | source)
XLA Modules:
  0.0 82.9 jit_solution(1883467166426126541)
XLA Ops:
  0.6 0.0 copy-start
  0.6 0.7 copy-done
  1.3 0.0 copy-start.1
  1.3 0.7 copy-done.1
  2.0 0.0 copy-start.2
  2.0 0.7 copy-done.2
  2.7 0.7 pack_kernel.1
  3.4 18.5 %all_to_all.30.recv = f32[32,18,1,128]{3,2,1,0:T(1,128)S(1)} all-to-all(f32[32,18,1,128]{3,2,1,0:T(1,128)S(1)} %pack_kernel.1), channel_id=1, replica_groups=mesh['gx'=4,'gy'=4,'gz'=2] {'gx','gy','gz'}, dimensions={0} | all-to-all | bytes 589824 | tf_op jit(solution)/shard_map/all_to_all | solution.py:19
  22.0 3.1 %build_kernel.1 = (f32[32,10,1,128]{3,2,1,0:T(1,128)S(1)}, bf16[27,768,128]{2,1,0:T(8,128)(2,1)S(1)}, f32[45,8,128]{2,1,0:T(8,128)S(1)}, f32[45,8,128]{2,1,0:T(8,128)S(1)}, f32[12,128]{1,0:T(8,128)S(1)}) custom-call(f32[32,18,1,128]{3,2,1,0:T(1,128)S(1)} %all_to_all.30.recv), custom_call_target="tpu_custom_call" | custom-call | tf_op jit(solution)/shard_map/build_kernel/pallas_call | solution.py:423
  25.1 10.4 %all_to_all.31.recv = f32[32,10,1,128]{3,2,1,0:T(1,128)S(1)} all-to-all(f32[32,10,1,128]{3,2,1,0:T(1,128)S(1)} %get-tuple-element.18), channel_id=1, replica_groups=mesh['gx'=4,'gy'=4,'gz'=2] {'gx','gy','gz'}, dimensions={0} | all-to-all | bytes 327680 | tf_op jit(solution)/shard_map/all_to_all | solution.py:19
  35.6 1.4 %second_kernel.1 = (f32[32,10,1,128]{3,2,1,0:T(1,128)S(1)}, f32[45,8,128]{2,1,0:T(8,128)S(1)}, f32[45,8,128]{2,1,0:T(8,128)S(1)}, f32[4,8,128]{2,1,0:T(8,128)S(1)}) custom-call(f32[32,10,1,128]{3,2,1,0:T(1,128)S(1)} %all_to_all.31.recv, bf16[27,768,128]{2,1,0:T(8,128)(2,1)S(1)} %get-tuple-element.19.tiles, f32[45,8,128]{2,1,0:T(8,128)S(1)} %get-tuple-element.20.right, ...), custom_call_target="tpu_custom_call" | custom-call | tf_op jit(solution)/shard_map/second_kernel/pallas_call | solution.py:423
  36.9 10.6 %all_to_all.32.recv = f32[32,10,1,128]{3,2,1,0:T(1,128)S(1)} all-to-all(f32[32,10,1,128]{3,2,1,0:T(1,128)S(1)} %get-tuple-element.22), channel_id=1, replica_groups=mesh['gx'=4,'gy'=4,'gz'=2] {'gx','gy','gz'}, dimensions={0} | all-to-all | bytes 327680 | tf_op jit(solution)/shard_map/all_to_all | solution.py:19
  47.5 1.4 %third_kernel.1 = (f32[32,13,1,128]{3,2,1,0:T(1,128)S(1)}, f32[18,128]{1,0:T(8,128)S(1)}) custom-call(f32[32,10,1,128]{3,2,1,0:T(1,128)S(1)} %all_to_all.32.recv, bf16[27,768,128]{2,1,0:T(8,128)(2,1)S(1)} %get-tuple-element.19.tiles, f32[45,8,128]{2,1,0:T(8,128)S(1)} %get-tuple-element.23.where, f32[45,8,128]{2,1,0:T(8,128)S(1)} %get-tuple-element.20.right, ...), custom_call_target="tpu_custom_call" | custom-call | tf_op jit(solution)/shard_map/third_kernel/pallas_call | solution.py:423
  49.0 11.1 %all_to_all.33.recv = f32[32,13,1,128]{3,2,1,0:T(1,128)S(1)} all-to-all(f32[32,13,1,128]{3,2,1,0:T(1,128)S(1)} %get-tuple-element.27), channel_id=1, replica_groups=mesh['gx'=4,'gy'=4,'gz'=2] {'gx','gy','gz'}, dimensions={0} | all-to-all | bytes 425984 | tf_op jit(solution)/shard_map/all_to_all | solution.py:19
  60.0 1.9 %fourth_kernel.1 = (f32[32,4,1,128]{3,2,1,0:T(1,128)S(1)}, f32[9,1,128]{2,1,0:T(1,128)}, f32[45,8,128]{2,1,0:T(8,128)S(1)}) custom-call(f32[32,13,1,128]{3,2,1,0:T(1,128)S(1)} %all_to_all.33.recv, bf16[27,768,128]{2,1,0:T(8,128)(2,1)S(1)} %get-tuple-element.19.tiles, f32[18,128]{1,0:T(8,128)S(1)} %get-tuple-element.28.ends, ...), custom_call_target="tpu_custom_call" | custom-call | tf_op jit(solution)/shard_map/fourth_kernel/pallas_call | solution.py:423
  61.9 10.1 %all_to_all.34.recv = f32[32,4,1,128]{3,2,1,0:T(1,128)S(1)} all-to-all(f32[32,4,1,128]{3,2,1,0:T(1,128)S(1)} %get-tuple-element.30), channel_id=1, replica_groups=mesh['gx'=4,'gy'=4,'gz'=2] {'gx','gy','gz'}, dimensions={0} | all-to-all | bytes 131072 | tf_op jit(solution)/shard_map/all_to_all | solution.py:19
  72.0 1.3 %fifth_kernel.1 = (f32[32,1,1,128]{3,2,1,0:T(1,128)S(1)}, f32[6,128]{1,0:T(8,128)S(1)}) custom-call(f32[32,4,1,128]{3,2,1,0:T(1,128)S(1)} %all_to_all.34.recv, bf16[27,768,128]{2,1,0:T(8,128)(2,1)S(1)} %get-tuple-element.19.tiles, f32[45,8,128]{2,1,0:T(8,128)S(1)} %get-tuple-element.31.source, f32[12,128]{1,0:T(8,128)S(1)} %get-tuple-element.21.state), custom_call_target="tpu_custom_call" | custom-call | tf_op jit(solution)/shard_map/fifth_kernel/pallas_call | solution.py:423
  73.3 8.8 %all_to_all.35.recv = f32[32,1,1,128]{3,2,1,0:T(1,128)S(1)} all-to-all(f32[32,1,1,128]{3,2,1,0:T(1,128)S(1)} %get-tuple-element.32), channel_id=1, replica_groups=mesh['gx'=4,'gy'=4,'gz'=2] {'gx','gy','gz'}, dimensions={0} | all-to-all | bytes 32768 | tf_op jit(solution)/shard_map/all_to_all | solution.py:19
  82.2 0.7 last_kernel.1
Async XLA Ops:
  0.6 0.7 copy-start
  1.3 0.7 copy-start.1
  2.0 0.7 copy-start.2

commit v3 on v2

--- a/solution.py
+++ b/solution.py
@@ -17,6 +17,16 @@
 
 def exchange(send):
     return lax.all_to_all(send, AXES, 0, 0, tiled=True)
+
+
+def exchange_layers(plan, send):
+    level = lax.all_to_all(send, AXES[:2], 0, 0, tiled=True)
+    deep = plan.count[2]
+    if deep == 2:
+        return [level, lax.ppermute(level, AXES[2], [(0, 1), (1, 0)])]
+    forward = [(i, i + 1) for i in range(deep - 1)]
+    backward = [(target, source) for source, target in forward]
+    return [level] + [lax.ppermute(level, AXES[2], pairs) for pairs in (forward, backward)]
 
 
 class Plan:
@@ -34,32 +44,33 @@
         return 4 * self.deep + block + 1
 
 
-def slots(plan):
+def slots(plan, axes=3):
     place = [lax.axis_index(axis) for axis in AXES]
     found = {}
     for code in range(27):
         at = [place[0] + code // 9 - 1, place[1] + code // 3 % 3 - 1, place[2] + code % 3 - 1]
         present = None
         slot = 0
-        for value, count in zip(at, plan.count):
+        for axis, (value, count) in enumerate(zip(at, plan.count)):
             inside = jnp.logical_and(value >= 0, value < count)
             present = inside if present is None else jnp.logical_and(present, inside)
-            slot = slot * count + jnp.clip(value, 0, count - 1)
+            if axis < axes:
+                slot = slot * count + jnp.clip(value, 0, count - 1)
         found[code] = (slot, present)
     return found
 
 
-def gather_ring(plan, found, recv, fields, store):
+def gather_ring(plan, found, layers, fields, store):
     for column in range(9):
         for level in range(plan.deep):
             if level == 0:
-                code, block = column * 3, plan.blocks - 1
+                step, block = 0, plan.blocks - 1
             elif level == plan.deep - 1:
-                code, block = column * 3 + 2, 0
+                step, block = 2, 0
             else:
-                code, block = column * 3 + 1, level - 1
-            slot, present = found[code]
-            rows = [recv[slot, field * plan.blocks + block] for field in range(fields)]
+                step, block = 1, level - 1
+            slot, present = found[column * 3 + step]
+            rows = [layers[step][slot, field * plan.blocks + block] for field in range(fields)]
             store(column * plan.deep + level, column, level, rows, present)
 
 
@@ -68,7 +79,7 @@
         for field, row in enumerate(rows):
             ref[at, pl.ds(field, 1), :] = row
 
-    gather_ring(plan, found, recv, fields, store)
+    gather_ring(plan, found, [recv] * 3, fields, store)
 
 
 def lane_ids(sublanes=1):
@@ -106,13 +117,13 @@
     return total
 
 
-def spread(plan, send, rows):
+def spread(send, rows):
     def body(slot, carry):
         for r, row in enumerate(rows):
             send[slot, r] = row
         return carry
 
-    lax.fori_loop(0, plan.devices, body, 0)
+    lax.fori_loop(0, send.shape[0], body, 0, unroll=4)
 
 
 def coarse(value):
@@ -155,26 +166,35 @@
         rows[block] = fold(total)
 
 
-def pack_kernel(plan, counts, offsets, velocity, send):
+def pack_kernel(plan, counts_in, offsets_in, velocity_in, send, counts, offsets, velocity, sems):
+    pairs = [(counts_in, counts), (offsets_in, offsets), (velocity_in, velocity)]
+    copies = [pltpu.make_async_copy(a, b, sems.at[i]) for i, (a, b) in enumerate(pairs)]
+    for copy in copies:
+        copy.start()
+    for copy in copies:
+        copy.wait()
     lane = lane_ids()
     rows = []
     for axis in range(3):
         for block in range(plan.blocks):
-            valid = lane < counts[0, 0, block]
+            valid = lane < counts[0, block]
             row = offsets[axis * plan.blocks + block]
             rows.append(jnp.where(valid, row, FAR) if axis == 0 else row)
     for axis in range(3):
         for block in range(plan.blocks):
-            valid = lane < counts[0, 0, block]
+            valid = lane < counts[0, block]
             row = velocity[axis * plan.blocks + block]
             if axis == 0:
                 row = row + GRAVITY_STEP
             rows.append(jnp.where(valid, row, 0.0))
-    spread(plan, send, rows)
-
-
-def build_kernel(plan, recv, send, tiles, where, right, state, points, flipped, mixed, packed, rows):
-    found = slots(plan)
+    spread(send, rows)
+
+
+def build_kernel(plan, *refs):
+    level, others = refs[0], refs[1:-10]
+    send, tiles, where, right, state, points, flipped, mixed, packed, rows = refs[-10:]
+    layers = [others[0], level, others[-1]]
+    found = slots(plan, 2)
 
     def store(at, column, level, got, present):
         shift = (column // 3 - 1, column % 3 - 1, level - (plan.deep - 1) // 2)
@@ -193,7 +213,7 @@
             right[at, pl.ds(axis, 1), :] = field
             mixed[at, pl.ds(axis, 1), :] = field
 
-    gather_ring(plan, found, recv, 6, store)
+    gather_ring(plan, found, layers, 6, store)
     for at in range(plan.ring):
         first, second, third = split(points[at])
         stacked = jnp.concatenate([first, second, third, first, second, first], axis=0)
@@ -249,7 +269,7 @@
         [dot(start[axis], whole[axis]) for axis in range(3)],
         [dot(whole[axis], whole[axis]) for axis in range(3)],
     ]
-    spread(plan, send, sum(image, []) + [pack(groups)])
+    spread(send, sum(image, []) + [pack(groups)])
 
 
 def second_kernel(plan, recv, tiles, right, state, send, residual, direction, scalars, image, packed, rows):
@@ -283,7 +303,7 @@
         groups[1].append(dot(ahead, whole))
         groups[2].append(dot(left, whole))
         groups[3].append(dot(whole, whole))
-    spread(plan, send, out + [pack(groups)])
+    spread(send, out + [pack(groups)])
 
 
 def third_kernel(
@@ -348,10 +368,10 @@
         [dot(rests[axis], rests[axis]) for axis in range(3)],
         [dot(heads[axis], wholes[axis]) for axis in range(3)],
     ]
-    spread(plan, send, base + sum(each, []) + [pack(groups)])
-
-
-def fourth_kernel(plan, recv, tiles, ends, state, send, star, source, parts, steps, packed, rows):
+    spread(send, base + sum(each, []) + [pack(groups)])
+
+
+def fourth_kernel(plan, recv, tiles, state, send, source, steps, parts, packed, rows):
     found = slots(plan)
     ring_into(plan, found, recv, 4, parts)
     current, curve = totals(recv, 4 * plan.blocks, 2)
@@ -361,13 +381,6 @@
     for at in range(plan.ring):
         gathered = jnp.where(sub < 4, parts[at] * factor, 0.0)
         source[at] = jnp.broadcast_to(-jnp.sum(gathered, axis=0, keepdims=True), (8, LANES))
-    for axis in range(3):
-        alpha = steps[pl.ds(axis, 1), :]
-        for block in range(plan.blocks):
-            star[axis * plan.blocks + block] = (
-                ends[pl.ds(axis * plan.blocks + block, 1), :]
-                + alpha * ends[pl.ds((3 + axis) * plan.blocks + block, 1), :]
-            )
     apply_tiles(plan, tiles, source, packed, rows)
     field, shot, whole = [], [], []
     for block in range(plan.blocks):
@@ -375,7 +388,7 @@
         shot.append(state[pl.ds(block, 1), :] * field[block] - rows[block, pl.ds(0, 1), :])
         whole.append(STIFFNESS * field[block] + shot[block])
     groups = [[dot(field, field)], [dot(field, whole)], [dot(whole, whole)]]
-    spread(plan, send, shot + [pack(groups)])
+    spread(send, shot + [pack(groups)])
 
 
 def fifth_kernel(plan, recv, tiles, source, state, send, ends, image, ahead, steps, packed, rows):
@@ -401,10 +414,10 @@
         wholes.append(STIFFNESS * heads[block] + shot)
         ends[pl.ds(block, 1), :] = alpha * source[own, pl.ds(0, 1), :]
         ends[pl.ds(plan.blocks + block, 1), :] = heads[block]
-    spread(plan, send, [pack([[dot(rests, rests)], [dot(heads, wholes)]])])
-
-
-def last_kernel(plan, recv, ends, pressure, steps):
+    spread(send, [pack([[dot(rests, rests)], [dot(heads, wholes)]])])
+
+
+def last_kernel(plan, recv, speeds, final, ends, star, pressure, steps):
     current, curve = totals(recv, 0, 2)
     steps[...] = current / curve
     alpha = steps[pl.ds(0, 1), :]
@@ -412,20 +425,24 @@
         pressure[block] = (
             ends[pl.ds(block, 1), :] + alpha * ends[pl.ds(plan.blocks + block, 1), :]
         )
-
-
-def call(plan, kernel, operands, outs, scratch=(), smem=0):
-    in_specs = [
-        pl.BlockSpec(memory_space=pltpu.SMEM if i < smem else pltpu.VMEM)
-        for i in range(len(operands))
-    ]
+    for axis in range(3):
+        alpha = final[pl.ds(axis, 1), :]
+        for block in range(plan.blocks):
+            at = axis * plan.blocks + block
+            star[at] = (
+                speeds[pl.ds(at, 1), :] + alpha * speeds[pl.ds(3 * plan.blocks + at, 1), :]
+            )
+
+
+def call(plan, kernel, operands, outs, scratch=(), space=pltpu.VMEM):
     typed = lambda shape: (shape, jnp.float32) if isinstance(shape[0], int) else shape
+    held = lambda item: pltpu.VMEM(*typed(item)) if isinstance(item, tuple) else item
     return pl.pallas_call(
         functools.partial(kernel, plan),
         out_shape=[jax.ShapeDtypeStruct(*typed(shape)) for shape in outs],
-        in_specs=in_specs,
+        in_specs=[pl.BlockSpec(memory_space=space) for _ in operands],
         out_specs=[pl.BlockSpec(memory_space=pltpu.VMEM) for _ in outs],
-        scratch_shapes=[pltpu.VMEM(*typed(shape)) for shape in scratch],
+        scratch_shapes=[held(item) for item in scratch],
         compiler_params=pltpu.CompilerParams(vmem_limit_bytes=24 * 1024 * 1024),
         name=kernel.__name__,
     )(*operands)
@@ -442,11 +459,16 @@
     rows = (blocks, 8, width)
     packed = ((32, plan.ring * width), jnp.bfloat16)
     (send,) = call(
-        plan, pack_kernel, [counts, lined(offsets), lined(velocity)], [slot(6 * blocks)], smem=1
-    )
-    recv = exchange(send)
+        plan, pack_kernel, [counts.reshape(1, blocks), lined(offsets), lined(velocity)],
+        [(plan.count[0] * plan.count[1], 6 * blocks, 1, width)],
+        [
+            pltpu.SMEM((1, blocks), jnp.int32), (3 * blocks, 1, width), (3 * blocks, 1, width),
+            pltpu.SemaphoreType.DMA((3,)),
+        ],
+        pltpu.HBM,
+    )
     send, tiles, where, right, state = call(
-        plan, build_kernel, [recv],
+        plan, build_kernel, exchange_layers(plan, send),
         [
             slot(3 * blocks + 1), ((9 * blocks, 6 * width, width), jnp.bfloat16),
             ring, ring, (4 * blocks, width),
@@ -460,16 +482,16 @@
         [ring, packed, rows],
     )
     recv = exchange(send)
-    send, ends = call(
+    send, speeds = call(
         plan, third_kernel, [recv, tiles, where, right, residual, direction, state, scalars],
         [slot(4 * blocks + 1), (6 * blocks, width)],
         [ring, rows, ring, tile, packed, rows],
     )
     recv = exchange(send)
-    send, star, source = call(
-        plan, fourth_kernel, [recv, tiles, ends, state],
-        [slot(blocks + 1), (3 * blocks, 1, width), ring],
-        [ring, tile, packed, rows],
+    send, source, final = call(
+        plan, fourth_kernel, [recv, tiles, state],
+        [slot(blocks + 1), ring, tile],
+        [ring, packed, rows],
     )
     recv = exchange(send)
     send, ends = call(
@@ -478,7 +500,10 @@
         [ring, ring, tile, packed, rows],
     )
     recv = exchange(send)
-    (pressure,) = call(plan, last_kernel, [recv, ends], [(blocks, 1, width)], [tile])
+    star, pressure = call(
+        plan, last_kernel, [recv, speeds, final, ends],
+        [(3 * blocks, 1, width), (blocks, 1, width)], [tile],
+    )
     star = star.reshape(3, 1, blocks, 1, width).transpose(0, 1, 3, 2, 4)
     pressure = pressure.reshape(1, blocks, 1, width).transpose(0, 2, 1, 3)
     return star, pressure

time: 83.2 us -> 80.7 us (0.970)
  blocking collectives: 69.6 us -> 66.9 us
  waiting for transfers between devices: 0 us -> 1.37 us
  Pallas kernels: 10.6 us -> 9.4 us
    all_to_all x6 -> x5, blocking collectives: 69.6 us -> 50.7 us  [exchange(): return lax.all_to_all(send, AXES, 0, 0, tiled=True)]
    all_to_all x0 -> x1, blocking collectives: none -> 16.2 us  [exchange_layers(): level = lax.all_to_all(send, AXES[:2], 0, 0, tiled=True)]
    ppermute x0 -> x1, waiting for transfers between devices: none -> 1.37 us  [exchange_layers(): return [level, lax.ppermute(level, AXES[2], [(0, 1), (1, 0)])]]
    pallas_call x7, Pallas kernels: 10.6 us -> 9.4 us  [call(): pl.pallas_call(functools.partial(kernel, plan), out_shape=[jax.ShapeDtype...]
  transfers between devices with their start and end apart: 0 -> 1, of which waited for: 0 -> 1; matrix products, arithmetic and copies ran while one was open for 0% -> 0% of each run, Pallas kernels for 0% -> 0%
where the time goes in v3:
time: 80.7 us; the launch traced here: 80.4 us
  blocking collectives  66.9 us (83%)
  Pallas kernels  9.4 us (12%)
  local copies, waits for them, and re-layouts  2.02 us (3%)
  waiting for transfers between devices  1.37 us (2%)
    all_to_all x5, blocking collectives, exchange(): return lax.all_to_all(send, AXES, 0, 0, tiled=True)  50.7 us
    all_to_all x1, blocking collectives, exchange_layers(): level = lax.all_to_all(send, AXES[:2], 0, 0, tiled=True)  16.2 us
    pallas_call x7, Pallas kernels, call(): pl.pallas_call(functools.partial(kernel, plan), out_shape=[jax.ShapeDtype...  9.4 us
    unnamed x6, local copies, waits for them, and re-layouts  2.02 us
  transfers between devices with their start and end apart: 1, of which 1 were waited for; matrix products, arithmetic and copies ran while one was open for 0% of the time, Pallas kernels for 0%

profile of v3, /device:TPU:0, one launch (start us, length us, event | category | flops | bytes accessed | tf_op | source)
XLA Modules:
  0.0 80.4 jit_solution(8203097648240646972)
XLA Ops:
  0.6 0.0 copy-start
  0.6 0.7 copy-done
  1.3 0.0 copy-start.1
  1.3 0.7 copy-done.1
  2.0 0.0 copy-start.2
  2.0 0.7 copy-done.2
  2.7 0.7 pack_kernel.1
  3.3 16.2 %all_to_all.30.refs_0_ = f32[16,18,1,128]{3,2,1,0:T(1,128)S(1)} all-to-all(f32[16,18,1,128]{3,2,1,0:T(1,128)S(1)} %pack_kernel.1), channel_id=1, replica_groups=mesh['gx'=4,'gy'=4,'gz'=2] {'gx','gy'}, dimensions={0} | all-to-all | bytes 294912 | tf_op jit(solution)/shard_map/all_to_all | solution.py:23
  19.6 0.0 collective-permute-start
  19.6 1.4 %collective-permute-done.refs_1_ = f32[16,18,1,128]{3,2,1,0:T(1,128)S(1)} collective-permute-done((f32[16,18,1,128]{3,2,1,0:T(1,128)S(1)}, f32[16,18,1,128]{3,2,1,0:T(1,128)S(1)}, u32[]{:S(2)}, u32[]{:S(2)}) %collective-permute-start) | collective-permute-done | bytes 147488 | tf_op jit(solution)/shard_map/ppermute | solution.py:26
  20.9 3.1 %build_kernel.1 = (f32[32,10,1,128]{3,2,1,0:T(1,128)S(1)}, bf16[27,768,128]{2,1,0:T(8,128)(2,1)S(1)}, f32[45,8,128]{2,1,0:T(8,128)S(1)}, f32[45,8,128]{2,1,0:T(8,128)S(1)}, f32[12,128]{1,0:T(8,128)S(1)}) custom-call(f32[16,18,1,128]{3,2,1,0:T(1,128)S(1)} %all_to_all.30.refs_0_, f32[16,18,1,128]{3,2,1,0:T(1,128)S(1)} %collective-permute-done.refs_1_), custom_call_target="tpu_custom_call" | custom-call | tf_op jit(solution)/shard_map/build_kernel/pallas_call | solution.py:440
  24.0 10.2 %all_to_all.31.recv = f32[32,10,1,128]{3,2,1,0:T(1,128)S(1)} all-to-all(f32[32,10,1,128]{3,2,1,0:T(1,128)S(1)} %get-tuple-element.20), channel_id=1, replica_groups=mesh['gx'=4,'gy'=4,'gz'=2] {'gx','gy','gz'}, dimensions={0} | all-to-all | bytes 327680 | tf_op jit(solution)/shard_map/all_to_all | solution.py:19
  34.2 1.3 %second_kernel.1 = (f32[32,10,1,128]{3,2,1,0:T(1,128)S(1)}, f32[45,8,128]{2,1,0:T(8,128)S(1)}, f32[45,8,128]{2,1,0:T(8,128)S(1)}, f32[4,8,128]{2,1,0:T(8,128)S(1)}) custom-call(f32[32,10,1,128]{3,2,1,0:T(1,128)S(1)} %all_to_all.31.recv, bf16[27,768,128]{2,1,0:T(8,128)(2,1)S(1)} %get-tuple-element.21.tiles, f32[45,8,128]{2,1,0:T(8,128)S(1)} %get-tuple-element.22.right, ...), custom_call_target="tpu_custom_call" | custom-call | tf_op jit(solution)/shard_map/second_kernel/pallas_call | solution.py:440
  35.5 10.5 %all_to_all.32.recv = f32[32,10,1,128]{3,2,1,0:T(1,128)S(1)} all-to-all(f32[32,10,1,128]{3,2,1,0:T(1,128)S(1)} %get-tuple-element.24), channel_id=1, replica_groups=mesh['gx'=4,'gy'=4,'gz'=2] {'gx','gy','gz'}, dimensions={0} | all-to-all | bytes 327680 | tf_op jit(solution)/shard_map/all_to_all | solution.py:19
  46.0 1.3 %third_kernel.1 = (f32[32,13,1,128]{3,2,1,0:T(1,128)S(1)}, f32[18,128]{1,0:T(8,128)S(1)}) custom-call(f32[32,10,1,128]{3,2,1,0:T(1,128)S(1)} %all_to_all.32.recv, bf16[27,768,128]{2,1,0:T(8,128)(2,1)S(1)} %get-tuple-element.21.tiles, f32[45,8,128]{2,1,0:T(8,128)S(1)} %get-tuple-element.25.where, f32[45,8,128]{2,1,0:T(8,128)S(1)} %get-tuple-element.22.right, ...), custom_call_target="tpu_custom_call" | custom-call | tf_op jit(solution)/shard_map/third_kernel/pallas_call | solution.py:440
  47.3 11.1 %all_to_all.33.recv = f32[32,13,1,128]{3,2,1,0:T(1,128)S(1)} all-to-all(f32[32,13,1,128]{3,2,1,0:T(1,128)S(1)} %get-tuple-element.29), channel_id=1, replica_groups=mesh['gx'=4,'gy'=4,'gz'=2] {'gx','gy','gz'}, dimensions={0} | all-to-all | bytes 425984 | tf_op jit(solution)/shard_map/all_to_all | solution.py:19
  58.4 1.2 %fourth_kernel.1 = (f32[32,4,1,128]{3,2,1,0:T(1,128)S(1)}, f32[45,8,128]{2,1,0:T(8,128)S(1)}, f32[8,128]{1,0:T(8,128)S(1)}) custom-call(f32[32,13,1,128]{3,2,1,0:T(1,128)S(1)} %all_to_all.33.recv, bf16[27,768,128]{2,1,0:T(8,128)(2,1)S(1)} %get-tuple-element.21.tiles, f32[12,128]{1,0:T(8,128)S(1)} %get-tuple-element.23.state), custom_call_target="tpu_custom_call" | custom-call | tf_op jit(solution)/shard_map/fourth_kernel/pallas_call | solution.py:440
  59.6 10.1 %all_to_all.34.recv = f32[32,4,1,128]{3,2,1,0:T(1,128)S(1)} all-to-all(f32[32,4,1,128]{3,2,1,0:T(1,128)S(1)} %get-tuple-element.30), channel_id=1, replica_groups=mesh['gx'=4,'gy'=4,'gz'=2] {'gx','gy','gz'}, dimensions={0} | all-to-all | bytes 131072 | tf_op jit(solution)/shard_map/all_to_all | solution.py:19
  69.7 1.1 %fifth_kernel.1 = (f32[32,1,1,128]{3,2,1,0:T(1,128)S(1)}, f32[6,128]{1,0:T(8,128)S(1)}) custom-call(f32[32,4,1,128]{3,2,1,0:T(1,128)S(1)} %all_to_all.34.recv, bf16[27,768,128]{2,1,0:T(8,128)(2,1)S(1)} %get-tuple-element.21.tiles, f32[45,8,128]{2,1,0:T(8,128)S(1)} %get-tuple-element.31.source, f32[12,128]{1,0:T(8,128)S(1)} %get-tuple-element.23.state), custom_call_target="tpu_custom_call" | custom-call | tf_op jit(solution)/shard_map/fifth_kernel/pallas_call | solution.py:440
  70.9 8.8 %all_to_all.35.recv = f32[32,1,1,128]{3,2,1,0:T(1,128)S(1)} all-to-all(f32[32,1,1,128]{3,2,1,0:T(1,128)S(1)} %get-tuple-element.32), channel_id=1, replica_groups=mesh['gx'=4,'gy'=4,'gz'=2] {'gx','gy','gz'}, dimensions={0} | all-to-all | bytes 32768 | tf_op jit(solution)/shard_map/all_to_all | solution.py:19
  79.7 0.7 last_kernel.1
Async XLA Ops:
  0.6 0.7 copy-start
  1.3 0.7 copy-start.1
  2.0 0.7 copy-start.2
  19.6 1.4 %collective-permute-start = (f32[16,18,1,128]{3,2,1,0:T(1,128)S(1)}, f32[16,18,1,128]{3,2,1,0:T(1,128)S(1)}, u32[]{:S(2)}, u32[]{:S(2)}) collective-permute-start(f32[16,18,1,128]{3,2,1,0:T(1,128)S(1)} %all_to_all.30.refs_0_), channel_id=1, source_target_pairs={{0,1},{1,0},{2,3},{3,2},{4,5},{5,4},{6,7},{7,6},{8,9},{9,8},{10,11... | collective-permute-start | bytes 442376 | tf_op jit(solution)/shard_map/ppermute | solution.py:26

commit v4 on v3

--- a/solution.py
+++ b/solution.py
@@ -144,25 +144,28 @@
         packed[:, pl.ds(at * LANES, LANES)] = stacked.astype(jnp.bfloat16)
 
 
-def tile_sum(plan, tiles, packed, block, column):
-    ahead = packed[:, pl.ds((column * plan.deep + block) * LANES, 3 * LANES)]
+def tile_sum(plan, tiles, packed, block, group):
+    span = 3 * plan.width
+    columns = range(2 * group, min(2 * group + 2, 9))
+    ahead = [packed[:, pl.ds((c * plan.deep + block) * LANES, span)] for c in columns]
     return jnp.dot(
-        jnp.concatenate([ahead, ahead], axis=1),
-        tiles[block * 9 + column],
+        jnp.concatenate(ahead, axis=1),
+        tiles[block, pl.ds(2 * group * span, len(ahead) * span), :],
         preferred_element_type=jnp.float32,
     )
 
 
 def fold(total):
-    return total[0:8] + total[8:16] + total[16:24]
+    both = total[:, :LANES] + total[:, LANES:]
+    return both[0:8] + both[8:16] + both[16:24]
 
 
 def apply_tiles(plan, tiles, ring, packed, rows):
     split_ring(plan, ring, packed)
     for block in range(plan.blocks):
         total = tile_sum(plan, tiles, packed, block, 0)
-        for column in range(1, 9):
-            total = total + tile_sum(plan, tiles, packed, block, column)
+        for group in range(1, 5):
+            total = total + tile_sum(plan, tiles, packed, block, group)
         rows[block] = fold(total)
 
 
@@ -241,12 +244,14 @@
             bump = jnp.maximum(rest, 0.0)
             weight = bump * bump * bump
             high = weight.astype(jnp.bfloat16)
-            tiles[block * 9 + column, pl.ds(0, 3 * plan.width), :] = high
-            tiles[block * 9 + column, pl.ds(3 * plan.width, 3 * plan.width), :] = (
+            span = pl.ds(3 * column * plan.width, 3 * plan.width)
+            tiles[block, span, pl.ds(0, LANES)] = high
+            tiles[block, span, pl.ds(LANES, LANES)] = (
                 weight - high.astype(jnp.float32)
             ).astype(jnp.bfloat16)
-            part = tile_sum(plan, tiles, packed, block, column)
-            total = part if total is None else total + part
+            if column % 2 == 1 or column == 8:
+                part = tile_sum(plan, tiles, packed, block, column // 2)
+                total = part if total is None else total + part
         rows[block] = fold(total)
     image = [[None] * plan.blocks for _ in range(3)]
     whole = [[None] * plan.blocks for _ in range(3)]
@@ -459,7 +464,11 @@
     rows = (blocks, 8, width)
     packed = ((32, plan.ring * width), jnp.bfloat16)
     (send,) = call(
-        plan, pack_kernel, [counts.reshape(1, blocks), lined(offsets), lined(velocity)],
+        plan, pack_kernel,
+        [
+            pltpu.with_memory_space_constraint(field, pltpu.HBM)
+            for field in (counts.reshape(1, blocks), lined(offsets), lined(velocity))
+        ],
         [(plan.count[0] * plan.count[1], 6 * blocks, 1, width)],
         [
             pltpu.SMEM((1, blocks), jnp.int32), (3 * blocks, 1, width), (3 * blocks, 1, width),
@@ -470,7 +479,7 @@
     send, tiles, where, right, state = call(
         plan, build_kernel, exchange_layers(plan, send),
         [
-            slot(3 * blocks + 1), ((9 * blocks, 6 * width, width), jnp.bfloat16),
+            slot(3 * blocks + 1), ((blocks, 27 * width, 2 * width), jnp.bfloat16),
             ring, ring, (4 * blocks, width),
         ],
         [ring, ((plan.ring * width, LANES), jnp.bfloat16), ring, packed, rows],

time: 80.7 us -> 78.1 us (0.968)
  local copies, waits for them, and re-layouts: 2.02 us -> 0 us
    unnamed x6 -> x0, local copies, waits for them, and re-layouts: 2.02 us -> none
where the time goes in v4:
time: 78.1 us; the launch traced here: 77.8 us
  blocking collectives  66.9 us (86%)
  Pallas kernels  8.87 us (11%)
  waiting for transfers between devices  1.37 us (2%)
    all_to_all x5, blocking collectives, exchange(): return lax.all_to_all(send, AXES, 0, 0, tiled=True)  50.7 us
    all_to_all x1, blocking collectives, exchange_layers(): level = lax.all_to_all(send, AXES[:2], 0, 0, tiled=True)  16.2 us
    pallas_call x7, Pallas kernels, call(): pl.pallas_call(functools.partial(kernel, plan), out_shape=[jax.ShapeDtype...  8.87 us
  transfers between devices with their start and end apart: 1, of which 1 were waited for; matrix products, arithmetic and copies ran while one was open for 0% of the time, Pallas kernels for 0%

profile of v4, /device:TPU:0, one launch (start us, length us, event | category | flops | bytes accessed | tf_op | source)
XLA Modules:
  0.0 77.8 jit_solution(10525778711416217864)
XLA Ops:
  0.6 0.8 %pack_kernel.1 = f32[16,18,1,128]{3,2,1,0:T(1,128)S(1)} custom-call(s32[1,3]{1,0:T(1,128)} %bitcast.11, f32[9,1,128]{2,1,0:T(1,128)} %bitcast.9, f32[9,1,128]{2,1,0:T(1,128)} %bitcast.10), custom_call_target="tpu_custom_call" | custom-call | tf_op jit(solution)/shard_map/pack_kernel/pallas_call | solution.py:445
  1.5 16.2 %all_to_all.30.refs_0_ = f32[16,18,1,128]{3,2,1,0:T(1,128)S(1)} all-to-all(f32[16,18,1,128]{3,2,1,0:T(1,128)S(1)} %pack_kernel.1), channel_id=1, replica_groups=mesh['gx'=4,'gy'=4,'gz'=2] {'gx','gy'}, dimensions={0} | all-to-all | bytes 294912 | tf_op jit(solution)/shard_map/all_to_all | solution.py:23
  17.7 0.0 collective-permute-start
  17.7 1.4 %collective-permute-done.refs_1_ = f32[16,18,1,128]{3,2,1,0:T(1,128)S(1)} collective-permute-done((f32[16,18,1,128]{3,2,1,0:T(1,128)S(1)}, f32[16,18,1,128]{3,2,1,0:T(1,128)S(1)}, u32[]{:S(2)}, u32[]{:S(2)}) %collective-permute-start) | collective-permute-done | bytes 147488 | tf_op jit(solution)/shard_map/ppermute | solution.py:26
  19.1 2.6 %build_kernel.1 = (f32[32,10,1,128]{3,2,1,0:T(1,128)S(1)}, bf16[3,3456,256]{2,1,0:T(8,128)(2,1)S(1)}, f32[45,8,128]{2,1,0:T(8,128)S(1)}, f32[45,8,128]{2,1,0:T(8,128)S(1)}, f32[12,128]{1,0:T(8,128)S(1)}) custom-call(f32[16,18,1,128]{3,2,1,0:T(1,128)S(1)} %all_to_all.30.refs_0_, f32[16,18,1,128]{3,2,1,0:T(1,128)S(1)} %collective-permute-done.refs_1_), custom_call_target="tpu_custom_call" | custom-call | tf_op jit(solution)/shard_map/build_kernel/pallas_call | solution.py:445
  21.7 10.2 %all_to_all.31.recv = f32[32,10,1,128]{3,2,1,0:T(1,128)S(1)} all-to-all(f32[32,10,1,128]{3,2,1,0:T(1,128)S(1)} %get-tuple-element.20), channel_id=1, replica_groups=mesh['gx'=4,'gy'=4,'gz'=2] {'gx','gy','gz'}, dimensions={0} | all-to-all | bytes 327680 | tf_op jit(solution)/shard_map/all_to_all | solution.py:19
  31.9 1.2 %second_kernel.1 = (f32[32,10,1,128]{3,2,1,0:T(1,128)S(1)}, f32[45,8,128]{2,1,0:T(8,128)S(1)}, f32[45,8,128]{2,1,0:T(8,128)S(1)}, f32[4,8,128]{2,1,0:T(8,128)S(1)}) custom-call(f32[32,10,1,128]{3,2,1,0:T(1,128)S(1)} %all_to_all.31.recv, bf16[3,3456,256]{2,1,0:T(8,128)(2,1)S(1)} %get-tuple-element.21.tiles, f32[45,8,128]{2,1,0:T(8,128)S(1)} %get-tuple-element.22.right, ...), custom_call_target="tpu_custom_call" | custom-call | tf_op jit(solution)/shard_map/second_kernel/pallas_call | solution.py:445
  33.1 10.5 %all_to_all.32.recv = f32[32,10,1,128]{3,2,1,0:T(1,128)S(1)} all-to-all(f32[32,10,1,128]{3,2,1,0:T(1,128)S(1)} %get-tuple-element.24), channel_id=1, replica_groups=mesh['gx'=4,'gy'=4,'gz'=2] {'gx','gy','gz'}, dimensions={0} | all-to-all | bytes 327680 | tf_op jit(solution)/shard_map/all_to_all | solution.py:19
  43.6 1.2 %third_kernel.1 = (f32[32,13,1,128]{3,2,1,0:T(1,128)S(1)}, f32[18,128]{1,0:T(8,128)S(1)}) custom-call(f32[32,10,1,128]{3,2,1,0:T(1,128)S(1)} %all_to_all.32.recv, bf16[3,3456,256]{2,1,0:T(8,128)(2,1)S(1)} %get-tuple-element.21.tiles, f32[45,8,128]{2,1,0:T(8,128)S(1)} %get-tuple-element.25.where, f32[45,8,128]{2,1,0:T(8,128)S(1)} %get-tuple-element.22.right, ...), custom_call_target="tpu_custom_call" | custom-call | tf_op jit(solution)/shard_map/third_kernel/pallas_call | solution.py:445
  44.9 11.1 %all_to_all.33.recv = f32[32,13,1,128]{3,2,1,0:T(1,128)S(1)} all-to-all(f32[32,13,1,128]{3,2,1,0:T(1,128)S(1)} %get-tuple-element.29), channel_id=1, replica_groups=mesh['gx'=4,'gy'=4,'gz'=2] {'gx','gy','gz'}, dimensions={0} | all-to-all | bytes 425984 | tf_op jit(solution)/shard_map/all_to_all | solution.py:19
  56.0 1.2 %fourth_kernel.1 = (f32[32,4,1,128]{3,2,1,0:T(1,128)S(1)}, f32[45,8,128]{2,1,0:T(8,128)S(1)}, f32[8,128]{1,0:T(8,128)S(1)}) custom-call(f32[32,13,1,128]{3,2,1,0:T(1,128)S(1)} %all_to_all.33.recv, bf16[3,3456,256]{2,1,0:T(8,128)(2,1)S(1)} %get-tuple-element.21.tiles, f32[12,128]{1,0:T(8,128)S(1)} %get-tuple-element.23.state), custom_call_target="tpu_custom_call" | custom-call | tf_op jit(solution)/shard_map/fourth_kernel/pallas_call | solution.py:445
  57.1 10.1 %all_to_all.34.recv = f32[32,4,1,128]{3,2,1,0:T(1,128)S(1)} all-to-all(f32[32,4,1,128]{3,2,1,0:T(1,128)S(1)} %get-tuple-element.30), channel_id=1, replica_groups=mesh['gx'=4,'gy'=4,'gz'=2] {'gx','gy','gz'}, dimensions={0} | all-to-all | bytes 131072 | tf_op jit(solution)/shard_map/all_to_all | solution.py:19
  67.2 1.1 %fifth_kernel.1 = (f32[32,1,1,128]{3,2,1,0:T(1,128)S(1)}, f32[6,128]{1,0:T(8,128)S(1)}) custom-call(f32[32,4,1,128]{3,2,1,0:T(1,128)S(1)} %all_to_all.34.recv, bf16[3,3456,256]{2,1,0:T(8,128)(2,1)S(1)} %get-tuple-element.21.tiles, f32[45,8,128]{2,1,0:T(8,128)S(1)} %get-tuple-element.31.source, f32[12,128]{1,0:T(8,128)S(1)} %get-tuple-element.23.state), custom_call_target="tpu_custom_call" | custom-call | tf_op jit(solution)/shard_map/fifth_kernel/pallas_call | solution.py:445
  68.3 8.8 %all_to_all.35.recv = f32[32,1,1,128]{3,2,1,0:T(1,128)S(1)} all-to-all(f32[32,1,1,128]{3,2,1,0:T(1,128)S(1)} %get-tuple-element.32), channel_id=1, replica_groups=mesh['gx'=4,'gy'=4,'gz'=2] {'gx','gy','gz'}, dimensions={0} | all-to-all | bytes 32768 | tf_op jit(solution)/shard_map/all_to_all | solution.py:19
  77.1 0.7 last_kernel.1
Async XLA Ops:
  17.7 1.4 %collective-permute-start = (f32[16,18,1,128]{3,2,1,0:T(1,128)S(1)}, f32[16,18,1,128]{3,2,1,0:T(1,128)S(1)}, u32[]{:S(2)}, u32[]{:S(2)}) collective-permute-start(f32[16,18,1,128]{3,2,1,0:T(1,128)S(1)} %all_to_all.30.refs_0_), channel_id=1, source_target_pairs={{0,1},{1,0},{2,3},{3,2},{4,5},{5,4},{6,7},{7,6},{8,9},{9,8},{10,11... | collective-permute-start | bytes 442376 | tf_op jit(solution)/shard_map/ppermute | solution.py:26

commit v5 on v4

--- a/solution.py
+++ b/solution.py
@@ -60,9 +60,9 @@
     return found
 
 
-def gather_ring(plan, found, layers, fields, store):
+def gather_ring(plan, found, layers, fields, store, levels=None):
     for column in range(9):
-        for level in range(plan.deep):
+        for level in levels or range(plan.deep):
             if level == 0:
                 step, block = 0, plan.blocks - 1
             elif level == plan.deep - 1:
@@ -137,20 +137,39 @@
     return first, second, rest - second
 
 
-def split_ring(plan, ref, packed):
-    for at in range(plan.ring):
-        first, second, third = split(ref[at])
-        stacked = jnp.concatenate([first, second, third, jnp.zeros_like(third)], axis=0)
-        packed[:, pl.ds(at * LANES, LANES)] = stacked.astype(jnp.bfloat16)
-
-
-def tile_sum(plan, tiles, packed, block, group):
-    span = 3 * plan.width
-    columns = range(2 * group, min(2 * group + 2, 9))
-    ahead = [packed[:, pl.ds((c * plan.deep + block) * LANES, span)] for c in columns]
+def split_ring(plan, ring, packed, levels=None):
+    for column in range(9):
+        for level in levels or range(plan.deep):
+            at = column * plan.deep + level
+            first, second, third = split(ring[at])
+            stacked = jnp.concatenate([first, second, third, jnp.zeros_like(third)], axis=0)
+            packed[:, pl.ds(at * LANES, LANES)] = stacked.astype(jnp.bfloat16)
+
+
+def inner_span(plan, block):
+    low = max(block, 1)
+    return low, min(block + 2, plan.blocks) + 1 - low
+
+
+def inner_base(plan, block):
+    return 9 * sum(inner_span(plan, before)[1] for before in range(block)) * plan.width
+
+
+def edges(plan):
+    return [(0, 0), (plan.blocks - 1, plan.blocks + 1)]
+
+
+def groups_of(number):
+    size = 3 if number % 2 == 0 else 4 if number == 1 else 2
+    return [range(c, min(c + size, 9)) for c in range(0, 9, size)]
+
+
+def tile_sum(plan, tiles, base, packed, level, number, columns):
+    span = number * plan.width
+    ahead = [packed[:, pl.ds((c * plan.deep + level) * LANES, span)] for c in columns]
     return jnp.dot(
-        jnp.concatenate(ahead, axis=1),
-        tiles[block, pl.ds(2 * group * span, len(ahead) * span), :],
+        jnp.concatenate(ahead, axis=1) if len(ahead) > 1 else ahead[0],
+        tiles[pl.ds(base + columns[0] * span, len(ahead) * span), :],
         preferred_element_type=jnp.float32,
     )
 
@@ -160,12 +179,25 @@
     return both[0:8] + both[8:16] + both[16:24]
 
 
-def apply_tiles(plan, tiles, ring, packed, rows):
+def apply_tiles(plan, tiles, rims, ring, packed, rows):
     split_ring(plan, ring, packed)
     for block in range(plan.blocks):
-        total = tile_sum(plan, tiles, packed, block, 0)
-        for group in range(1, 5):
-            total = total + tile_sum(plan, tiles, packed, block, group)
+        low, number = inner_span(plan, block)
+        base = inner_base(plan, block)
+        parts = [
+            tile_sum(plan, tiles, base, packed, low, number, columns)
+            for columns in groups_of(number)
+        ]
+        for edge, (at, level) in enumerate(edges(plan)):
+            if at == block:
+                base = edge * 9 * plan.width
+                parts += [
+                    tile_sum(plan, rims, base, packed, level, 1, columns)
+                    for columns in groups_of(1)
+                ]
+        total = parts[0]
+        for part in parts[1:]:
+            total = total + part
         rows[block] = fold(total)
 
 
@@ -193,12 +225,7 @@
     spread(send, rows)
 
 
-def build_kernel(plan, *refs):
-    level, others = refs[0], refs[1:-10]
-    send, tiles, where, right, state, points, flipped, mixed, packed, rows = refs[-10:]
-    layers = [others[0], level, others[-1]]
-    found = slots(plan, 2)
-
+def place_ring(plan, found, layers, levels, points, mixed, where, right):
     def store(at, column, level, got, present):
         shift = (column // 3 - 1, column % 3 - 1, level - (plan.deep - 1) // 2)
         spots = [plan.unit * (got[axis] + shift[axis]) for axis in range(3)]
@@ -216,13 +243,39 @@
             right[at, pl.ds(axis, 1), :] = field
             mixed[at, pl.ds(axis, 1), :] = field
 
-    gather_ring(plan, found, layers, 6, store)
-    for at in range(plan.ring):
-        first, second, third = split(points[at])
-        stacked = jnp.concatenate([first, second, third, first, second, first], axis=0)
-        padded = jnp.concatenate([stacked, jnp.zeros((LANES - 48, LANES), jnp.float32)], axis=0)
-        flipped[pl.ds(at * plan.width, plan.width), :] = jnp.transpose(padded).astype(jnp.bfloat16)
-    split_ring(plan, mixed, packed)
+    gather_ring(plan, found, layers, 6, store, levels)
+
+
+def flip_points(plan, levels, points, flipped):
+    for column in range(9):
+        for level in levels:
+            at = column * plan.deep + level
+            first, second, third = split(points[at])
+            stacked = jnp.concatenate([first, second, third, first, second, first], axis=0)
+            padded = jnp.concatenate([stacked, jnp.zeros((LANES - 48, LANES), jnp.float32)], axis=0)
+            flipped[pl.ds(at * plan.width, plan.width), :] = jnp.transpose(padded).astype(jnp.bfloat16)
+
+
+def weigh(plan, flipped, centre, level, number, columns, tiles, base):
+    for column in columns:
+        span = number * plan.width
+        rest = jnp.dot(
+            flipped[pl.ds((column * plan.deep + level) * plan.width, span), :],
+            centre, preferred_element_type=jnp.float32,
+        )
+        bump = jnp.maximum(rest, 0.0)
+        weight = bump * bump * bump
+        high = weight.astype(jnp.bfloat16)
+        spot = pl.ds(base + column * span, span)
+        tiles[spot, pl.ds(0, LANES)] = high
+        tiles[spot, pl.ds(LANES, LANES)] = (weight - high.astype(jnp.float32)).astype(jnp.bfloat16)
+
+
+def inner_kernel(plan, recv, tiles, where, right, centres, partial, points, flipped, mixed, packed):
+    levels = range(1, plan.blocks + 1)
+    place_ring(plan, slots(plan, 2), [None, recv, None], levels, points, mixed, where, right)
+    flip_points(plan, levels, points, flipped)
+    split_ring(plan, mixed, packed, levels)
     sub = sublane_ids()
     for block in range(plan.blocks):
         own = points[plan.own(block)]
@@ -235,24 +288,44 @@
         stacked = jnp.concatenate([first, first, first, second, second, third], axis=0)
         padded = jnp.concatenate([stacked, jnp.zeros((LANES - 48, LANES), jnp.float32)], axis=0)
         centre = padded.astype(jnp.bfloat16)
+        centres[block] = centre
+        low, number = inner_span(plan, block)
+        base = inner_base(plan, block)
         total = None
-        for column in range(9):
-            at = (column * plan.deep + block) * plan.width
-            rest = jnp.dot(
-                flipped[pl.ds(at, 3 * plan.width), :], centre, preferred_element_type=jnp.float32
-            )
-            bump = jnp.maximum(rest, 0.0)
-            weight = bump * bump * bump
-            high = weight.astype(jnp.bfloat16)
-            span = pl.ds(3 * column * plan.width, 3 * plan.width)
-            tiles[block, span, pl.ds(0, LANES)] = high
-            tiles[block, span, pl.ds(LANES, LANES)] = (
-                weight - high.astype(jnp.float32)
-            ).astype(jnp.bfloat16)
-            if column % 2 == 1 or column == 8:
-                part = tile_sum(plan, tiles, packed, block, column // 2)
-                total = part if total is None else total + part
-        rows[block] = fold(total)
+        for columns in groups_of(number):
+            weigh(plan, flipped, centre, low, number, columns, tiles, base)
+            part = tile_sum(plan, tiles, base, packed, low, number, columns)
+            total = part if total is None else total + part
+        partial[block] = fold(total)
+
+
+def edge_kernel(plan, *refs):
+    others = refs[:-14]
+    (
+        near_where, near_right, centres, partial,
+        send, rims, where, right, state, points, flipped, mixed, packed, rows,
+    ) = refs[-14:]
+    levels = [0, plan.deep - 1]
+    place_ring(
+        plan, slots(plan, 2), [others[0], None, others[-1]], levels, points, mixed, where, right
+    )
+    for column in range(9):
+        for level in range(1, plan.blocks + 1):
+            at = column * plan.deep + level
+            where[at] = near_where[at]
+            right[at] = near_right[at]
+    flip_points(plan, levels, points, flipped)
+    split_ring(plan, mixed, packed, levels)
+    for block in range(plan.blocks):
+        rows[block] = partial[block]
+    for edge, (block, level) in enumerate(edges(plan)):
+        base = edge * 9 * plan.width
+        total = None
+        for columns in groups_of(1):
+            weigh(plan, flipped, centres[block], level, 1, columns, rims, base)
+            part = tile_sum(plan, rims, base, packed, level, 1, columns)
+            total = part if total is None else total + part
+        rows[block] = rows[block] + fold(total)
     image = [[None] * plan.blocks for _ in range(3)]
     whole = [[None] * plan.blocks for _ in range(3)]
     start = [[None] * plan.blocks for _ in range(3)]
@@ -277,7 +350,7 @@
     spread(send, sum(image, []) + [pack(groups)])
 
 
-def second_kernel(plan, recv, tiles, right, state, send, residual, direction, scalars, image, packed, rows):
+def second_kernel(plan, recv, tiles, rims, right, state, send, residual, direction, scalars, image, packed, rows):
     found = slots(plan)
     ring_into(plan, found, recv, 3, image)
     current, curve, square = totals(recv, 3 * plan.blocks, 3)
@@ -292,7 +365,7 @@
     scalars[plan.blocks] = alpha
     for block in range(plan.blocks):
         scalars[block] = image[plan.own(block)]
-    apply_tiles(plan, tiles, direction, packed, rows)
+    apply_tiles(plan, tiles, rims, direction, packed, rows)
     out = []
     groups = [[], [], [], []]
     for axis in range(3):
@@ -312,7 +385,7 @@
 
 
 def third_kernel(
-    plan, recv, tiles, where, right, residual, direction, state, scalars,
+    plan, recv, tiles, rims, where, right, residual, direction, state, scalars,
     send, ends, image, sofar, ahead, steps, packed, rows,
 ):
     found = slots(plan)
@@ -343,7 +416,7 @@
         if at - plan.own(0) in range(plan.blocks):
             image[at] = rest
             sofar[at - plan.own(0)] = made
-    apply_tiles(plan, tiles, ahead, packed, rows)
+    apply_tiles(plan, tiles, rims, ahead, packed, rows)
     scale = 1.0 / plan.unit
     base = []
     each = [[None] * plan.blocks for _ in range(3)]
@@ -376,7 +449,7 @@
     spread(send, base + sum(each, []) + [pack(groups)])
 
 
-def fourth_kernel(plan, recv, tiles, state, send, source, steps, parts, packed, rows):
+def fourth_kernel(plan, recv, tiles, rims, state, send, source, steps, parts, packed, rows):
     found = slots(plan)
     ring_into(plan, found, recv, 4, parts)
     current, curve = totals(recv, 4 * plan.blocks, 2)
@@ -386,7 +459,7 @@
     for at in range(plan.ring):
         gathered = jnp.where(sub < 4, parts[at] * factor, 0.0)
         source[at] = jnp.broadcast_to(-jnp.sum(gathered, axis=0, keepdims=True), (8, LANES))
-    apply_tiles(plan, tiles, source, packed, rows)
+    apply_tiles(plan, tiles, rims, source, packed, rows)
     field, shot, whole = [], [], []
     for block in range(plan.blocks):
         field.append(source[plan.own(block), pl.ds(0, 1), :])
@@ -396,7 +469,7 @@
     spread(send, shot + [pack(groups)])
 
 
-def fifth_kernel(plan, recv, tiles, source, state, send, ends, image, ahead, steps, packed, rows):
+def fifth_kernel(plan, recv, tiles, rims, source, state, send, ends, image, ahead, steps, packed, rows):
     found = slots(plan)
     ring_into(plan, found, recv, 1, image)
     current, curve, square = totals(recv, plan.blocks, 3)
@@ -409,7 +482,7 @@
         left = field - alpha * (STIFFNESS * field + image[at])
         image[at] = left
         ahead[at] = left + beta * field
-    apply_tiles(plan, tiles, ahead, packed, rows)
+    apply_tiles(plan, tiles, rims, ahead, packed, rows)
     rests, heads, wholes = [], [], []
     for block in range(plan.blocks):
         own = plan.own(block)
@@ -476,35 +549,45 @@
         ],
         pltpu.HBM,
     )
-    send, tiles, where, right, state = call(
-        plan, build_kernel, exchange_layers(plan, send),
+    level, *others = exchange_layers(plan, send)
+    flipped = ((plan.ring * width, LANES), jnp.bfloat16)
+    tiles, where, right, centres, partial = call(
+        plan, inner_kernel, [level],
         [
-            slot(3 * blocks + 1), ((blocks, 27 * width, 2 * width), jnp.bfloat16),
+            ((inner_base(plan, blocks), 2 * width), jnp.bfloat16), ring, ring,
+            ((blocks, LANES, width), jnp.bfloat16), rows,
+        ],
+        [ring, flipped, ring, packed],
+    )
+    send, rims, where, right, state = call(
+        plan, edge_kernel, [*others, where, right, centres, partial],
+        [
+            slot(3 * blocks + 1), ((2 * 9 * width, 2 * width), jnp.bfloat16),
             ring, ring, (4 * blocks, width),
         ],
-        [ring, ((plan.ring * width, LANES), jnp.bfloat16), ring, packed, rows],
+        [ring, flipped, ring, packed, rows],
     )
     recv = exchange(send)
     send, residual, direction, scalars = call(
-        plan, second_kernel, [recv, tiles, right, state],
+        plan, second_kernel, [recv, tiles, rims, right, state],
         [slot(3 * blocks + 1), ring, ring, (blocks + 1, 8, width)],
         [ring, packed, rows],
     )
     recv = exchange(send)
     send, speeds = call(
-        plan, third_kernel, [recv, tiles, where, right, residual, direction, state, scalars],
+        plan, third_kernel, [recv, tiles, rims, where, right, residual, direction, state, scalars],
         [slot(4 * blocks + 1), (6 * blocks, width)],
         [ring, rows, ring, tile, packed, rows],
     )
     recv = exchange(send)
     send, source, final = call(
-        plan, fourth_kernel, [recv, tiles, state],
+        plan, fourth_kernel, [recv, tiles, rims, state],
         [slot(blocks + 1), ring, tile],
         [ring, packed, rows],
     )
     recv = exchange(send)
     send, ends = call(
-        plan, fifth_kernel, [recv, tiles, source, state],
+        plan, fifth_kernel, [recv, tiles, rims, source, state],
         [slot(1), (2 * blocks, width)],
         [ring, ring, tile, packed, rows],
     )

time: 78.1 us -> 77.4 us (level)
  waiting for transfers between devices: 1.37 us -> 0.01 us
    ppermute x1, waiting for transfers between devices: 1.37 us -> 0.01 us  [exchange_layers(): return [level, lax.ppermute(level, AXES[2], [(0, 1), (1, 0)])]]
    pallas_call x7 -> x8, Pallas kernels: 8.87 us -> 9.39 us  [call(): pl.pallas_call(functools.partial(kernel, plan), out_shape=[jax.ShapeDtype...]
  transfers between devices with their start and end apart: 1 -> 1, of which waited for: 1 -> 0; matrix products, arithmetic and copies ran while one was open for 0% -> 0% of each run, Pallas kernels for 0% -> 3%
where the time goes in v5:
time: 77.4 us; the launch traced here: 77.1 us
  blocking collectives  67 us (87%)
  Pallas kernels  9.39 us (12%)
    all_to_all x5, blocking collectives, exchange(): return lax.all_to_all(send, AXES, 0, 0, tiled=True)  50.8 us
    all_to_all x1, blocking collectives, exchange_layers(): level = lax.all_to_all(send, AXES[:2], 0, 0, tiled=True)  16.2 us
    pallas_call x8, Pallas kernels, call(): pl.pallas_call(functools.partial(kernel, plan), out_shape=[jax.ShapeDtype...  9.39 us
  transfers between devices with their start and end apart: 1, of which 0 were waited for; matrix products, arithmetic and copies ran while one was open for 0% of the time, Pallas kernels for 3%

profile of v5, /device:TPU:0, one launch (start us, length us, event | category | flops | bytes accessed | tf_op | source)
XLA Modules:
  0.0 77.1 jit_solution(16708257379796350826)
XLA Ops:
  0.6 0.8 %pack_kernel.1 = f32[16,18,1,128]{3,2,1,0:T(1,128)S(1)} custom-call(s32[1,3]{1,0:T(1,128)} %bitcast.11, f32[9,1,128]{2,1,0:T(1,128)} %bitcast.9, f32[9,1,128]{2,1,0:T(1,128)} %bitcast.10), custom_call_target="tpu_custom_call" | custom-call | tf_op jit(solution)/shard_map/pack_kernel/pallas_call | solution.py:518
  1.5 16.2 %all_to_all.30.recv = f32[16,18,1,128]{3,2,1,0:T(1,128)S(1)} all-to-all(f32[16,18,1,128]{3,2,1,0:T(1,128)S(1)} %pack_kernel.1), channel_id=1, replica_groups=mesh['gx'=4,'gy'=4,'gz'=2] {'gx','gy'}, dimensions={0} | all-to-all | bytes 294912 | tf_op jit(solution)/shard_map/all_to_all | solution.py:23
  17.7 0.0 collective-permute-start
  17.7 2.0 %inner_kernel.1 = (bf16[8064,256]{1,0:T(8,128)(2,1)S(1)}, f32[45,8,128]{2,1,0:T(8,128)S(1)}, f32[45,8,128]{2,1,0:T(8,128)S(1)}, bf16[3,128,128]{2,1,0:T(8,128)(2,1)S(1)}, f32[3,8,128]{2,1,0:T(8,128)S(1)}) custom-call(f32[16,18,1,128]{3,2,1,0:T(1,128)S(1)} %all_to_all.30.recv), custom_call_target="tpu_custom_call" | custom-call | tf_op jit(solution)/shard_map/inner_kernel/pallas_call | solution.py:518
  19.7 0.0 collective-permute-done.refs_0_
  19.7 1.3 %edge_kernel.1 = (f32[32,10,1,128]{3,2,1,0:T(1,128)S(1)}, bf16[2304,256]{1,0:T(8,128)(2,1)S(1)}, f32[45,8,128]{2,1,0:T(8,128)S(1)}, f32[45,8,128]{2,1,0:T(8,128)S(1)}, f32[12,128]{1,0:T(8,128)S(1)}) custom-call(f32[16,18,1,128]{3,2,1,0:T(1,128)S(1)} %collective-permute-done.refs_0_, f32[45,8,128]{2,1,0:T(8,128)S(1)} %get-tuple-element.25.refs_1_, ...), custom_call_target="tpu_custom_call" | custom-call | tf_op jit(solution)/shard_map/edge_kernel/pallas_call | solution.py:518
  21.0 10.2 %all_to_all.31.recv = f32[32,10,1,128]{3,2,1,0:T(1,128)S(1)} all-to-all(f32[32,10,1,128]{3,2,1,0:T(1,128)S(1)} %get-tuple-element.29), channel_id=1, replica_groups=mesh['gx'=4,'gy'=4,'gz'=2] {'gx','gy','gz'}, dimensions={0} | all-to-all | bytes 327680 | tf_op jit(solution)/shard_map/all_to_all | solution.py:19
  31.2 1.2 %second_kernel.1 = (f32[32,10,1,128]{3,2,1,0:T(1,128)S(1)}, f32[45,8,128]{2,1,0:T(8,128)S(1)}, f32[45,8,128]{2,1,0:T(8,128)S(1)}, f32[4,8,128]{2,1,0:T(8,128)S(1)}) custom-call(f32[32,10,1,128]{3,2,1,0:T(1,128)S(1)} %all_to_all.31.recv, bf16[8064,256]{1,0:T(8,128)(2,1)S(1)} %get-tuple-element.30.tiles, bf16[2304,256]{1,0:T(8,128)(2,1)S(1)} %get-tuple-element.31.rims, ...), custom_call_target="tpu_custom_call" | custom-call | tf_op jit(solution)/shard_map/second_kernel/pallas_call | solution.py:518
  32.4 10.6 %all_to_all.32.recv = f32[32,10,1,128]{3,2,1,0:T(1,128)S(1)} all-to-all(f32[32,10,1,128]{3,2,1,0:T(1,128)S(1)} %get-tuple-element.34), channel_id=1, replica_groups=mesh['gx'=4,'gy'=4,'gz'=2] {'gx','gy','gz'}, dimensions={0} | all-to-all | bytes 327680 | tf_op jit(solution)/shard_map/all_to_all | solution.py:19
  43.0 1.2 %third_kernel.1 = (f32[32,13,1,128]{3,2,1,0:T(1,128)S(1)}, f32[18,128]{1,0:T(8,128)S(1)}) custom-call(f32[32,10,1,128]{3,2,1,0:T(1,128)S(1)} %all_to_all.32.recv, bf16[8064,256]{1,0:T(8,128)(2,1)S(1)} %get-tuple-element.30.tiles, bf16[2304,256]{1,0:T(8,128)(2,1)S(1)} %get-tuple-element.31.rims, f32[45,8,128]{2,1,0:T(8,128)S(1)} %get-tuple-element.35.where, ...), custom_call_target="tpu_custom_call" | custom-call | tf_op jit(solution)/shard_map/third_kernel/pallas_call | solution.py:518
  44.2 11.1 %all_to_all.33.recv = f32[32,13,1,128]{3,2,1,0:T(1,128)S(1)} all-to-all(f32[32,13,1,128]{3,2,1,0:T(1,128)S(1)} %get-tuple-element.39), channel_id=1, replica_groups=mesh['gx'=4,'gy'=4,'gz'=2] {'gx','gy','gz'}, dimensions={0} | all-to-all | bytes 425984 | tf_op jit(solution)/shard_map/all_to_all | solution.py:19
  55.3 1.1 %fourth_kernel.1 = (f32[32,4,1,128]{3,2,1,0:T(1,128)S(1)}, f32[45,8,128]{2,1,0:T(8,128)S(1)}, f32[8,128]{1,0:T(8,128)S(1)}) custom-call(f32[32,13,1,128]{3,2,1,0:T(1,128)S(1)} %all_to_all.33.recv, bf16[8064,256]{1,0:T(8,128)(2,1)S(1)} %get-tuple-element.30.tiles, bf16[2304,256]{1,0:T(8,128)(2,1)S(1)} %get-tuple-element.31.rims, ...), custom_call_target="tpu_custom_call" | custom-call | tf_op jit(solution)/shard_map/fourth_kernel/pallas_call | solution.py:518
  56.4 10.1 %all_to_all.34.recv = f32[32,4,1,128]{3,2,1,0:T(1,128)S(1)} all-to-all(f32[32,4,1,128]{3,2,1,0:T(1,128)S(1)} %get-tuple-element.40), channel_id=1, replica_groups=mesh['gx'=4,'gy'=4,'gz'=2] {'gx','gy','gz'}, dimensions={0} | all-to-all | bytes 131072 | tf_op jit(solution)/shard_map/all_to_all | solution.py:19
  66.5 1.1 %fifth_kernel.1 = (f32[32,1,1,128]{3,2,1,0:T(1,128)S(1)}, f32[6,128]{1,0:T(8,128)S(1)}) custom-call(f32[32,4,1,128]{3,2,1,0:T(1,128)S(1)} %all_to_all.34.recv, bf16[8064,256]{1,0:T(8,128)(2,1)S(1)} %get-tuple-element.30.tiles, bf16[2304,256]{1,0:T(8,128)(2,1)S(1)} %get-tuple-element.31.rims, f32[45,8,128]{2,1,0:T(8,128)S(1)} %get-tuple-element.41.source, ...), custom_call_target="tpu_custom_call" | custom-call | tf_op jit(solution)/shard_map/fifth_kernel/pallas_call | solution.py:518
  67.6 8.8 %all_to_all.35.recv = f32[32,1,1,128]{3,2,1,0:T(1,128)S(1)} all-to-all(f32[32,1,1,128]{3,2,1,0:T(1,128)S(1)} %get-tuple-element.42), channel_id=1, replica_groups=mesh['gx'=4,'gy'=4,'gz'=2] {'gx','gy','gz'}, dimensions={0} | all-to-all | bytes 32768 | tf_op jit(solution)/shard_map/all_to_all | solution.py:19
  76.4 0.7 last_kernel.1
Async XLA Ops:
  17.7 2.0 %collective-permute-start = (f32[16,18,1,128]{3,2,1,0:T(1,128)S(1)}, f32[16,18,1,128]{3,2,1,0:T(1,128)S(1)}, u32[]{:S(2)}, u32[]{:S(2)}) collective-permute-start(f32[16,18,1,128]{3,2,1,0:T(1,128)S(1)} %all_to_all.30.recv), channel_id=1, source_target_pairs={{0,1},{1,0},{2,3},{3,2},{4,5},{5,4},{6,7},{7,6},{8,9},{9,8},{10,11... | collective-permute-start | bytes 442376 | tf_op jit(solution)/shard_map/ppermute | solution.py:26

commit v6 on v5

--- a/solution.py
+++ b/solution.py
@@ -35,51 +35,62 @@
         self.devices = self.count[0] * self.count[1] * self.count[2]
         self.blocks = blocks
         self.width = width
-        self.deep = blocks + 2
+        self.rims = 1 if self.count[2] == 2 else 2
+        self.deep = blocks + self.rims
         self.ring = 9 * self.deep
         self.cube = (2.0 / width) ** (1.0 / 3.0)
         self.unit = self.cube ** 0.5
 
     def own(self, block):
-        return 4 * self.deep + block + 1
-
-
-def slots(plan, axes=3):
+        return 4 * self.deep + block
+
+
+def rims_of(plan):
+    last = plan.blocks - 1
+    if plan.rims == 2:
+        return [(-1, 0, last, -1), (1, last, 0, plan.blocks)]
+    above = lax.axis_index(AXES[2]) == 0
+    choose = lambda yes, no: jnp.where(above, jnp.int32(yes), jnp.int32(no))
+    return [(choose(1, -1), choose(last, 0), choose(0, last), choose(plan.blocks, -1))]
+
+
+def slots(plan, rims, axes=3):
     place = [lax.axis_index(axis) for axis in AXES]
-    found = {}
-    for code in range(27):
-        at = [place[0] + code // 9 - 1, place[1] + code // 3 % 3 - 1, place[2] + code % 3 - 1]
-        present = None
-        slot = 0
-        for axis, (value, count) in enumerate(zip(at, plan.count)):
-            inside = jnp.logical_and(value >= 0, value < count)
-            present = inside if present is None else jnp.logical_and(present, inside)
-            if axis < axes:
-                slot = slot * count + jnp.clip(value, 0, count - 1)
-        found[code] = (slot, present)
+    found = []
+    for column in range(9):
+        beside = []
+        for step in [0] + [rim[0] for rim in rims]:
+            at = [place[0] + column // 3 - 1, place[1] + column % 3 - 1, place[2] + step]
+            present = None
+            slot = 0
+            for axis, (value, count) in enumerate(zip(at, plan.count)):
+                inside = jnp.logical_and(value >= 0, value < count)
+                present = inside if present is None else jnp.logical_and(present, inside)
+                if axis < axes:
+                    slot = slot * count + jnp.clip(value, 0, count - 1)
+            beside.append((slot, present))
+        found.append(beside)
     return found
 
 
-def gather_ring(plan, found, layers, fields, store, levels=None):
+def gather_ring(plan, rims, found, layers, fields, store, levels=None):
     for column in range(9):
         for level in levels or range(plan.deep):
-            if level == 0:
-                step, block = 0, plan.blocks - 1
-            elif level == plan.deep - 1:
-                step, block = 2, 0
-            else:
-                step, block = 1, level - 1
-            slot, present = found[column * 3 + step]
-            rows = [layers[step][slot, field * plan.blocks + block] for field in range(fields)]
-            store(column * plan.deep + level, column, level, rows, present)
-
-
-def ring_into(plan, found, recv, fields, ref):
-    def store(at, column, level, rows, present):
+            layer, block, depth = 0, level, level
+            if level >= plan.blocks:
+                layer = level - plan.blocks + 1
+                block, depth = rims[layer - 1][2:]
+            slot, present = found[column][layer]
+            rows = [layers[layer][slot, field * plan.blocks + block] for field in range(fields)]
+            store(column * plan.deep + level, column, depth, rows, present)
+
+
+def ring_into(plan, rims, recv, fields, ref):
+    def store(at, column, depth, rows, present):
         for field, row in enumerate(rows):
             ref[at, pl.ds(field, 1), :] = row
 
-    gather_ring(plan, found, [recv] * 3, fields, store)
+    gather_ring(plan, rims, slots(plan, rims), [recv] * (1 + plan.rims), fields, store)
 
 
 def lane_ids(sublanes=1):
@@ -147,16 +158,12 @@
 
 
 def inner_span(plan, block):
-    low = max(block, 1)
-    return low, min(block + 2, plan.blocks) + 1 - low
+    low = max(block - 1, 0)
+    return low, min(block + 2, plan.blocks) - low
 
 
 def inner_base(plan, block):
     return 9 * sum(inner_span(plan, before)[1] for before in range(block)) * plan.width
-
-
-def edges(plan):
-    return [(0, 0), (plan.blocks - 1, plan.blocks + 1)]
 
 
 def groups_of(number):
@@ -179,26 +186,28 @@
     return both[0:8] + both[8:16] + both[16:24]
 
 
-def apply_tiles(plan, tiles, rims, ring, packed, rows):
+def apply_tiles(plan, rims, tiles, outer, ring, packed, rows):
     split_ring(plan, ring, packed)
     for block in range(plan.blocks):
         low, number = inner_span(plan, block)
         base = inner_base(plan, block)
-        parts = [
-            tile_sum(plan, tiles, base, packed, low, number, columns)
-            for columns in groups_of(number)
-        ]
-        for edge, (at, level) in enumerate(edges(plan)):
-            if at == block:
-                base = edge * 9 * plan.width
-                parts += [
-                    tile_sum(plan, rims, base, packed, level, 1, columns)
-                    for columns in groups_of(1)
-                ]
-        total = parts[0]
-        for part in parts[1:]:
-            total = total + part
+        total = None
+        for columns in groups_of(number):
+            part = tile_sum(plan, tiles, base, packed, low, number, columns)
+            total = part if total is None else total + part
         rows[block] = fold(total)
+    add_rims(plan, rims, outer, packed, rows, lambda e, columns: None)
+
+
+def add_rims(plan, rims, outer, packed, rows, before):
+    for e, rim in enumerate(rims):
+        total = None
+        for columns in groups_of(1):
+            before(e, columns)
+            base = e * 9 * plan.width
+            part = tile_sum(plan, outer, base, packed, plan.blocks + e, 1, columns)
+            total = part if total is None else total + part
+        rows[rim[1]] = rows[rim[1]] + fold(total)
 
 
 def pack_kernel(plan, counts_in, offsets_in, velocity_in, send, counts, offsets, velocity, sems):
@@ -225,10 +234,12 @@
     spread(send, rows)
 
 
-def place_ring(plan, found, layers, levels, points, mixed, where, right):
-    def store(at, column, level, got, present):
-        shift = (column // 3 - 1, column % 3 - 1, level - (plan.deep - 1) // 2)
-        spots = [plan.unit * (got[axis] + shift[axis]) for axis in range(3)]
+def place_ring(plan, rims, layers, levels, points, mixed, where, right):
+    def store(at, column, depth, got, present):
+        shift = (column // 3 - 1, column % 3 - 1, depth - (plan.blocks - 1) // 2)
+        spots = [
+            plan.unit * (got[axis] + jnp.asarray(shift[axis], jnp.float32)) for axis in range(3)
+        ]
         spots[0] = jnp.where(present, spots[0], FAR)
         points[at, pl.ds(3, 1), :] = spots[0] * spots[0] + spots[1] * spots[1] + spots[2] * spots[2]
         points[at, pl.ds(4, 1), :] = jnp.ones((1, LANES), jnp.float32)
@@ -243,7 +254,7 @@
             right[at, pl.ds(axis, 1), :] = field
             mixed[at, pl.ds(axis, 1), :] = field
 
-    gather_ring(plan, found, layers, 6, store, levels)
+    gather_ring(plan, rims, slots(plan, rims, 2), layers, 6, store, levels)
 
 
 def flip_points(plan, levels, points, flipped):
@@ -252,8 +263,7 @@
             at = column * plan.deep + level
             first, second, third = split(points[at])
             stacked = jnp.concatenate([first, second, third, first, second, first], axis=0)
-            padded = jnp.concatenate([stacked, jnp.zeros((LANES - 48, LANES), jnp.float32)], axis=0)
-            flipped[pl.ds(at * plan.width, plan.width), :] = jnp.transpose(padded).astype(jnp.bfloat16)
+            flipped[pl.ds(at * plan.width, plan.width), :] = jnp.transpose(stacked).astype(jnp.bfloat16)
 
 
 def weigh(plan, flipped, centre, level, number, columns, tiles, base):
@@ -272,8 +282,8 @@
 
 
 def inner_kernel(plan, recv, tiles, where, right, centres, partial, points, flipped, mixed, packed):
-    levels = range(1, plan.blocks + 1)
-    place_ring(plan, slots(plan, 2), [None, recv, None], levels, points, mixed, where, right)
+    levels = range(plan.blocks)
+    place_ring(plan, rims_of(plan), [recv], levels, points, mixed, where, right)
     flip_points(plan, levels, points, flipped)
     split_ring(plan, mixed, packed, levels)
     sub = sublane_ids()
@@ -286,8 +296,7 @@
         own = jnp.where(sub == 4, plan.cube - square, own)
         first, second, third = split(own)
         stacked = jnp.concatenate([first, first, first, second, second, third], axis=0)
-        padded = jnp.concatenate([stacked, jnp.zeros((LANES - 48, LANES), jnp.float32)], axis=0)
-        centre = padded.astype(jnp.bfloat16)
+        centre = stacked.astype(jnp.bfloat16)
         centres[block] = centre
         low, number = inner_span(plan, block)
         base = inner_base(plan, block)
@@ -303,14 +312,13 @@
     others = refs[:-14]
     (
         near_where, near_right, centres, partial,
-        send, rims, where, right, state, points, flipped, mixed, packed, rows,
+        send, outer, where, right, state, points, flipped, mixed, packed, rows,
     ) = refs[-14:]
-    levels = [0, plan.deep - 1]
-    place_ring(
-        plan, slots(plan, 2), [others[0], None, others[-1]], levels, points, mixed, where, right
-    )
+    rims = rims_of(plan)
+    levels = range(plan.blocks, plan.deep)
+    place_ring(plan, rims, [None, *others], levels, points, mixed, where, right)
     for column in range(9):
-        for level in range(1, plan.blocks + 1):
+        for level in range(plan.blocks):
             at = column * plan.deep + level
             where[at] = near_where[at]
             right[at] = near_right[at]
@@ -318,14 +326,12 @@
     split_ring(plan, mixed, packed, levels)
     for block in range(plan.blocks):
         rows[block] = partial[block]
-    for edge, (block, level) in enumerate(edges(plan)):
-        base = edge * 9 * plan.width
-        total = None
-        for columns in groups_of(1):
-            weigh(plan, flipped, centres[block], level, 1, columns, rims, base)
-            part = tile_sum(plan, rims, base, packed, level, 1, columns)
-            total = part if total is None else total + part
-        rows[block] = rows[block] + fold(total)
+
+    def before(e, columns):
+        centre = centres[rims[e][1]]
+        weigh(plan, flipped, centre, plan.blocks + e, 1, columns, outer, e * 9 * plan.width)
+
+    add_rims(plan, rims, outer, packed, rows, before)
     image = [[None] * plan.blocks for _ in range(3)]
     whole = [[None] * plan.blocks for _ in range(3)]
     start = [[None] * plan.blocks for _ in range(3)]
@@ -350,9 +356,9 @@
     spread(send, sum(image, []) + [pack(groups)])
 
 
-def second_kernel(plan, recv, tiles, rims, right, state, send, residual, direction, scalars, image, packed, rows):
-    found = slots(plan)
-    ring_into(plan, found, recv, 3, image)
+def second_kernel(plan, recv, tiles, outer, right, state, send, residual, direction, scalars, image, packed, rows):
+    rims = rims_of(plan)
+    ring_into(plan, rims, recv, 3, image)
     current, curve, square = totals(recv, 3 * plan.blocks, 3)
     alpha = current / curve
     following = jnp.maximum(alpha * alpha * square - current, 0.0)
@@ -365,7 +371,7 @@
     scalars[plan.blocks] = alpha
     for block in range(plan.blocks):
         scalars[block] = image[plan.own(block)]
-    apply_tiles(plan, tiles, rims, direction, packed, rows)
+    apply_tiles(plan, rims, tiles, outer, direction, packed, rows)
     out = []
     groups = [[], [], [], []]
     for axis in range(3):
@@ -385,11 +391,11 @@
 
 
 def third_kernel(
-    plan, recv, tiles, rims, where, right, residual, direction, state, scalars,
+    plan, recv, tiles, outer, where, right, residual, direction, state, scalars,
     send, ends, image, sofar, ahead, steps, packed, rows,
 ):
-    found = slots(plan)
-    ring_into(plan, found, recv, 3, image)
+    rims = rims_of(plan)
+    ring_into(plan, rims, recv, 3, image)
     current, curve, cross, square = totals(recv, 3 * plan.blocks, 4)
     alpha = current / curve
     following = jnp.maximum(current - 2.0 * alpha * cross + alpha * alpha * square, 0.0)
@@ -416,7 +422,7 @@
         if at - plan.own(0) in range(plan.blocks):
             image[at] = rest
             sofar[at - plan.own(0)] = made
-    apply_tiles(plan, tiles, rims, ahead, packed, rows)
+    apply_tiles(plan, rims, tiles, outer, ahead, packed, rows)
     scale = 1.0 / plan.unit
     base = []
     each = [[None] * plan.blocks for _ in range(3)]
@@ -449,9 +455,9 @@
     spread(send, base + sum(each, []) + [pack(groups)])
 
 
-def fourth_kernel(plan, recv, tiles, rims, state, send, source, steps, parts, packed, rows):
-    found = slots(plan)
-    ring_into(plan, found, recv, 4, parts)
+def fourth_kernel(plan, recv, tiles, outer, state, send, source, steps, parts, packed, rows):
+    rims = rims_of(plan)
+    ring_into(plan, rims, recv, 4, parts)
     current, curve = totals(recv, 4 * plan.blocks, 2)
     sub = sublane_ids()
     steps[...] = current / curve
@@ -459,7 +465,7 @@
     for at in range(plan.ring):
         gathered = jnp.where(sub < 4, parts[at] * factor, 0.0)
         source[at] = jnp.broadcast_to(-jnp.sum(gathered, axis=0, keepdims=True), (8, LANES))
-    apply_tiles(plan, tiles, rims, source, packed, rows)
+    apply_tiles(plan, rims, tiles, outer, source, packed, rows)
     field, shot, whole = [], [], []
     for block in range(plan.blocks):
         field.append(source[plan.own(block), pl.ds(0, 1), :])
@@ -469,9 +475,9 @@
     spread(send, shot + [pack(groups)])
 
 
-def fifth_kernel(plan, recv, tiles, rims, source, state, send, ends, image, ahead, steps, packed, rows):
-    found = slots(plan)
-    ring_into(plan, found, recv, 1, image)
+def fifth_kernel(plan, recv, tiles, outer, source, state, send, ends, image, ahead, steps, packed, rows):
+    rims = rims_of(plan)
+    ring_into(plan, rims, recv, 1, image)
     current, curve, square = totals(recv, plan.blocks, 3)
     steps[...] = current / curve
     alpha = steps[pl.ds(0, 1), :]
@@ -482,7 +488,7 @@
         left = field - alpha * (STIFFNESS * field + image[at])
         image[at] = left
         ahead[at] = left + beta * field
-    apply_tiles(plan, tiles, rims, ahead, packed, rows)
+    apply_tiles(plan, rims, tiles, outer, ahead, packed, rows)
     rests, heads, wholes = [], [], []
     for block in range(plan.blocks):
         own = plan.own(block)
@@ -550,44 +556,44 @@
         pltpu.HBM,
     )
     level, *others = exchange_layers(plan, send)
-    flipped = ((plan.ring * width, LANES), jnp.bfloat16)
+    flipped = ((plan.ring * width, 48), jnp.bfloat16)
     tiles, where, right, centres, partial = call(
         plan, inner_kernel, [level],
         [
             ((inner_base(plan, blocks), 2 * width), jnp.bfloat16), ring, ring,
-            ((blocks, LANES, width), jnp.bfloat16), rows,
+            ((blocks, 48, width), jnp.bfloat16), rows,
         ],
         [ring, flipped, ring, packed],
     )
-    send, rims, where, right, state = call(
+    send, outer, where, right, state = call(
         plan, edge_kernel, [*others, where, right, centres, partial],
         [
-            slot(3 * blocks + 1), ((2 * 9 * width, 2 * width), jnp.bfloat16),
+            slot(3 * blocks + 1), ((plan.rims * 9 * width, 2 * width), jnp.bfloat16),
             ring, ring, (4 * blocks, width),
         ],
         [ring, flipped, ring, packed, rows],
     )
     recv = exchange(send)
     send, residual, direction, scalars = call(
-        plan, second_kernel, [recv, tiles, rims, right, state],
+        plan, second_kernel, [recv, tiles, outer, right, state],
         [slot(3 * blocks + 1), ring, ring, (blocks + 1, 8, width)],
         [ring, packed, rows],
     )
     recv = exchange(send)
     send, speeds = call(
-        plan, third_kernel, [recv, tiles, rims, where, right, residual, direction, state, scalars],
+        plan, third_kernel, [recv, tiles, outer, where, right, residual, direction, state, scalars],
         [slot(4 * blocks + 1), (6 * blocks, width)],
         [ring, rows, ring, tile, packed, rows],
     )
     recv = exchange(send)
     send, source, final = call(
-        plan, fourth_kernel, [recv, tiles, rims, state],
+        plan, fourth_kernel, [recv, tiles, outer, state],
         [slot(blocks + 1), ring, tile],
         [ring, packed, rows],
     )
     recv = exchange(send)
     send, ends = call(
-        plan, fifth_kernel, [recv, tiles, rims, source, state],
+        plan, fifth_kernel, [recv, tiles, outer, source, state],
         [slot(1), (2 * blocks, width)],
         [ring, ring, tile, packed, rows],
     )

time: 77.4 us -> 77.1 us (level)
  no operation moved by 1% of the time
where the time goes in v6:
time: 77.1 us; the launch traced here: 76.8 us
  blocking collectives  67 us (87%)
  Pallas kernels  9.07 us (12%)
    all_to_all x5, blocking collectives, exchange(): return lax.all_to_all(send, AXES, 0, 0, tiled=True)  50.8 us
    all_to_all x1, blocking collectives, exchange_layers(): level = lax.all_to_all(send, AXES[:2], 0, 0, tiled=True)  16.2 us
    pallas_call x8, Pallas kernels, call(): pl.pallas_call(functools.partial(kernel, plan), out_shape=[jax.ShapeDtype...  9.07 us
  transfers between devices with their start and end apart: 1, of which 0 were waited for; matrix products, arithmetic and copies ran while one was open for 0% of the time, Pallas kernels for 3%

profile of v6, /device:TPU:0, one launch (start us, length us, event | category | flops | bytes accessed | tf_op | source)
XLA Modules:
  0.0 76.8 jit_solution(1294398894886606876)
XLA Ops:
  0.6 0.8 %pack_kernel.1 = f32[16,18,1,128]{3,2,1,0:T(1,128)S(1)} custom-call(s32[1,3]{1,0:T(1,128)} %bitcast.11, f32[9,1,128]{2,1,0:T(1,128)} %bitcast.9, f32[9,1,128]{2,1,0:T(1,128)} %bitcast.10), custom_call_target="tpu_custom_call" | custom-call | tf_op jit(solution)/shard_map/pack_kernel/pallas_call | solution.py:524
  1.5 16.2 %all_to_all.30.recv = f32[16,18,1,128]{3,2,1,0:T(1,128)S(1)} all-to-all(f32[16,18,1,128]{3,2,1,0:T(1,128)S(1)} %pack_kernel.1), channel_id=1, replica_groups=mesh['gx'=4,'gy'=4,'gz'=2] {'gx','gy'}, dimensions={0} | all-to-all | bytes 294912 | tf_op jit(solution)/shard_map/all_to_all | solution.py:23
  17.7 0.0 collective-permute-start
  17.7 2.0 %inner_kernel.1 = (bf16[8064,256]{1,0:T(8,128)(2,1)S(1)}, f32[36,8,128]{2,1,0:T(8,128)S(1)}, f32[36,8,128]{2,1,0:T(8,128)S(1)}, bf16[3,48,128]{2,1,0:T(8,128)(2,1)S(1)}, f32[3,8,128]{2,1,0:T(8,128)S(1)}) custom-call(f32[16,18,1,128]{3,2,1,0:T(1,128)S(1)} %all_to_all.30.recv), custom_call_target="tpu_custom_call" | custom-call | tf_op jit(solution)/shard_map/inner_kernel/pallas_call | solution.py:524
  19.7 0.0 collective-permute-done.refs_0_
  19.7 1.0 %edge_kernel.1 = (f32[32,10,1,128]{3,2,1,0:T(1,128)S(1)}, bf16[1152,256]{1,0:T(8,128)(2,1)S(1)}, f32[36,8,128]{2,1,0:T(8,128)S(1)}, f32[36,8,128]{2,1,0:T(8,128)S(1)}, f32[12,128]{1,0:T(8,128)S(1)}) custom-call(f32[16,18,1,128]{3,2,1,0:T(1,128)S(1)} %collective-permute-done.refs_0_, f32[36,8,128]{2,1,0:T(8,128)S(1)} %get-tuple-element.25.refs_1_, ...), custom_call_target="tpu_custom_call" | custom-call | tf_op jit(solution)/shard_map/edge_kernel/pallas_call | solution.py:524
  20.7 10.2 %all_to_all.31.recv = f32[32,10,1,128]{3,2,1,0:T(1,128)S(1)} all-to-all(f32[32,10,1,128]{3,2,1,0:T(1,128)S(1)} %get-tuple-element.29), channel_id=1, replica_groups=mesh['gx'=4,'gy'=4,'gz'=2] {'gx','gy','gz'}, dimensions={0} | all-to-all | bytes 327680 | tf_op jit(solution)/shard_map/all_to_all | solution.py:19
  30.9 1.2 %second_kernel.1 = (f32[32,10,1,128]{3,2,1,0:T(1,128)S(1)}, f32[36,8,128]{2,1,0:T(8,128)S(1)}, f32[36,8,128]{2,1,0:T(8,128)S(1)}, f32[4,8,128]{2,1,0:T(8,128)S(1)}) custom-call(f32[32,10,1,128]{3,2,1,0:T(1,128)S(1)} %all_to_all.31.recv, bf16[8064,256]{1,0:T(8,128)(2,1)S(1)} %get-tuple-element.30.tiles, bf16[1152,256]{1,0:T(8,128)(2,1)S(1)} %get-tuple-element.31.outer, ...), custom_call_target="tpu_custom_call" | custom-call | tf_op jit(solution)/shard_map/second_kernel/pallas_call | solution.py:524
  32.1 10.6 %all_to_all.32.recv = f32[32,10,1,128]{3,2,1,0:T(1,128)S(1)} all-to-all(f32[32,10,1,128]{3,2,1,0:T(1,128)S(1)} %get-tuple-element.34), channel_id=1, replica_groups=mesh['gx'=4,'gy'=4,'gz'=2] {'gx','gy','gz'}, dimensions={0} | all-to-all | bytes 327680 | tf_op jit(solution)/shard_map/all_to_all | solution.py:19
  42.7 1.2 %third_kernel.1 = (f32[32,13,1,128]{3,2,1,0:T(1,128)S(1)}, f32[18,128]{1,0:T(8,128)S(1)}) custom-call(f32[32,10,1,128]{3,2,1,0:T(1,128)S(1)} %all_to_all.32.recv, bf16[8064,256]{1,0:T(8,128)(2,1)S(1)} %get-tuple-element.30.tiles, bf16[1152,256]{1,0:T(8,128)(2,1)S(1)} %get-tuple-element.31.outer, f32[36,8,128]{2,1,0:T(8,128)S(1)} %get-tuple-element.35.where, ...), custom_call_target="tpu_custom_call" | custom-call | tf_op jit(solution)/shard_map/third_kernel/pallas_call | solution.py:524
  43.8 11.1 %all_to_all.33.recv = f32[32,13,1,128]{3,2,1,0:T(1,128)S(1)} all-to-all(f32[32,13,1,128]{3,2,1,0:T(1,128)S(1)} %get-tuple-element.39), channel_id=1, replica_groups=mesh['gx'=4,'gy'=4,'gz'=2] {'gx','gy','gz'}, dimensions={0} | all-to-all | bytes 425984 | tf_op jit(solution)/shard_map/all_to_all | solution.py:19
  54.9 1.1 %fourth_kernel.1 = (f32[32,4,1,128]{3,2,1,0:T(1,128)S(1)}, f32[36,8,128]{2,1,0:T(8,128)S(1)}, f32[8,128]{1,0:T(8,128)S(1)}) custom-call(f32[32,13,1,128]{3,2,1,0:T(1,128)S(1)} %all_to_all.33.recv, bf16[8064,256]{1,0:T(8,128)(2,1)S(1)} %get-tuple-element.30.tiles, bf16[1152,256]{1,0:T(8,128)(2,1)S(1)} %get-tuple-element.31.outer, ...), custom_call_target="tpu_custom_call" | custom-call | tf_op jit(solution)/shard_map/fourth_kernel/pallas_call | solution.py:524
  56.1 10.1 %all_to_all.34.recv = f32[32,4,1,128]{3,2,1,0:T(1,128)S(1)} all-to-all(f32[32,4,1,128]{3,2,1,0:T(1,128)S(1)} %get-tuple-element.40), channel_id=1, replica_groups=mesh['gx'=4,'gy'=4,'gz'=2] {'gx','gy','gz'}, dimensions={0} | all-to-all | bytes 131072 | tf_op jit(solution)/shard_map/all_to_all | solution.py:19
  66.1 1.1 %fifth_kernel.1 = (f32[32,1,1,128]{3,2,1,0:T(1,128)S(1)}, f32[6,128]{1,0:T(8,128)S(1)}) custom-call(f32[32,4,1,128]{3,2,1,0:T(1,128)S(1)} %all_to_all.34.recv, bf16[8064,256]{1,0:T(8,128)(2,1)S(1)} %get-tuple-element.30.tiles, bf16[1152,256]{1,0:T(8,128)(2,1)S(1)} %get-tuple-element.31.outer, f32[36,8,128]{2,1,0:T(8,128)S(1)} %get-tuple-element.41.source, ...), custom_call_target="tpu_custom_call" | custom-call | tf_op jit(solution)/shard_map/fifth_kernel/pallas_call | solution.py:524
  67.3 8.8 %all_to_all.35.recv = f32[32,1,1,128]{3,2,1,0:T(1,128)S(1)} all-to-all(f32[32,1,1,128]{3,2,1,0:T(1,128)S(1)} %get-tuple-element.42), channel_id=1, replica_groups=mesh['gx'=4,'gy'=4,'gz'=2] {'gx','gy','gz'}, dimensions={0} | all-to-all | bytes 32768 | tf_op jit(solution)/shard_map/all_to_all | solution.py:19
  76.1 0.7 last_kernel.1
Async XLA Ops:
  17.7 2.0 %collective-permute-start = (f32[16,18,1,128]{3,2,1,0:T(1,128)S(1)}, f32[16,18,1,128]{3,2,1,0:T(1,128)S(1)}, u32[]{:S(2)}, u32[]{:S(2)}) collective-permute-start(f32[16,18,1,128]{3,2,1,0:T(1,128)S(1)} %all_to_all.30.recv), channel_id=1, source_target_pairs={{0,1},{1,0},{2,3},{3,2},{4,5},{5,4},{6,7},{7,6},{8,9},{9,8},{10,11... | collective-permute-start | bytes 442376 | tf_op jit(solution)/shard_map/ppermute | solution.py:26

commit v7 on v6

--- a/solution.py
+++ b/solution.py
@@ -148,13 +148,49 @@
     return first, second, rest - second
 
 
-def split_ring(plan, ring, packed, levels=None):
+def stack_full(value):
+    first, second, third = split(value)
+    return jnp.concatenate([first, second, third, jnp.zeros_like(third)], axis=0)
+
+
+def fold_full(total):
+    both = total[:, :LANES] + total[:, LANES:]
+    return both[0:8] + both[8:16] + both[16:24]
+
+
+def stack_three(value):
+    first, second, third = split(value)
+    joined = jnp.where(sublane_ids() < 3, first, pltpu.roll(second, 3, 0))
+    return jnp.concatenate([joined, third], axis=0)
+
+
+def fold_three(total):
+    both = total[:, :LANES] + total[:, LANES:]
+    return both[0:8] + pltpu.roll(both[0:8], 5, 0) + both[8:16]
+
+
+def stack_one(value):
+    first, second, third = split(value)
+    sub = sublane_ids()
+    joined = jnp.where(sub == 0, first, jnp.where(sub == 1, second, third))
+    return jnp.concatenate([jnp.where(sub < 3, joined, 0.0), jnp.zeros_like(third)], axis=0)
+
+
+def fold_one(total):
+    both = total[0:8, :LANES] + total[0:8, LANES:]
+    return jnp.broadcast_to(jnp.sum(both, axis=0, keepdims=True), (8, LANES))
+
+
+FULL = (stack_full, fold_full)
+THREE = (stack_three, fold_three)
+ONE = (stack_one, fold_one)
+
+
+def split_ring(plan, ring, packed, form, levels=None):
     for column in range(9):
         for level in levels or range(plan.deep):
             at = column * plan.deep + level
-            first, second, third = split(ring[at])
-            stacked = jnp.concatenate([first, second, third, jnp.zeros_like(third)], axis=0)
-            packed[:, pl.ds(at * LANES, LANES)] = stacked.astype(jnp.bfloat16)
+            packed[:, pl.ds(at * LANES, LANES)] = form[0](ring[at]).astype(jnp.bfloat16)
 
 
 def inner_span(plan, block):
@@ -181,13 +217,8 @@
     )
 
 
-def fold(total):
-    both = total[:, :LANES] + total[:, LANES:]
-    return both[0:8] + both[8:16] + both[16:24]
-
-
-def apply_tiles(plan, rims, tiles, outer, ring, packed, rows):
-    split_ring(plan, ring, packed)
+def apply_tiles(plan, rims, tiles, outer, ring, packed, rows, form):
+    split_ring(plan, ring, packed, form)
     for block in range(plan.blocks):
         low, number = inner_span(plan, block)
         base = inner_base(plan, block)
@@ -195,11 +226,11 @@
         for columns in groups_of(number):
             part = tile_sum(plan, tiles, base, packed, low, number, columns)
             total = part if total is None else total + part
-        rows[block] = fold(total)
-    add_rims(plan, rims, outer, packed, rows, lambda e, columns: None)
-
-
-def add_rims(plan, rims, outer, packed, rows, before):
+        rows[block] = form[1](total)
+    add_rims(plan, rims, outer, packed, rows, form, lambda e, columns: None)
+
+
+def add_rims(plan, rims, outer, packed, rows, form, before):
     for e, rim in enumerate(rims):
         total = None
         for columns in groups_of(1):
@@ -207,7 +238,7 @@
             base = e * 9 * plan.width
             part = tile_sum(plan, outer, base, packed, plan.blocks + e, 1, columns)
             total = part if total is None else total + part
-        rows[rim[1]] = rows[rim[1]] + fold(total)
+        rows[rim[1]] = rows[rim[1]] + form[1](total)
 
 
 def pack_kernel(plan, counts_in, offsets_in, velocity_in, send, counts, offsets, velocity, sems):
@@ -285,7 +316,7 @@
     levels = range(plan.blocks)
     place_ring(plan, rims_of(plan), [recv], levels, points, mixed, where, right)
     flip_points(plan, levels, points, flipped)
-    split_ring(plan, mixed, packed, levels)
+    split_ring(plan, mixed, packed, FULL, levels)
     sub = sublane_ids()
     for block in range(plan.blocks):
         own = points[plan.own(block)]
@@ -305,7 +336,7 @@
             weigh(plan, flipped, centre, low, number, columns, tiles, base)
             part = tile_sum(plan, tiles, base, packed, low, number, columns)
             total = part if total is None else total + part
-        partial[block] = fold(total)
+        partial[block] = fold_full(total)
 
 
 def edge_kernel(plan, *refs):
@@ -323,7 +354,7 @@
             where[at] = near_where[at]
             right[at] = near_right[at]
     flip_points(plan, levels, points, flipped)
-    split_ring(plan, mixed, packed, levels)
+    split_ring(plan, mixed, packed, FULL, levels)
     for block in range(plan.blocks):
         rows[block] = partial[block]
 
@@ -331,7 +362,7 @@
         centre = centres[rims[e][1]]
         weigh(plan, flipped, centre, plan.blocks + e, 1, columns, outer, e * 9 * plan.width)
 
-    add_rims(plan, rims, outer, packed, rows, before)
+    add_rims(plan, rims, outer, packed, rows, FULL, before)
     image = [[None] * plan.blocks for _ in range(3)]
     whole = [[None] * plan.blocks for _ in range(3)]
     start = [[None] * plan.blocks for _ in range(3)]
@@ -371,7 +402,7 @@
     scalars[plan.blocks] = alpha
     for block in range(plan.blocks):
         scalars[block] = image[plan.own(block)]
-    apply_tiles(plan, rims, tiles, outer, direction, packed, rows)
+    apply_tiles(plan, rims, tiles, outer, direction, packed, rows, THREE)
     out = []
     groups = [[], [], [], []]
     for axis in range(3):
@@ -422,7 +453,7 @@
         if at - plan.own(0) in range(plan.blocks):
             image[at] = rest
             sofar[at - plan.own(0)] = made
-    apply_tiles(plan, rims, tiles, outer, ahead, packed, rows)
+    apply_tiles(plan, rims, tiles, outer, ahead, packed, rows, FULL)
     scale = 1.0 / plan.unit
     base = []
     each = [[None] * plan.blocks for _ in range(3)]
@@ -465,7 +496,7 @@
     for at in range(plan.ring):
         gathered = jnp.where(sub < 4, parts[at] * factor, 0.0)
         source[at] = jnp.broadcast_to(-jnp.sum(gathered, axis=0, keepdims=True), (8, LANES))
-    apply_tiles(plan, rims, tiles, outer, source, packed, rows)
+    apply_tiles(plan, rims, tiles, outer, source, packed, rows, ONE)
     field, shot, whole = [], [], []
     for block in range(plan.blocks):
         field.append(source[plan.own(block), pl.ds(0, 1), :])
@@ -485,10 +516,10 @@
     beta = steps[pl.ds(0, 1), :]
     for at in range(plan.ring):
         field = source[at]
-        left = field - alpha * (STIFFNESS * field + image[at])
+        left = field - alpha * (STIFFNESS * field + image[at, pl.ds(0, 1), :])
         image[at] = left
         ahead[at] = left + beta * field
-    apply_tiles(plan, rims, tiles, outer, ahead, packed, rows)
+    apply_tiles(plan, rims, tiles, outer, ahead, packed, rows, ONE)
     rests, heads, wholes = [], [], []
     for block in range(plan.blocks):
         own = plan.own(block)
@@ -542,6 +573,7 @@
     tile = (8, width)
     rows = (blocks, 8, width)
     packed = ((32, plan.ring * width), jnp.bfloat16)
+    packed_low = ((16, plan.ring * width), jnp.bfloat16)
     (send,) = call(
         plan, pack_kernel,
         [
@@ -577,7 +609,7 @@
     send, residual, direction, scalars = call(
         plan, second_kernel, [recv, tiles, outer, right, state],
         [slot(3 * blocks + 1), ring, ring, (blocks + 1, 8, width)],
-        [ring, packed, rows],
+        [ring, packed_low, rows],
     )
     recv = exchange(send)
     send, speeds = call(
@@ -589,13 +621,13 @@
     send, source, final = call(
         plan, fourth_kernel, [recv, tiles, outer, state],
         [slot(blocks + 1), ring, tile],
-        [ring, packed, rows],
+        [ring, packed_low, rows],
     )
     recv = exchange(send)
     send, ends = call(
         plan, fifth_kernel, [recv, tiles, outer, source, state],
         [slot(1), (2 * blocks, width)],
-        [ring, ring, tile, packed, rows],
+        [ring, ring, tile, packed_low, rows],
     )
     recv = exchange(send)
     star, pressure = call(

time: 77.1 us -> 76.7 us (level)
  no operation moved by 1% of the time
where the time goes in v7:
time: 76.7 us; the launch traced here: 76.4 us
  blocking collectives  67 us (87%)
  Pallas kernels  8.67 us (11%)
    all_to_all x5, blocking collectives, exchange(): return lax.all_to_all(send, AXES, 0, 0, tiled=True)  50.8 us
    all_to_all x1, blocking collectives, exchange_layers(): level = lax.all_to_all(send, AXES[:2], 0, 0, tiled=True)  16.2 us
    pallas_call x8, Pallas kernels, call(): pl.pallas_call(functools.partial(kernel, plan), out_shape=[jax.ShapeDtype...  8.67 us
  transfers between devices with their start and end apart: 1, of which 0 were waited for; matrix products, arithmetic and copies ran while one was open for 0% of the time, Pallas kernels for 3%

profile of v7, /device:TPU:0, one launch (start us, length us, event | category | flops | bytes accessed | tf_op | source)
XLA Modules:
  0.0 76.4 jit_solution(15909931329583046674)
XLA Ops:
  0.6 0.8 %pack_kernel.1 = f32[16,18,1,128]{3,2,1,0:T(1,128)S(1)} custom-call(s32[1,3]{1,0:T(1,128)} %bitcast.11, f32[9,1,128]{2,1,0:T(1,128)} %bitcast.9, f32[9,1,128]{2,1,0:T(1,128)} %bitcast.10), custom_call_target="tpu_custom_call" | custom-call | tf_op jit(solution)/shard_map/pack_kernel/pallas_call | solution.py:555
  1.5 16.2 %all_to_all.30.recv = f32[16,18,1,128]{3,2,1,0:T(1,128)S(1)} all-to-all(f32[16,18,1,128]{3,2,1,0:T(1,128)S(1)} %pack_kernel.1), channel_id=1, replica_groups=mesh['gx'=4,'gy'=4,'gz'=2] {'gx','gy'}, dimensions={0} | all-to-all | bytes 294912 | tf_op jit(solution)/shard_map/all_to_all | solution.py:23
  17.7 0.0 collective-permute-start
  17.7 2.0 %inner_kernel.1 = (bf16[8064,256]{1,0:T(8,128)(2,1)S(1)}, f32[36,8,128]{2,1,0:T(8,128)S(1)}, f32[36,8,128]{2,1,0:T(8,128)S(1)}, bf16[3,48,128]{2,1,0:T(8,128)(2,1)S(1)}, f32[3,8,128]{2,1,0:T(8,128)S(1)}) custom-call(f32[16,18,1,128]{3,2,1,0:T(1,128)S(1)} %all_to_all.30.recv), custom_call_target="tpu_custom_call" | custom-call | tf_op jit(solution)/shard_map/inner_kernel/pallas_call | solution.py:555
  19.7 0.0 collective-permute-done.refs_0_
  19.7 1.0 %edge_kernel.1 = (f32[32,10,1,128]{3,2,1,0:T(1,128)S(1)}, bf16[1152,256]{1,0:T(8,128)(2,1)S(1)}, f32[36,8,128]{2,1,0:T(8,128)S(1)}, f32[36,8,128]{2,1,0:T(8,128)S(1)}, f32[12,128]{1,0:T(8,128)S(1)}) custom-call(f32[16,18,1,128]{3,2,1,0:T(1,128)S(1)} %collective-permute-done.refs_0_, f32[36,8,128]{2,1,0:T(8,128)S(1)} %get-tuple-element.25.refs_1_, ...), custom_call_target="tpu_custom_call" | custom-call | tf_op jit(solution)/shard_map/edge_kernel/pallas_call | solution.py:555
  20.7 10.2 %all_to_all.31.recv = f32[32,10,1,128]{3,2,1,0:T(1,128)S(1)} all-to-all(f32[32,10,1,128]{3,2,1,0:T(1,128)S(1)} %get-tuple-element.29), channel_id=1, replica_groups=mesh['gx'=4,'gy'=4,'gz'=2] {'gx','gy','gz'}, dimensions={0} | all-to-all | bytes 327680 | tf_op jit(solution)/shard_map/all_to_all | solution.py:19
  30.9 1.1 %second_kernel.1 = (f32[32,10,1,128]{3,2,1,0:T(1,128)S(1)}, f32[36,8,128]{2,1,0:T(8,128)S(1)}, f32[36,8,128]{2,1,0:T(8,128)S(1)}, f32[4,8,128]{2,1,0:T(8,128)S(1)}) custom-call(f32[32,10,1,128]{3,2,1,0:T(1,128)S(1)} %all_to_all.31.recv, bf16[8064,256]{1,0:T(8,128)(2,1)S(1)} %get-tuple-element.30.tiles, bf16[1152,256]{1,0:T(8,128)(2,1)S(1)} %get-tuple-element.31.outer, ...), custom_call_target="tpu_custom_call" | custom-call | tf_op jit(solution)/shard_map/second_kernel/pallas_call | solution.py:555
  31.9 10.6 %all_to_all.32.recv = f32[32,10,1,128]{3,2,1,0:T(1,128)S(1)} all-to-all(f32[32,10,1,128]{3,2,1,0:T(1,128)S(1)} %get-tuple-element.34), channel_id=1, replica_groups=mesh['gx'=4,'gy'=4,'gz'=2] {'gx','gy','gz'}, dimensions={0} | all-to-all | bytes 327680 | tf_op jit(solution)/shard_map/all_to_all | solution.py:19
  42.5 1.2 %third_kernel.1 = (f32[32,13,1,128]{3,2,1,0:T(1,128)S(1)}, f32[18,128]{1,0:T(8,128)S(1)}) custom-call(f32[32,10,1,128]{3,2,1,0:T(1,128)S(1)} %all_to_all.32.recv, bf16[8064,256]{1,0:T(8,128)(2,1)S(1)} %get-tuple-element.30.tiles, bf16[1152,256]{1,0:T(8,128)(2,1)S(1)} %get-tuple-element.31.outer, f32[36,8,128]{2,1,0:T(8,128)S(1)} %get-tuple-element.35.where, ...), custom_call_target="tpu_custom_call" | custom-call | tf_op jit(solution)/shard_map/third_kernel/pallas_call | solution.py:555
  43.7 11.1 %all_to_all.33.recv = f32[32,13,1,128]{3,2,1,0:T(1,128)S(1)} all-to-all(f32[32,13,1,128]{3,2,1,0:T(1,128)S(1)} %get-tuple-element.39), channel_id=1, replica_groups=mesh['gx'=4,'gy'=4,'gz'=2] {'gx','gy','gz'}, dimensions={0} | all-to-all | bytes 425984 | tf_op jit(solution)/shard_map/all_to_all | solution.py:19
  54.8 1.0 %fourth_kernel.1 = (f32[32,4,1,128]{3,2,1,0:T(1,128)S(1)}, f32[36,8,128]{2,1,0:T(8,128)S(1)}, f32[8,128]{1,0:T(8,128)S(1)}) custom-call(f32[32,13,1,128]{3,2,1,0:T(1,128)S(1)} %all_to_all.33.recv, bf16[8064,256]{1,0:T(8,128)(2,1)S(1)} %get-tuple-element.30.tiles, bf16[1152,256]{1,0:T(8,128)(2,1)S(1)} %get-tuple-element.31.outer, ...), custom_call_target="tpu_custom_call" | custom-call | tf_op jit(solution)/shard_map/fourth_kernel/pallas_call | solution.py:555
  55.8 10.1 %all_to_all.34.recv = f32[32,4,1,128]{3,2,1,0:T(1,128)S(1)} all-to-all(f32[32,4,1,128]{3,2,1,0:T(1,128)S(1)} %get-tuple-element.40), channel_id=1, replica_groups=mesh['gx'=4,'gy'=4,'gz'=2] {'gx','gy','gz'}, dimensions={0} | all-to-all | bytes 131072 | tf_op jit(solution)/shard_map/all_to_all | solution.py:19
  65.9 1.0 %fifth_kernel.1 = (f32[32,1,1,128]{3,2,1,0:T(1,128)S(1)}, f32[6,128]{1,0:T(8,128)S(1)}) custom-call(f32[32,4,1,128]{3,2,1,0:T(1,128)S(1)} %all_to_all.34.recv, bf16[8064,256]{1,0:T(8,128)(2,1)S(1)} %get-tuple-element.30.tiles, bf16[1152,256]{1,0:T(8,128)(2,1)S(1)} %get-tuple-element.31.outer, f32[36,8,128]{2,1,0:T(8,128)S(1)} %get-tuple-element.41.source, ...), custom_call_target="tpu_custom_call" | custom-call | tf_op jit(solution)/shard_map/fifth_kernel/pallas_call | solution.py:555
  66.8 8.8 %all_to_all.35.recv = f32[32,1,1,128]{3,2,1,0:T(1,128)S(1)} all-to-all(f32[32,1,1,128]{3,2,1,0:T(1,128)S(1)} %get-tuple-element.42), channel_id=1, replica_groups=mesh['gx'=4,'gy'=4,'gz'=2] {'gx','gy','gz'}, dimensions={0} | all-to-all | bytes 32768 | tf_op jit(solution)/shard_map/all_to_all | solution.py:19
  75.7 0.7 last_kernel.1
Async XLA Ops:
  17.7 2.0 %collective-permute-start = (f32[16,18,1,128]{3,2,1,0:T(1,128)S(1)}, f32[16,18,1,128]{3,2,1,0:T(1,128)S(1)}, u32[]{:S(2)}, u32[]{:S(2)}) collective-permute-start(f32[16,18,1,128]{3,2,1,0:T(1,128)S(1)} %all_to_all.30.recv), channel_id=1, source_target_pairs={{0,1},{1,0},{2,3},{3,2},{4,5},{5,4},{6,7},{7,6},{8,9},{9,8},{10,11... | collective-permute-start | bytes 442376 | tf_op jit(solution)/shard_map/ppermute | solution.py:26

commit v8 on v7

--- a/solution.py
+++ b/solution.py
@@ -73,6 +73,12 @@
     return found
 
 
+def take(recv, slot, row):
+    if recv.shape[2] == 1:
+        return recv[slot, row]
+    return recv[slot, row // 2, pl.ds(row % 2, 1), :]
+
+
 def gather_ring(plan, rims, found, layers, fields, store, levels=None):
     for column in range(9):
         for level in levels or range(plan.deep):
@@ -81,7 +87,8 @@
                 layer = level - plan.blocks + 1
                 block, depth = rims[layer - 1][2:]
             slot, present = found[column][layer]
-            rows = [layers[layer][slot, field * plan.blocks + block] for field in range(fields)]
+            got = layers[layer]
+            rows = [take(got, slot, field * plan.blocks + block) for field in range(fields)]
             store(column * plan.deep + level, column, depth, rows, present)
 
 
@@ -102,7 +109,7 @@
 
 
 def totals(recv, row, number):
-    summed = jnp.broadcast_to(jnp.sum(recv[:, row], axis=0), (8, LANES))
+    summed = jnp.broadcast_to(jnp.sum(take(recv, slice(None), row), axis=0), (8, LANES))
     place = lane_ids(8) - sublane_ids()
     return [
         jnp.broadcast_to(
@@ -129,6 +136,9 @@
 
 
 def spread(send, rows):
+    size = send.shape[2]
+    rows = [jnp.concatenate(rows[r : r + size], axis=0) for r in range(0, len(rows), size)]
+
     def body(slot, carry):
         for r, row in enumerate(rows):
             send[slot, r] = row
@@ -265,34 +275,39 @@
     spread(send, rows)
 
 
-def place_ring(plan, rims, layers, levels, points, mixed, where, right):
+def place_ring(plan, rims, layers, levels, mixed):
+    blank = jnp.where(sublane_ids() == 3, 1.0, 0.0)
+
     def store(at, column, depth, got, present):
         shift = (column // 3 - 1, column % 3 - 1, depth - (plan.blocks - 1) // 2)
         spots = [
             plan.unit * (got[axis] + jnp.asarray(shift[axis], jnp.float32)) for axis in range(3)
         ]
         spots[0] = jnp.where(present, spots[0], FAR)
-        points[at, pl.ds(3, 1), :] = spots[0] * spots[0] + spots[1] * spots[1] + spots[2] * spots[2]
-        points[at, pl.ds(4, 1), :] = jnp.ones((1, LANES), jnp.float32)
-        points[at, pl.ds(5, 3), :] = jnp.zeros((3, LANES), jnp.float32)
-        mixed[at, pl.ds(3, 1), :] = jnp.ones((1, LANES), jnp.float32)
-        mixed[at, pl.ds(7, 1), :] = jnp.zeros((1, LANES), jnp.float32)
+        mixed[at] = blank
         for axis in range(3):
-            points[at, pl.ds(axis, 1), :] = spots[axis]
-            where[at, pl.ds(axis, 1), :] = spots[axis]
+            mixed[at, pl.ds(axis, 1), :] = jnp.where(present, got[3 + axis], 0.0)
             mixed[at, pl.ds(4 + axis, 1), :] = spots[axis]
-            field = jnp.where(present, got[3 + axis], 0.0)
-            right[at, pl.ds(axis, 1), :] = field
-            mixed[at, pl.ds(axis, 1), :] = field
 
     gather_ring(plan, rims, slots(plan, rims, 2), layers, 6, store, levels)
 
 
-def flip_points(plan, levels, points, flipped):
+def spot_of(tile):
+    return pltpu.roll(tile, 4, 0)
+
+
+def point_of(tile):
+    sub = sublane_ids()
+    spot = jnp.where(sub < 3, spot_of(tile), 0.0)
+    square = jnp.sum(spot * spot, axis=0, keepdims=True)
+    return jnp.where(sub == 3, square, jnp.where(sub == 4, 1.0, spot))
+
+
+def flip_points(plan, levels, mixed, flipped):
     for column in range(9):
         for level in levels:
             at = column * plan.deep + level
-            first, second, third = split(points[at])
+            first, second, third = split(point_of(mixed[at]))
             stacked = jnp.concatenate([first, second, third, first, second, first], axis=0)
             flipped[pl.ds(at * plan.width, plan.width), :] = jnp.transpose(stacked).astype(jnp.bfloat16)
 
@@ -312,14 +327,14 @@
         tiles[spot, pl.ds(LANES, LANES)] = (weight - high.astype(jnp.float32)).astype(jnp.bfloat16)
 
 
-def inner_kernel(plan, recv, tiles, where, right, centres, partial, points, flipped, mixed, packed):
+def inner_kernel(plan, recv, tiles, mixed, centres, partial, flipped, packed):
     levels = range(plan.blocks)
-    place_ring(plan, rims_of(plan), [recv], levels, points, mixed, where, right)
-    flip_points(plan, levels, points, flipped)
+    place_ring(plan, rims_of(plan), [recv], levels, mixed)
+    flip_points(plan, levels, mixed, flipped)
     split_ring(plan, mixed, packed, FULL, levels)
     sub = sublane_ids()
     for block in range(plan.blocks):
-        own = points[plan.own(block)]
+        own = point_of(mixed[plan.own(block)])
         own = jnp.where(jnp.logical_and(sub == 0, own > 0.25 * FAR), -FAR, own)
         square = jnp.broadcast_to(own[3:4], (8, LANES))
         own = jnp.where(sub < 3, 2.0 * own, 0.0)
@@ -340,20 +355,16 @@
 
 
 def edge_kernel(plan, *refs):
-    others = refs[:-14]
-    (
-        near_where, near_right, centres, partial,
-        send, outer, where, right, state, points, flipped, mixed, packed, rows,
-    ) = refs[-14:]
+    others = refs[:-10]
+    near, centres, partial, send, outer, mixed, state, flipped, packed, rows = refs[-10:]
     rims = rims_of(plan)
     levels = range(plan.blocks, plan.deep)
-    place_ring(plan, rims, [None, *others], levels, points, mixed, where, right)
+    place_ring(plan, rims, [None, *others], levels, mixed)
     for column in range(9):
         for level in range(plan.blocks):
             at = column * plan.deep + level
-            where[at] = near_where[at]
-            right[at] = near_right[at]
-    flip_points(plan, levels, points, flipped)
+            mixed[at] = near[at]
+    flip_points(plan, levels, mixed, flipped)
     split_ring(plan, mixed, packed, FULL, levels)
     for block in range(plan.blocks):
         rows[block] = partial[block]
@@ -371,11 +382,11 @@
         reach = rows[block, pl.ds(3, 1), :]
         state[pl.ds(block, 1), :] = reach
         for axis in range(3):
-            field = right[own, pl.ds(axis, 1), :]
+            field = mixed[own, pl.ds(axis, 1), :]
             start[axis][block] = field
             image[axis][block] = reach * field - rows[block, pl.ds(axis, 1), :]
             whole[axis][block] = field + VISCOUS * image[axis][block]
-            spot = where[own, pl.ds(axis, 1), :]
+            spot = mixed[own, pl.ds(4 + axis, 1), :]
             state[pl.ds((1 + axis) * plan.blocks + block, 1), :] = (
                 reach * spot - rows[block, pl.ds(4 + axis, 1), :]
             )
@@ -387,7 +398,7 @@
     spread(send, sum(image, []) + [pack(groups)])
 
 
-def second_kernel(plan, recv, tiles, outer, right, state, send, residual, direction, scalars, image, packed, rows):
+def second_kernel(plan, recv, tiles, outer, mixed, state, send, residual, direction, scalars, image, packed, rows):
     rims = rims_of(plan)
     ring_into(plan, rims, recv, 3, image)
     current, curve, square = totals(recv, 3 * plan.blocks, 3)
@@ -395,7 +406,7 @@
     following = jnp.maximum(alpha * alpha * square - current, 0.0)
     beta = following / current
     for at in range(plan.ring):
-        field = right[at]
+        field = mixed[at]
         left = field - alpha * (field + VISCOUS * image[at])
         residual[at] = left
         direction[at] = left + beta * field
@@ -422,7 +433,7 @@
 
 
 def third_kernel(
-    plan, recv, tiles, outer, where, right, residual, direction, state, scalars,
+    plan, recv, tiles, outer, mixed, residual, direction, state, scalars,
     send, ends, image, sofar, ahead, steps, packed, rows,
 ):
     rims = rims_of(plan)
@@ -444,8 +455,8 @@
         field = direction[at]
         rest = residual[at] - alpha * (field + VISCOUS * image[at])
         fresh = rest + beta * field
-        spot = where[at]
-        made = first * right[at] + alpha * field
+        spot = spot_of(mixed[at])
+        made = first * mixed[at] + alpha * field
         moved = made * spot
         moved = pltpu.roll(moved, 6, 0) + pltpu.roll(moved, 5, 0) + pltpu.roll(moved, 4, 0)
         joined = jnp.where(sub < 3, fresh, pltpu.roll(fresh * spot, 3, 0))
@@ -466,7 +477,7 @@
         total = rows[block, pl.ds(6, 1), :] - reach * ahead[own, pl.ds(6, 1), :]
         for axis in range(3):
             head = ahead[own, pl.ds(axis, 1), :]
-            spot = where[own, pl.ds(axis, 1), :]
+            spot = mixed[own, pl.ds(4 + axis, 1), :]
             lean = state[pl.ds((1 + axis) * plan.blocks + block, 1), :]
             shot = reach * head - rows[block, pl.ds(axis, 1), :]
             twice = reach * ahead[own, pl.ds(3 + axis, 1), :] - rows[block, pl.ds(3 + axis, 1), :]
@@ -568,7 +579,8 @@
     width = offsets.shape[-1]
     plan = Plan(mesh, blocks, width)
     lined = lambda field: field.transpose(0, 1, 3, 2, 4).reshape(3 * blocks, 1, width)
-    slot = lambda rows: (plan.devices, rows, 1, width)
+    paired = lambda rows: (rows // 2, 2, width) if rows % 2 == 0 else (rows, 1, width)
+    slot = lambda rows: (plan.devices, *paired(rows))
     ring = (plan.ring, 8, width)
     tile = (8, width)
     rows = (blocks, 8, width)
@@ -580,7 +592,7 @@
             pltpu.with_memory_space_constraint(field, pltpu.HBM)
             for field in (counts.reshape(1, blocks), lined(offsets), lined(velocity))
         ],
-        [(plan.count[0] * plan.count[1], 6 * blocks, 1, width)],
+        [(plan.count[0] * plan.count[1], *paired(6 * blocks))],
         [
             pltpu.SMEM((1, blocks), jnp.int32), (3 * blocks, 1, width), (3 * blocks, 1, width),
             pltpu.SemaphoreType.DMA((3,)),
@@ -589,31 +601,31 @@
     )
     level, *others = exchange_layers(plan, send)
     flipped = ((plan.ring * width, 48), jnp.bfloat16)
-    tiles, where, right, centres, partial = call(
+    tiles, mixed, centres, partial = call(
         plan, inner_kernel, [level],
         [
-            ((inner_base(plan, blocks), 2 * width), jnp.bfloat16), ring, ring,
+            ((inner_base(plan, blocks), 2 * width), jnp.bfloat16), ring,
             ((blocks, 48, width), jnp.bfloat16), rows,
         ],
-        [ring, flipped, ring, packed],
-    )
-    send, outer, where, right, state = call(
-        plan, edge_kernel, [*others, where, right, centres, partial],
+        [flipped, packed],
+    )
+    send, outer, mixed, state = call(
+        plan, edge_kernel, [*others, mixed, centres, partial],
         [
             slot(3 * blocks + 1), ((plan.rims * 9 * width, 2 * width), jnp.bfloat16),
-            ring, ring, (4 * blocks, width),
+            ring, (4 * blocks, width),
         ],
-        [ring, flipped, ring, packed, rows],
+        [flipped, packed, rows],
     )
     recv = exchange(send)
     send, residual, direction, scalars = call(
-        plan, second_kernel, [recv, tiles, outer, right, state],
+        plan, second_kernel, [recv, tiles, outer, mixed, state],
         [slot(3 * blocks + 1), ring, ring, (blocks + 1, 8, width)],
         [ring, packed_low, rows],
     )
     recv = exchange(send)
     send, speeds = call(
-        plan, third_kernel, [recv, tiles, outer, where, right, residual, direction, state, scalars],
+        plan, third_kernel, [recv, tiles, outer, mixed, residual, direction, state, scalars],
         [slot(4 * blocks + 1), (6 * blocks, width)],
         [ring, rows, ring, tile, packed, rows],
     )

time: 76.7 us -> 76.6 us (level)
  no operation moved by 1% of the time
where the time goes in v8:
time: 76.6 us; the launch traced here: 76.3 us
  blocking collectives  67 us (87%)
  Pallas kernels  8.59 us (11%)
    all_to_all x5, blocking collectives, exchange(): return lax.all_to_all(send, AXES, 0, 0, tiled=True)  50.8 us
    all_to_all x1, blocking collectives, exchange_layers(): level = lax.all_to_all(send, AXES[:2], 0, 0, tiled=True)  16.2 us
    pallas_call x8, Pallas kernels, call(): pl.pallas_call(functools.partial(kernel, plan), out_shape=[jax.ShapeDtype...  8.59 us
  transfers between devices with their start and end apart: 1, of which 0 were waited for; matrix products, arithmetic and copies ran while one was open for 0% of the time, Pallas kernels for 3%

profile of v8, /device:TPU:0, one launch (start us, length us, event | category | flops | bytes accessed | tf_op | source)
XLA Modules:
  0.0 76.3 jit_solution(17885653389340523874)
XLA Ops:
  0.6 0.8 %pack_kernel.1 = f32[16,9,2,128]{3,2,1,0:T(2,128)S(1)} custom-call(s32[1,3]{1,0:T(1,128)} %bitcast.11, f32[9,1,128]{2,1,0:T(1,128)} %bitcast.9, f32[9,1,128]{2,1,0:T(1,128)} %bitcast.10), custom_call_target="tpu_custom_call" | custom-call | tf_op jit(solution)/shard_map/pack_kernel/pallas_call | solution.py:566
  1.4 16.2 %all_to_all.30.recv = f32[16,9,2,128]{3,2,1,0:T(2,128)S(1)} all-to-all(f32[16,9,2,128]{3,2,1,0:T(2,128)S(1)} %pack_kernel.1), channel_id=1, replica_groups=mesh['gx'=4,'gy'=4,'gz'=2] {'gx','gy'}, dimensions={0} | all-to-all | bytes 294912 | tf_op jit(solution)/shard_map/all_to_all | solution.py:23
  17.7 0.0 collective-permute-start
  17.7 2.0 %inner_kernel.1 = (bf16[8064,256]{1,0:T(8,128)(2,1)S(1)}, f32[36,8,128]{2,1,0:T(8,128)S(1)}, bf16[3,48,128]{2,1,0:T(8,128)(2,1)S(1)}, f32[3,8,128]{2,1,0:T(8,128)S(1)}) custom-call(f32[16,9,2,128]{3,2,1,0:T(2,128)S(1)} %all_to_all.30.recv), custom_call_target="tpu_custom_call" | custom-call | tf_op jit(solution)/shard_map/inner_kernel/pallas_call | solution.py:566
  19.6 0.0 collective-permute-done.refs_0_
  19.6 1.0 %edge_kernel.1 = (f32[32,5,2,128]{3,2,1,0:T(2,128)S(1)}, bf16[1152,256]{1,0:T(8,128)(2,1)S(1)}, f32[36,8,128]{2,1,0:T(8,128)S(1)}, f32[12,128]{1,0:T(8,128)S(1)}) custom-call(f32[16,9,2,128]{3,2,1,0:T(2,128)S(1)} %collective-permute-done.refs_0_, f32[36,8,128]{2,1,0:T(8,128)S(1)} %get-tuple-element.23.refs_1_, ...), custom_call_target="tpu_custom_call" | custom-call | tf_op jit(solution)/shard_map/edge_kernel/pallas_call | solution.py:566
  20.6 10.2 %all_to_all.31.recv = f32[32,5,2,128]{3,2,1,0:T(2,128)S(1)} all-to-all(f32[32,5,2,128]{3,2,1,0:T(2,128)S(1)} %get-tuple-element.26), channel_id=1, replica_groups=mesh['gx'=4,'gy'=4,'gz'=2] {'gx','gy','gz'}, dimensions={0} | all-to-all | bytes 327680 | tf_op jit(solution)/shard_map/all_to_all | solution.py:19
  30.8 1.0 %second_kernel.1 = (f32[32,5,2,128]{3,2,1,0:T(2,128)S(1)}, f32[36,8,128]{2,1,0:T(8,128)S(1)}, f32[36,8,128]{2,1,0:T(8,128)S(1)}, f32[4,8,128]{2,1,0:T(8,128)S(1)}) custom-call(f32[32,5,2,128]{3,2,1,0:T(2,128)S(1)} %all_to_all.31.recv, bf16[8064,256]{1,0:T(8,128)(2,1)S(1)} %get-tuple-element.27.tiles, bf16[1152,256]{1,0:T(8,128)(2,1)S(1)} %get-tuple-element.28.outer, ...), custom_call_target="tpu_custom_call" | custom-call | tf_op jit(solution)/shard_map/second_kernel/pallas_call | solution.py:566
  31.9 10.6 %all_to_all.32.recv = f32[32,5,2,128]{3,2,1,0:T(2,128)S(1)} all-to-all(f32[32,5,2,128]{3,2,1,0:T(2,128)S(1)} %get-tuple-element.31), channel_id=1, replica_groups=mesh['gx'=4,'gy'=4,'gz'=2] {'gx','gy','gz'}, dimensions={0} | all-to-all | bytes 327680 | tf_op jit(solution)/shard_map/all_to_all | solution.py:19
  42.4 1.2 %third_kernel.1 = (f32[32,13,1,128]{3,2,1,0:T(1,128)S(1)}, f32[18,128]{1,0:T(8,128)S(1)}) custom-call(f32[32,5,2,128]{3,2,1,0:T(2,128)S(1)} %all_to_all.32.recv, bf16[8064,256]{1,0:T(8,128)(2,1)S(1)} %get-tuple-element.27.tiles, bf16[1152,256]{1,0:T(8,128)(2,1)S(1)} %get-tuple-element.28.outer, f32[36,8,128]{2,1,0:T(8,128)S(1)} %get-tuple-element.29.mixed, ...), custom_call_target="tpu_custom_call" | custom-call | tf_op jit(solution)/shard_map/third_kernel/pallas_call | solution.py:566
  43.6 11.1 %all_to_all.33.recv = f32[32,13,1,128]{3,2,1,0:T(1,128)S(1)} all-to-all(f32[32,13,1,128]{3,2,1,0:T(1,128)S(1)} %get-tuple-element.35), channel_id=1, replica_groups=mesh['gx'=4,'gy'=4,'gz'=2] {'gx','gy','gz'}, dimensions={0} | all-to-all | bytes 425984 | tf_op jit(solution)/shard_map/all_to_all | solution.py:19
  54.7 1.0 %fourth_kernel.1 = (f32[32,2,2,128]{3,2,1,0:T(2,128)S(1)}, f32[36,8,128]{2,1,0:T(8,128)S(1)}, f32[8,128]{1,0:T(8,128)S(1)}) custom-call(f32[32,13,1,128]{3,2,1,0:T(1,128)S(1)} %all_to_all.33.recv, bf16[8064,256]{1,0:T(8,128)(2,1)S(1)} %get-tuple-element.27.tiles, bf16[1152,256]{1,0:T(8,128)(2,1)S(1)} %get-tuple-element.28.outer, ...), custom_call_target="tpu_custom_call" | custom-call | tf_op jit(solution)/shard_map/fourth_kernel/pallas_call | solution.py:566
  55.7 10.1 %all_to_all.34.recv = f32[32,2,2,128]{3,2,1,0:T(2,128)S(1)} all-to-all(f32[32,2,2,128]{3,2,1,0:T(2,128)S(1)} %get-tuple-element.36), channel_id=1, replica_groups=mesh['gx'=4,'gy'=4,'gz'=2] {'gx','gy','gz'}, dimensions={0} | all-to-all | bytes 131072 | tf_op jit(solution)/shard_map/all_to_all | solution.py:19
  65.8 1.0 %fifth_kernel.1 = (f32[32,1,1,128]{3,2,1,0:T(1,128)S(1)}, f32[6,128]{1,0:T(8,128)S(1)}) custom-call(f32[32,2,2,128]{3,2,1,0:T(2,128)S(1)} %all_to_all.34.recv, bf16[8064,256]{1,0:T(8,128)(2,1)S(1)} %get-tuple-element.27.tiles, bf16[1152,256]{1,0:T(8,128)(2,1)S(1)} %get-tuple-element.28.outer, f32[36,8,128]{2,1,0:T(8,128)S(1)} %get-tuple-element.37.source, ...), custom_call_target="tpu_custom_call" | custom-call | tf_op jit(solution)/shard_map/fifth_kernel/pallas_call | solution.py:566
  66.8 8.8 %all_to_all.35.recv = f32[32,1,1,128]{3,2,1,0:T(1,128)S(1)} all-to-all(f32[32,1,1,128]{3,2,1,0:T(1,128)S(1)} %get-tuple-element.38), channel_id=1, replica_groups=mesh['gx'=4,'gy'=4,'gz'=2] {'gx','gy','gz'}, dimensions={0} | all-to-all | bytes 32768 | tf_op jit(solution)/shard_map/all_to_all | solution.py:19
  75.6 0.7 last_kernel.1
Async XLA Ops:
  17.7 2.0 %collective-permute-start = (f32[16,9,2,128]{3,2,1,0:T(2,128)S(1)}, f32[16,9,2,128]{3,2,1,0:T(2,128)S(1)}, u32[]{:S(2)}, u32[]{:S(2)}) collective-permute-start(f32[16,9,2,128]{3,2,1,0:T(2,128)S(1)} %all_to_all.30.recv), channel_id=1, source_target_pairs={{0,1},{1,0},{2,3},{3,2},{4,5},{5,4},{6,7},{7,6},{8,9},{9,8},{10,11... | collective-permute-start | bytes 442376 | tf_op jit(solution)/shard_map/ppermute | solution.py:26

commit v9 on v8

--- a/solution.py
+++ b/solution.py
@@ -213,7 +213,7 @@
 
 
 def groups_of(number):
-    size = 3 if number % 2 == 0 else 4 if number == 1 else 2
+    size = 3 if number % 2 == 0 else 9 if number == 1 else 2
     return [range(c, min(c + size, 9)) for c in range(0, 9, size)]
 
 

time: 76.6 us -> 76.4 us (level)
  no operation moved by 1% of the time
where the time goes in v9:
time: 76.4 us; the launch traced here: 76.2 us
  blocking collectives  67 us (88%)
  Pallas kernels  8.45 us (11%)
    all_to_all x5, blocking collectives, exchange(): return lax.all_to_all(send, AXES, 0, 0, tiled=True)  50.8 us
    all_to_all x1, blocking collectives, exchange_layers(): level = lax.all_to_all(send, AXES[:2], 0, 0, tiled=True)  16.2 us
    pallas_call x8, Pallas kernels, call(): pl.pallas_call(functools.partial(kernel, plan), out_shape=[jax.ShapeDtype...  8.45 us
  transfers between devices with their start and end apart: 1, of which 0 were waited for; matrix products, arithmetic and copies ran while one was open for 0% of the time, Pallas kernels for 3%

profile of v9, /device:TPU:0, one launch (start us, length us, event | category | flops | bytes accessed | tf_op | source)
XLA Modules:
  0.0 76.2 jit_solution(8096492845162361771)
XLA Ops:
  0.6 0.8 %pack_kernel.1 = f32[16,9,2,128]{3,2,1,0:T(2,128)S(1)} custom-call(s32[1,3]{1,0:T(1,128)} %bitcast.11, f32[9,1,128]{2,1,0:T(1,128)} %bitcast.9, f32[9,1,128]{2,1,0:T(1,128)} %bitcast.10), custom_call_target="tpu_custom_call" | custom-call | tf_op jit(solution)/shard_map/pack_kernel/pallas_call | solution.py:566
  1.4 16.2 %all_to_all.30.recv = f32[16,9,2,128]{3,2,1,0:T(2,128)S(1)} all-to-all(f32[16,9,2,128]{3,2,1,0:T(2,128)S(1)} %pack_kernel.1), channel_id=1, replica_groups=mesh['gx'=4,'gy'=4,'gz'=2] {'gx','gy'}, dimensions={0} | all-to-all | bytes 294912 | tf_op jit(solution)/shard_map/all_to_all | solution.py:23
  17.7 0.0 collective-permute-start
  17.7 2.0 %inner_kernel.1 = (bf16[8064,256]{1,0:T(8,128)(2,1)S(1)}, f32[36,8,128]{2,1,0:T(8,128)S(1)}, bf16[3,48,128]{2,1,0:T(8,128)(2,1)S(1)}, f32[3,8,128]{2,1,0:T(8,128)S(1)}) custom-call(f32[16,9,2,128]{3,2,1,0:T(2,128)S(1)} %all_to_all.30.recv), custom_call_target="tpu_custom_call" | custom-call | tf_op jit(solution)/shard_map/inner_kernel/pallas_call | solution.py:566
  19.6 0.0 collective-permute-done.refs_0_
  19.6 0.8 %edge_kernel.1 = (f32[32,5,2,128]{3,2,1,0:T(2,128)S(1)}, bf16[1152,256]{1,0:T(8,128)(2,1)S(1)}, f32[36,8,128]{2,1,0:T(8,128)S(1)}, f32[12,128]{1,0:T(8,128)S(1)}) custom-call(f32[16,9,2,128]{3,2,1,0:T(2,128)S(1)} %collective-permute-done.refs_0_, f32[36,8,128]{2,1,0:T(8,128)S(1)} %get-tuple-element.23.refs_1_, ...), custom_call_target="tpu_custom_call" | custom-call | tf_op jit(solution)/shard_map/edge_kernel/pallas_call | solution.py:566
  20.5 10.2 %all_to_all.31.recv = f32[32,5,2,128]{3,2,1,0:T(2,128)S(1)} all-to-all(f32[32,5,2,128]{3,2,1,0:T(2,128)S(1)} %get-tuple-element.26), channel_id=1, replica_groups=mesh['gx'=4,'gy'=4,'gz'=2] {'gx','gy','gz'}, dimensions={0} | all-to-all | bytes 327680 | tf_op jit(solution)/shard_map/all_to_all | solution.py:19
  30.7 1.0 %second_kernel.1 = (f32[32,5,2,128]{3,2,1,0:T(2,128)S(1)}, f32[36,8,128]{2,1,0:T(8,128)S(1)}, f32[36,8,128]{2,1,0:T(8,128)S(1)}, f32[4,8,128]{2,1,0:T(8,128)S(1)}) custom-call(f32[32,5,2,128]{3,2,1,0:T(2,128)S(1)} %all_to_all.31.recv, bf16[8064,256]{1,0:T(8,128)(2,1)S(1)} %get-tuple-element.27.tiles, bf16[1152,256]{1,0:T(8,128)(2,1)S(1)} %get-tuple-element.28.outer, ...), custom_call_target="tpu_custom_call" | custom-call | tf_op jit(solution)/shard_map/second_kernel/pallas_call | solution.py:566
  31.7 10.6 %all_to_all.32.recv = f32[32,5,2,128]{3,2,1,0:T(2,128)S(1)} all-to-all(f32[32,5,2,128]{3,2,1,0:T(2,128)S(1)} %get-tuple-element.31), channel_id=1, replica_groups=mesh['gx'=4,'gy'=4,'gz'=2] {'gx','gy','gz'}, dimensions={0} | all-to-all | bytes 327680 | tf_op jit(solution)/shard_map/all_to_all | solution.py:19
  42.3 1.2 %third_kernel.1 = (f32[32,13,1,128]{3,2,1,0:T(1,128)S(1)}, f32[18,128]{1,0:T(8,128)S(1)}) custom-call(f32[32,5,2,128]{3,2,1,0:T(2,128)S(1)} %all_to_all.32.recv, bf16[8064,256]{1,0:T(8,128)(2,1)S(1)} %get-tuple-element.27.tiles, bf16[1152,256]{1,0:T(8,128)(2,1)S(1)} %get-tuple-element.28.outer, f32[36,8,128]{2,1,0:T(8,128)S(1)} %get-tuple-element.29.mixed, ...), custom_call_target="tpu_custom_call" | custom-call | tf_op jit(solution)/shard_map/third_kernel/pallas_call | solution.py:566
  43.5 11.1 %all_to_all.33.recv = f32[32,13,1,128]{3,2,1,0:T(1,128)S(1)} all-to-all(f32[32,13,1,128]{3,2,1,0:T(1,128)S(1)} %get-tuple-element.35), channel_id=1, replica_groups=mesh['gx'=4,'gy'=4,'gz'=2] {'gx','gy','gz'}, dimensions={0} | all-to-all | bytes 425984 | tf_op jit(solution)/shard_map/all_to_all | solution.py:19
  54.6 1.0 %fourth_kernel.1 = (f32[32,2,2,128]{3,2,1,0:T(2,128)S(1)}, f32[36,8,128]{2,1,0:T(8,128)S(1)}, f32[8,128]{1,0:T(8,128)S(1)}) custom-call(f32[32,13,1,128]{3,2,1,0:T(1,128)S(1)} %all_to_all.33.recv, bf16[8064,256]{1,0:T(8,128)(2,1)S(1)} %get-tuple-element.27.tiles, bf16[1152,256]{1,0:T(8,128)(2,1)S(1)} %get-tuple-element.28.outer, ...), custom_call_target="tpu_custom_call" | custom-call | tf_op jit(solution)/shard_map/fourth_kernel/pallas_call | solution.py:566
  55.6 10.1 %all_to_all.34.recv = f32[32,2,2,128]{3,2,1,0:T(2,128)S(1)} all-to-all(f32[32,2,2,128]{3,2,1,0:T(2,128)S(1)} %get-tuple-element.36), channel_id=1, replica_groups=mesh['gx'=4,'gy'=4,'gz'=2] {'gx','gy','gz'}, dimensions={0} | all-to-all | bytes 131072 | tf_op jit(solution)/shard_map/all_to_all | solution.py:19
  65.7 1.0 %fifth_kernel.1 = (f32[32,1,1,128]{3,2,1,0:T(1,128)S(1)}, f32[6,128]{1,0:T(8,128)S(1)}) custom-call(f32[32,2,2,128]{3,2,1,0:T(2,128)S(1)} %all_to_all.34.recv, bf16[8064,256]{1,0:T(8,128)(2,1)S(1)} %get-tuple-element.27.tiles, bf16[1152,256]{1,0:T(8,128)(2,1)S(1)} %get-tuple-element.28.outer, f32[36,8,128]{2,1,0:T(8,128)S(1)} %get-tuple-element.37.source, ...), custom_call_target="tpu_custom_call" | custom-call | tf_op jit(solution)/shard_map/fifth_kernel/pallas_call | solution.py:566
  66.6 8.8 %all_to_all.35.recv = f32[32,1,1,128]{3,2,1,0:T(1,128)S(1)} all-to-all(f32[32,1,1,128]{3,2,1,0:T(1,128)S(1)} %get-tuple-element.38), channel_id=1, replica_groups=mesh['gx'=4,'gy'=4,'gz'=2] {'gx','gy','gz'}, dimensions={0} | all-to-all | bytes 32768 | tf_op jit(solution)/shard_map/all_to_all | solution.py:19
  75.5 0.7 last_kernel.1
Async XLA Ops:
  17.7 2.0 %collective-permute-start = (f32[16,9,2,128]{3,2,1,0:T(2,128)S(1)}, f32[16,9,2,128]{3,2,1,0:T(2,128)S(1)}, u32[]{:S(2)}, u32[]{:S(2)}) collective-permute-start(f32[16,9,2,128]{3,2,1,0:T(2,128)S(1)} %all_to_all.30.recv), channel_id=1, source_target_pairs={{0,1},{1,0},{2,3},{3,2},{4,5},{5,4},{6,7},{7,6},{8,9},{9,8},{10,11... | collective-permute-start | bytes 442376 | tf_op jit(solution)/shard_map/ppermute | solution.py:26

commit v10 on v9

--- a/solution.py
+++ b/solution.py
@@ -144,7 +144,7 @@
             send[slot, r] = row
         return carry
 
-    lax.fori_loop(0, send.shape[0], body, 0, unroll=4)
+    lax.fori_loop(0, send.shape[0], body, 0, unroll=16)
 
 
 def coarse(value):

time: 76.4 us -> 76.4 us (level)
  no operation moved by 1% of the time
where the time goes in v10:
time: 76.4 us; the launch traced here: 76.1 us
  blocking collectives  67 us (88%)
  Pallas kernels  8.37 us (11%)
    all_to_all x5, blocking collectives, exchange(): return lax.all_to_all(send, AXES, 0, 0, tiled=True)  50.8 us
    all_to_all x1, blocking collectives, exchange_layers(): level = lax.all_to_all(send, AXES[:2], 0, 0, tiled=True)  16.2 us
    pallas_call x8, Pallas kernels, call(): pl.pallas_call(functools.partial(kernel, plan), out_shape=[jax.ShapeDtype...  8.37 us
  transfers between devices with their start and end apart: 1, of which 0 were waited for; matrix products, arithmetic and copies ran while one was open for 0% of the time, Pallas kernels for 3%

profile of v10, /device:TPU:0, one launch (start us, length us, event | category | flops | bytes accessed | tf_op | source)
XLA Modules:
  0.0 76.1 jit_solution(2462930021788772954)
XLA Ops:
  0.6 0.8 %pack_kernel.1 = f32[16,9,2,128]{3,2,1,0:T(2,128)S(1)} custom-call(s32[1,3]{1,0:T(1,128)} %bitcast.11, f32[9,1,128]{2,1,0:T(1,128)} %bitcast.9, f32[9,1,128]{2,1,0:T(1,128)} %bitcast.10), custom_call_target="tpu_custom_call" | custom-call | tf_op jit(solution)/shard_map/pack_kernel/pallas_call | solution.py:566
  1.4 16.2 %all_to_all.30.recv = f32[16,9,2,128]{3,2,1,0:T(2,128)S(1)} all-to-all(f32[16,9,2,128]{3,2,1,0:T(2,128)S(1)} %pack_kernel.1), channel_id=1, replica_groups=mesh['gx'=4,'gy'=4,'gz'=2] {'gx','gy'}, dimensions={0} | all-to-all | bytes 294912 | tf_op jit(solution)/shard_map/all_to_all | solution.py:23
  17.6 0.0 collective-permute-start
  17.7 2.0 %inner_kernel.1 = (bf16[8064,256]{1,0:T(8,128)(2,1)S(1)}, f32[36,8,128]{2,1,0:T(8,128)S(1)}, bf16[3,48,128]{2,1,0:T(8,128)(2,1)S(1)}, f32[3,8,128]{2,1,0:T(8,128)S(1)}) custom-call(f32[16,9,2,128]{3,2,1,0:T(2,128)S(1)} %all_to_all.30.recv), custom_call_target="tpu_custom_call" | custom-call | tf_op jit(solution)/shard_map/inner_kernel/pallas_call | solution.py:566
  19.6 0.0 collective-permute-done.refs_0_
  19.6 0.8 %edge_kernel.1 = (f32[32,5,2,128]{3,2,1,0:T(2,128)S(1)}, bf16[1152,256]{1,0:T(8,128)(2,1)S(1)}, f32[36,8,128]{2,1,0:T(8,128)S(1)}, f32[12,128]{1,0:T(8,128)S(1)}) custom-call(f32[16,9,2,128]{3,2,1,0:T(2,128)S(1)} %collective-permute-done.refs_0_, f32[36,8,128]{2,1,0:T(8,128)S(1)} %get-tuple-element.23.refs_1_, ...), custom_call_target="tpu_custom_call" | custom-call | tf_op jit(solution)/shard_map/edge_kernel/pallas_call | solution.py:566
  20.5 10.2 %all_to_all.31.recv = f32[32,5,2,128]{3,2,1,0:T(2,128)S(1)} all-to-all(f32[32,5,2,128]{3,2,1,0:T(2,128)S(1)} %get-tuple-element.26), channel_id=1, replica_groups=mesh['gx'=4,'gy'=4,'gz'=2] {'gx','gy','gz'}, dimensions={0} | all-to-all | bytes 327680 | tf_op jit(solution)/shard_map/all_to_all | solution.py:19
  30.7 1.0 %second_kernel.1 = (f32[32,5,2,128]{3,2,1,0:T(2,128)S(1)}, f32[36,8,128]{2,1,0:T(8,128)S(1)}, f32[36,8,128]{2,1,0:T(8,128)S(1)}, f32[4,8,128]{2,1,0:T(8,128)S(1)}) custom-call(f32[32,5,2,128]{3,2,1,0:T(2,128)S(1)} %all_to_all.31.recv, bf16[8064,256]{1,0:T(8,128)(2,1)S(1)} %get-tuple-element.27.tiles, bf16[1152,256]{1,0:T(8,128)(2,1)S(1)} %get-tuple-element.28.outer, ...), custom_call_target="tpu_custom_call" | custom-call | tf_op jit(solution)/shard_map/second_kernel/pallas_call | solution.py:566
  31.7 10.6 %all_to_all.32.recv = f32[32,5,2,128]{3,2,1,0:T(2,128)S(1)} all-to-all(f32[32,5,2,128]{3,2,1,0:T(2,128)S(1)} %get-tuple-element.31), channel_id=1, replica_groups=mesh['gx'=4,'gy'=4,'gz'=2] {'gx','gy','gz'}, dimensions={0} | all-to-all | bytes 327680 | tf_op jit(solution)/shard_map/all_to_all | solution.py:19
  42.3 1.2 %third_kernel.1 = (f32[32,13,1,128]{3,2,1,0:T(1,128)S(1)}, f32[18,128]{1,0:T(8,128)S(1)}) custom-call(f32[32,5,2,128]{3,2,1,0:T(2,128)S(1)} %all_to_all.32.recv, bf16[8064,256]{1,0:T(8,128)(2,1)S(1)} %get-tuple-element.27.tiles, bf16[1152,256]{1,0:T(8,128)(2,1)S(1)} %get-tuple-element.28.outer, f32[36,8,128]{2,1,0:T(8,128)S(1)} %get-tuple-element.29.mixed, ...), custom_call_target="tpu_custom_call" | custom-call | tf_op jit(solution)/shard_map/third_kernel/pallas_call | solution.py:566
  43.4 11.1 %all_to_all.33.recv = f32[32,13,1,128]{3,2,1,0:T(1,128)S(1)} all-to-all(f32[32,13,1,128]{3,2,1,0:T(1,128)S(1)} %get-tuple-element.35), channel_id=1, replica_groups=mesh['gx'=4,'gy'=4,'gz'=2] {'gx','gy','gz'}, dimensions={0} | all-to-all | bytes 425984 | tf_op jit(solution)/shard_map/all_to_all | solution.py:19
  54.5 1.0 %fourth_kernel.1 = (f32[32,2,2,128]{3,2,1,0:T(2,128)S(1)}, f32[36,8,128]{2,1,0:T(8,128)S(1)}, f32[8,128]{1,0:T(8,128)S(1)}) custom-call(f32[32,13,1,128]{3,2,1,0:T(1,128)S(1)} %all_to_all.33.recv, bf16[8064,256]{1,0:T(8,128)(2,1)S(1)} %get-tuple-element.27.tiles, bf16[1152,256]{1,0:T(8,128)(2,1)S(1)} %get-tuple-element.28.outer, ...), custom_call_target="tpu_custom_call" | custom-call | tf_op jit(solution)/shard_map/fourth_kernel/pallas_call | solution.py:566
  55.5 10.1 %all_to_all.34.recv = f32[32,2,2,128]{3,2,1,0:T(2,128)S(1)} all-to-all(f32[32,2,2,128]{3,2,1,0:T(2,128)S(1)} %get-tuple-element.36), channel_id=1, replica_groups=mesh['gx'=4,'gy'=4,'gz'=2] {'gx','gy','gz'}, dimensions={0} | all-to-all | bytes 131072 | tf_op jit(solution)/shard_map/all_to_all | solution.py:19
  65.6 1.0 %fifth_kernel.1 = (f32[32,1,1,128]{3,2,1,0:T(1,128)S(1)}, f32[6,128]{1,0:T(8,128)S(1)}) custom-call(f32[32,2,2,128]{3,2,1,0:T(2,128)S(1)} %all_to_all.34.recv, bf16[8064,256]{1,0:T(8,128)(2,1)S(1)} %get-tuple-element.27.tiles, bf16[1152,256]{1,0:T(8,128)(2,1)S(1)} %get-tuple-element.28.outer, f32[36,8,128]{2,1,0:T(8,128)S(1)} %get-tuple-element.37.source, ...), custom_call_target="tpu_custom_call" | custom-call | tf_op jit(solution)/shard_map/fifth_kernel/pallas_call | solution.py:566
  66.6 8.8 %all_to_all.35.recv = f32[32,1,1,128]{3,2,1,0:T(1,128)S(1)} all-to-all(f32[32,1,1,128]{3,2,1,0:T(1,128)S(1)} %get-tuple-element.38), channel_id=1, replica_groups=mesh['gx'=4,'gy'=4,'gz'=2] {'gx','gy','gz'}, dimensions={0} | all-to-all | bytes 32768 | tf_op jit(solution)/shard_map/all_to_all | solution.py:19
  75.4 0.7 last_kernel.1
Async XLA Ops:
  17.6 2.0 %collective-permute-start = (f32[16,9,2,128]{3,2,1,0:T(2,128)S(1)}, f32[16,9,2,128]{3,2,1,0:T(2,128)S(1)}, u32[]{:S(2)}, u32[]{:S(2)}) collective-permute-start(f32[16,9,2,128]{3,2,1,0:T(2,128)S(1)} %all_to_all.30.recv), channel_id=1, source_target_pairs={{0,1},{1,0},{2,3},{3,2},{4,5},{5,4},{6,7},{7,6},{8,9},{9,8},{10,11... | collective-permute-start | bytes 442376 | tf_op jit(solution)/shard_map/ppermute | solution.py:26
